TPU v7x, 32 devices: a whole 2x2x4 slice. The times are simulated.
32 devices in a mesh: dp: 8 (over z, x), mp: 4 (over y, core).
Axes of the slice: x: 2, y: 2, z: 4, core: 2. Of those that a mesh axis runs over, the one named last changes fastest.
Arguments:
- tokens: bfloat16 [8192, 1024], P(('dp', 'mp')), may hold values from -6 to 6
- w_query: bfloat16 [1024, 1024], P(None, 'mp'), may hold values from -0.046875 to 0.046875
- w_key: bfloat16 [1024, 1024], P(None, 'mp'), may hold values from -0.1875 to 0.1875
- w_value: bfloat16 [1024, 1024], P(None, 'mp'), may hold values from -0.1875 to 0.1875
- w_attn_out: bfloat16 [1024, 1024], P('mp'), may hold values from -1 to 1
- w_gate: bfloat16 [1024, 2816], P(None, 'mp'), may hold values from -0.1875 to 0.1875
- w_up: bfloat16 [1024, 2816], P(None, 'mp'), may hold values from -0.1875 to 0.1875
- w_down: bfloat16 [2816, 1024], P('mp'), may hold values from -0.109375 to 0.109375
- norm_attn: float32 [1024], replicated, may hold values from 0.1 to 1.9
- norm_ffn: float32 [1024], replicated, may hold values from 0.1 to 1.9
- rel_table: float32 [32, 16], P(None, 'mp'), may hold values from -3 to 3
- x_table: float32 [32, 16], P(None, 'mp'), may hold values from -3 to 3
- y_table: float32 [32, 16], P(None, 'mp'), may hold values from -3 to 3
- lengths: int32 [8, 2], P('dp'), may hold values from 0 to 1024, as said below
- boxes: int32 [2, 8192], P(None, 'dp'), may hold values from 0 to 127
- cotangent: bfloat16 [8192, 1024], P(('dp', 'mp')), may hold values from -6 to 6
Outputs:
- result: float32 [8192, 1024], P(('dp', 'mp'))
- d_tokens: float32 [8192, 1024], P(('dp', 'mp'))
- grad_query: float32 [1024, 1024], P('dp', 'mp')
- grad_key: float32 [1024, 1024], P('dp', 'mp')
- grad_value: float32 [1024, 1024], P('dp', 'mp')
- grad_attn_out: float32 [1024, 1024], P('mp', 'dp')
- grad_gate: float32 [1024, 2816], P('dp', 'mp')
- grad_up: float32 [1024, 2816], P('dp', 'mp')
- grad_down: float32 [2816, 1024], P('mp', 'dp')
- grad_norm_attn: float32 [1024], P(('dp', 'mp'))
- grad_norm_ffn: float32 [1024], P(('dp', 'mp'))
- grad_rel: float32 [32, 16], P('dp', 'mp')
- grad_x: float32 [32, 16], P('dp', 'mp')
- grad_y: float32 [32, 16], P('dp', 'mp')
Inputs may be any that keep to these rules, and one draw needn't show every extreme that they name: `lengths`: in a group whose index modulo 8 is under 5 the odd slots are 0 and the even slots hold 512 to 1024; in the other groups every slot holds 256 to 512. Group 0 has a sequence of 1024 and group 5 one of 512.
All inputs are finite; a program needn't handle non-finite values.
Results may differ from a plain program's by a relative error of at most 0.03.
Values may be sent and summed in bfloat16 or wider, within the bound.
No kernel may reach another device: no remote copies, remote signals or barrier semaphores. Data moves between devices by JAX's collectives and lax.ppermute only.
A program may use at most 832 MiB of HBM per device.

v0:
```python
import functools

import jax
import jax.numpy as jnp
from jax import lax
from jax.experimental import pallas as pl
from jax.experimental.pallas import tpu as pltpu
from jax.sharding import PartitionSpec as P

f32, bf16, i32 = jnp.float32, jnp.bfloat16, jnp.int32
HEAD = 64
NB = 32
COORD = 128
SHORT = 512
NEAR = 3 * COORD
EXTRA = 16
KEYS = 512
thresholds = (1, 2, 3, 4, 5, 6, 7, 8, 12, 16, 23, 32, 46, 64, 91)
masked_score = -1000000000.0


def dot(a, b):
    return jnp.dot(a, b, preferred_element_type=f32)


def dot_nt(a, b):
    return lax.dot_general(a, b, (((1,), (1,)), ((), ())), preferred_element_type=f32)


def dot_tn(a, b):
    return lax.dot_general(a, b, (((0,), (0,)), ((), ())), preferred_element_type=f32)


def bucket_of(offsets):
    distance = jnp.abs(offsets)
    bucket_ids = jnp.where(offsets > 0, NB // 2, 0)
    for threshold in thresholds:
        bucket_ids = bucket_ids + jnp.where(distance >= threshold, 1, 0)
    return bucket_ids


def offset_hot(sign=1):
    offsets = sign * (lax.broadcasted_iota(i32, (NB, 512), 1) - 256)
    return (bucket_of(offsets) == lax.broadcasted_iota(i32, (NB, 512), 0)).astype(f32)


def toeplitz(row, base):
    wide = jnp.broadcast_to(row, (COORD, 512))
    return pltpu.roll(wide, (256 - base) % 512, 1, stride=1, stride_axis=0)


def start_of(len0, len1):
    return jnp.where(len1 > 0, 1, 0), jnp.where(len1 > 0, len1, len0)


def build(lens, tab_ref, box_cols, box_rows, k_ref, b_scr, hot_scr, lut_scr, strip_scr, n_heads):
    n_keys = k_ref.shape[0]
    len0, len1 = lens[0, 0], lens[0, 1]
    start1, start1_len = start_of(len0, len1)
    lane = lax.broadcasted_iota(i32, (n_keys, COORD), 1)
    pos = lax.broadcasted_iota(i32, (n_keys, COORD), 0)
    x_hot = (box_cols[:, 0:1] == lane).astype(bf16)
    y_hot = (box_cols[:, 1:2] == lane).astype(bf16)
    second = pos >= SHORT
    start_k = jnp.where(second, start1, 0)
    limit = jnp.where(second, start1_len, len0)
    valid = pos - start_k * SHORT < limit
    masked0 = jnp.where(valid & (start_k == 0), 0.0, masked_score)
    masked1 = jnp.where(valid & (start_k == start1), 0.0, masked_score)
    extra = jnp.where(lane == 0, masked0, jnp.where(lane == 1, masked1, 0.0))
    extra = extra.astype(bf16)[:, 0:EXTRA]
    for pair in range(n_heads // 2):
        b_scr[pair, :, 0:128] = k_ref[:, pair * 128 : pair * 128 + 128]
        b_scr[pair, :, 128:256] = x_hot
        b_scr[pair, :, 256:384] = y_hot
        b_scr[pair, :, 384 : 384 + EXTRA] = extra
    level = lax.broadcasted_iota(i32, (COORD, n_keys), 0)
    hot_scr[0:128, :] = (box_rows[0:1, :] == level).astype(bf16)
    hot_scr[128:256, :] = (box_rows[1:2, :] == level).astype(bf16)
    vec = jnp.dot(tab_ref[...], offset_hot(), precision=lax.Precision.HIGHEST, preferred_element_type=f32)
    n_strip = strip_scr.shape[1]
    for h in range(n_heads):
        for axis in range(2):
            at = n_heads * (1 + axis) + h
            table = toeplitz(vec[at : at + 1, :], 0)[:, 0:128]
            lut_scr[h, axis] = table.T.astype(bf16)
        row = vec[h : h + 1, :]
        near = toeplitz(row, -128)[:, 0:NEAR]
        mid = (n_strip - NEAR) // 2
        left = jnp.broadcast_to(row[:, 0:1], (mid, COORD))
        right = jnp.broadcast_to(row[:, 511:512], (mid, COORD))
        strip_scr[h, 0:mid, :] = left
        strip_scr[h, mid : mid + NEAR, :] = near.T
        strip_scr[h, mid + NEAR :, :] = right


def query_side(lens, block, qb, h, qt, hot_q, lut_scr):
    half = jnp.zeros((HEAD, qb), bf16)
    own = qt[(h % 2) * HEAD : (h % 2) * HEAD + HEAD, :]
    parts = [own, half] if h % 2 == 0 else [half, own]
    x_rows = dot(lut_scr[h, 0], hot_q[0:128, :]).astype(bf16)
    y_rows = dot(lut_scr[h, 1], hot_q[128:256, :]).astype(bf16)
    row = lax.broadcasted_iota(i32, (EXTRA, qb), 0)
    q_pos = block * qb + lax.broadcasted_iota(i32, (EXTRA, qb), 1)
    extra = jnp.where(row == jnp.where(q_pos >= SHORT, 1, 0), 1.0, 0.0)
    return jnp.concatenate(parts + [x_rows, y_rows, extra.astype(bf16)], axis=0)


def pieces(value):
    high = value.astype(bf16).astype(f32)
    rest = value - high
    mid = rest.astype(bf16).astype(f32)
    return high, mid, (rest - mid).astype(bf16).astype(f32)


def scores(block, qb, h, at, b_scr, strip_scr, key_at):
    s = dot(b_scr[h // 2, key_at : key_at + KEYS, :], at)
    blocks = qb // COORD
    top = b_scr.shape[1] // COORD - 1
    parts = []
    for t in range(blocks):
        off = pl.multiple_of((top - (block * blocks + t)) * COORD + key_at, COORD)
        parts.append(s[:, t * 128 : t * 128 + 128] + strip_scr[h, pl.ds(off, KEYS), :])
    return jnp.concatenate(parts, axis=1)


def lone(lens, block, qb):
    len0, len1 = lens[0, 0], lens[0, 1]
    start1, start1_len = start_of(len0, len1)
    in_second = block * qb >= SHORT
    begin = jnp.where(in_second, start1, 0) * SHORT
    limit = jnp.where(in_second, start1_len, len0)
    pos = block * qb + lax.broadcasted_iota(i32, (1, qb), 1) - begin
    return block * qb + qb - 1 - begin >= limit, pos >= limit


def own_score(h, qt, kt, strip_scr, lut_scr):
    mine = slice((h % 2) * HEAD, (h % 2) * HEAD + HEAD)
    product = qt[mine, :].astype(f32) * kt[mine, :].astype(f32)
    centre = (strip_scr.shape[1] - COORD) // 2
    bias = strip_scr[h, centre : centre + 1, 0:1] + lut_scr[h, 0, 0:1, 0:1].astype(f32) + lut_scr[h, 1, 0:1, 0:1].astype(f32)
    return jnp.sum(product, axis=0, keepdims=True) + bias


def fwd_kernel(n_heads, qb, base, lens, tab_ref, box_cols, box_rows, q_ref, k_ref, v_ref, *refs):
    ctx_ref, ctxt_ref, rows_ref, p_ref, out_ref, b_scr, hot_scr, lut_scr, strip_scr, vt_scr, s_scr, top_scr, log_scr = refs[-13:]
    n_keys = k_ref.shape[0]
    block = pl.program_id(0) + base

    @pl.when(pl.program_id(0) == 0)
    def _():
        build(lens, tab_ref, box_cols, box_rows, k_ref, b_scr, hot_scr, lut_scr, strip_scr, n_heads)
        for pair in range(n_heads // 2):
            vt_scr[pair, 0:128, :] = v_ref[:, pair * 128 : pair * 128 + 128].T
            vt_scr[pair, 128:144, :] = jnp.ones((16, n_keys), bf16)

    hot_q = hot_scr[:, pl.ds(pl.multiple_of(block * qb, qb), qb)]
    for pair in range(n_heads // 2):
        qt = q_ref[:, pair * 128 : pair * 128 + 128].T
        halves = []
        for h in (2 * pair, 2 * pair + 1):
            at = query_side(lens, block, qb, h, qt, hot_q, lut_scr)
            top = None
            for key_at in range(0, n_keys, KEYS):
                s = scores(block, qb, h, at, b_scr, strip_scr, key_at)
                s_scr[h % 2, key_at : key_at + KEYS, :] = s
                high = jnp.max(s, axis=0, keepdims=True)
                top = high if top is None else jnp.maximum(top, high)
            out = None
            for key_at in range(0, n_keys, KEYS):
                p = jnp.exp(s_scr[h % 2, key_at : key_at + KEYS, :] - top).astype(bf16)
                p_ref[h, key_at : key_at + KEYS, :] = p
                part = dot(vt_scr[pair, :, key_at : key_at + KEYS], p)
                out = part if out is None else out + part
            total = out[128:129, :]
            factor = 1.0 / total
            halves.append(out[(h % 2) * HEAD : (h % 2) * HEAD + HEAD, :] * factor)
            rows_ref[h : h + 1, :] = factor
            rows_ref[n_heads + h : n_heads + h + 1, :] = jnp.zeros((1, qb), f32)
            top_scr[h : h + 1, :] = top
            log_scr[h : h + 1, :] = top + jnp.log(total)
        ctxt = jnp.concatenate(halves, axis=0)
        ctxt_ref[pair * 128 : pair * 128 + 128, :] = ctxt
        ctx_ref[:, pair * 128 : pair * 128 + 128] = ctxt.T.astype(bf16)
    some, which = lone(lens, block, qb)

    @pl.when(some)
    def _():
        rows_q = pl.ds(pl.multiple_of(block * qb, qb), qb)
        for pair in range(n_heads // 2):
            cols = slice(pair * 128, pair * 128 + 128)
            qt, kt = q_ref[:, cols].T, k_ref[rows_q, cols].T
            for h in (2 * pair, 2 * pair + 1):
                own = own_score(h, qt, kt, strip_scr, lut_scr)
                log = log_scr[h : h + 1, :]
                high = jnp.maximum(own, log)
                new = high + jnp.log(jnp.exp(own - high) + jnp.exp(log - high))
                mine = slice(h * HEAD, h * HEAD + HEAD)
                value = vt_scr[pair, (h % 2) * HEAD : (h % 2) * HEAD + HEAD, rows_q].astype(f32)
                old = ctxt_ref[mine, :]
                alone = jnp.exp(own - new)
                ctxt_ref[mine, :] = jnp.where(which, old * jnp.exp(log - new) + value * alone, old)
                factor = rows_ref[h : h + 1, :]
                rows_ref[h : h + 1, :] = jnp.where(which, jnp.exp(top_scr[h : h + 1, :] - new), factor)
                rows_ref[n_heads + h : n_heads + h + 1, :] = jnp.where(which, alone, 0.0)
            ctx_ref[:, cols] = ctxt_ref[cols, :].T.astype(bf16)

    out_ref[...] = ctx_ref[...]


def scratch(n_keys, n_heads):
    return [
        pltpu.VMEM((n_heads // 2, n_keys, 384 + EXTRA), bf16),
        pltpu.VMEM((256, n_keys), bf16),
        pltpu.VMEM((n_heads, 2, COORD, COORD), bf16),
        pltpu.VMEM((n_heads, 2 * n_keys - COORD, COORD), f32),
    ]


def whole(shape):
    return pl.BlockSpec(shape, lambda *at: (0,) * len(shape))


def params():
    return pltpu.CompilerParams(dimension_semantics=("arbitrary",), vmem_limit_bytes=62 << 20)


def row_block(step, ids):
    return step // 2 * 2 + (step + ids[1]) % 2


def attend(chunk, q, k, v, tables, lengths, box_cols, box_rows, before):
    n_keys, width = k.shape
    qb = n_keys // 4
    n_heads = width // HEAD
    return pl.pallas_call(
        functools.partial(fwd_kernel, n_heads, qb, 2 * chunk),
        out_shape=(
            jax.ShapeDtypeStruct((n_keys, width), bf16),
            jax.ShapeDtypeStruct((width, n_keys), f32),
            jax.ShapeDtypeStruct((8, n_keys), f32),
            jax.ShapeDtypeStruct((n_heads, n_keys, n_keys), bf16),
            jax.ShapeDtypeStruct((2 * qb, width), bf16),
        ),
        grid=(2,),
        in_specs=[
            pl.BlockSpec(memory_space=pltpu.SMEM),
            whole(tables.shape), whole(box_cols.shape), whole(box_rows.shape),
            pl.BlockSpec((qb, width), lambda i: (i + 2 * chunk, 0)), whole(k.shape), whole(v.shape),
        ] + [anywhere()] * len(before),
        out_specs=(
            pl.BlockSpec((qb, width), lambda i: (i + 2 * chunk, 0)),
            pl.BlockSpec((width, qb), lambda i: (0, i + 2 * chunk)),
            pl.BlockSpec((8, qb), lambda i: (0, i + 2 * chunk)),
            pl.BlockSpec((n_heads, n_keys, qb), lambda i: (0, 0, i + 2 * chunk)),
            pl.BlockSpec((qb, width), lambda i: (i, 0)),
        ),
        scratch_shapes=scratch(n_keys, n_heads) + [
            pltpu.VMEM((n_heads // 2, 144, n_keys), bf16),
            pltpu.VMEM((2, n_keys, qb), f32),
            pltpu.VMEM((8, qb), f32),
            pltpu.VMEM((8, qb), f32),
        ],
        input_output_aliases={7 + i: i for i in range(len(before))},
        compiler_params=params(),
        cost_estimate=estimate(),
        name="attend",
    )(lengths, tables, box_cols, box_rows, q, k, v, *before)


def skew_sums(tile, base):
    width = tile.shape[1]
    wide = jnp.concatenate([tile, jnp.zeros((128, 512 - width), f32)], axis=1)
    wide = pltpu.roll(wide, (257 - width - base) % 512, 1, stride=1, stride_axis=0)
    return jnp.sum(wide, axis=0, keepdims=True)


def bwd_kernel(n_heads, qb, ids, lens, box_cols, box_rows, q_ref, k_ref, v_ref, d0_ref, d1_ref, d2_ref, d3_ref, wo_ref, ctxt_ref, rows_ref, p_ref,
               out_ref, dtab_ref, da_ref, v_scr, kt_scr, ds_scr, dk_scr, dv_scr, near_scr, part_scr, far_acc, self_acc):
    step = pl.program_id(0)
    block = row_block(step, ids)
    n_keys = k_ref.shape[0]
    blocks = qb // COORD

    @pl.when(step == 0)
    def _():
        lane = lax.broadcasted_iota(i32, (n_keys, 128), 1)
        level = COORD - 1 - lax.broadcasted_iota(i32, (COORD, n_keys), 0)
        kb = lax.broadcasted_iota(i32, (16, n_keys), 0)
        kp = lax.broadcasted_iota(i32, (16, n_keys), 1)
        for pair in range(n_heads // 2):
            cols = slice(pair * 128, pair * 128 + 128)
            v_scr[pair, :, 0:128] = v_ref[:, cols]
            v_scr[pair, :, 128 : 128 + EXTRA] = jnp.where(lane < 3, -1.0, 0.0).astype(bf16)[:, 0:EXTRA]
            kt_scr[pair, 0:128, :] = k_ref[:, cols].T
            for axis in range(2):
                kt_scr[pair, 128 + 128 * axis : 256 + 128 * axis, :] = (box_rows[axis : axis + 1, :] == level).astype(bf16)
            kt_scr[pair, 384:400, :] = (kp // COORD == kb).astype(bf16)
        dk_scr[...] = jnp.zeros_like(dk_scr)
        dv_scr[...] = jnp.zeros_like(dv_scr)
        near_scr[...] = jnp.zeros_like(near_scr)
        far_acc[...] = jnp.zeros_like(far_acc)
        self_acc[...] = jnp.zeros_like(self_acc)
        for h in range(n_heads):
            ds_scr[h, 0:128, :] = jnp.zeros((128, qb), bf16)
            ds_scr[h, 128 + n_keys :, :] = jnp.zeros((128, qb), bf16)

    rows_q = pl.ds(pl.multiple_of(block * qb, qb), qb)
    lane_half = lax.broadcasted_iota(i32, (qb, 128), 1) >= HEAD
    for at_step, piece in enumerate((d0_ref, d1_ref, d2_ref, d3_ref)):

        @pl.when(step == at_step)
        def _():
            da_ref[...] = piece[...]

    d_ctx = dot_nt(wo_ref[...], da_ref[...])
    prod = d_ctx * ctxt_ref[...]
    scaled = []
    operands = []
    for h in range(n_heads):
        mine = slice(h * HEAD, h * HEAD + HEAD)
        factor = rows_ref[h : h + 1, :]
        delta = jnp.sum(prod[mine, :], axis=0, keepdims=True) * factor
        row = lax.broadcasted_iota(i32, (EXTRA, qb), 0)
        extra = jnp.zeros((EXTRA, qb), f32)
        for piece, value in enumerate(pieces(delta)):
            extra = jnp.where(row == piece, value, extra)
        none = jnp.zeros((HEAD, qb), bf16)
        own = (d_ctx[mine, :] * factor).astype(bf16)
        scaled.append(own)
        operands.append(jnp.concatenate(([own, none] if h % 2 == 0 else [none, own]) + [extra.astype(bf16)], axis=0))
    for h, dat in enumerate(operands):
        for key_at in range(0, n_keys, KEYS):
            dp = dot(v_scr[h // 2, key_at : key_at + KEYS, :], dat)
            p = p_ref[h, key_at : key_at + KEYS, :].astype(f32)
            ds_scr[h, 128 + key_at : 128 + key_at + KEYS, :] = (p * dp).astype(bf16)
    key_block = lax.broadcasted_iota(i32, (8, qb), 0)
    q_block = block * blocks + lax.broadcasted_iota(i32, (8, qb), 1) // COORD

    def of_head(x, h):
        return jnp.where(lane_half, x if h else 0.0, 0.0 if h else x).astype(bf16)

    for pair in range(n_heads // 2):
        dq_halves = []
        for h in (2 * pair, 2 * pair + 1):
            got = dot(kt_scr[pair], ds_scr[h, 128 : 128 + n_keys, :])
            dq_halves.append(got[h % 2 * HEAD : h % 2 * HEAD + HEAD, :])
            part_scr[h, :, rows_q] = got[128:384, :].astype(bf16)
            by_block = got[384:392, :]
            far_acc[h, 0] += jnp.where(key_block + 1 < q_block, by_block, 0.0)
            far_acc[h, 1] += jnp.where(key_block > q_block + 1, by_block, 0.0)
        out_ref[rows_q, 384 * pair : 384 * pair + 128] = jnp.concatenate(dq_halves, axis=0).T.astype(bf16)
        do = jnp.concatenate(scaled[2 * pair : 2 * pair + 2], axis=0).T.astype(f32)
        q = q_ref[:, 128 * pair : 128 * pair + 128].astype(f32)
        dv_scr[pair] += dot(p_ref[2 * pair], of_head(do, 0)) + dot(p_ref[2 * pair + 1], of_head(do, 1))
        ds = [ds_scr[2 * pair + h, 128 : 128 + n_keys, :] for h in range(2)]
        dk_scr[pair] += dot(ds[0], of_head(q, 0)) + dot(ds[1], of_head(q, 1))
    for h in range(n_heads):
        for t in range(blocks):
            rows = pl.ds(pl.multiple_of((block * blocks + t) * COORD, COORD), NEAR)
            near_scr[h] += ds_scr[h, rows, t * 128 : t * 128 + 128].astype(f32)

    some, _ = lone(lens, block, qb)

    @pl.when(some)
    def _():
        d_out = dot_nt(wo_ref[...], da_ref[...])
        product = d_out * ctxt_ref[...]
        for pair in range(n_heads // 2):
            cols = slice(pair * 128, pair * 128 + 128)
            q_t, kt, vt = q_ref[:, cols].T, k_ref[rows_q, cols].T, v_ref[rows_q, cols].T
            add_q, add_k, add_v = [], [], []
            for h in (2 * pair, 2 * pair + 1):
                mine = slice(h % 2 * HEAD, h % 2 * HEAD + HEAD)
                d_own = d_out[h * HEAD : h * HEAD + HEAD, :]
                p = rows_ref[n_heads + h : n_heads + h + 1, :]
                dp = jnp.sum(d_own * vt[mine, :].astype(f32) - product[h * HEAD : h * HEAD + HEAD, :], axis=0, keepdims=True)
                ds = p * dp
                add_q.append(kt[mine, :].astype(f32) * ds)
                add_k.append(q_t[mine, :].astype(f32) * ds)
                add_v.append(d_own * p)
                self_acc[h : h + 1, :] += ds
            at = slice(384 * pair, 384 * pair + 128)
            out_ref[rows_q, at] = (out_ref[rows_q, at].astype(f32) + jnp.concatenate(add_q, axis=0).T).astype(bf16)
            dk_scr[pair, rows_q, :] += jnp.concatenate(add_k, axis=0).T
            dv_scr[pair, rows_q, :] += jnp.concatenate(add_v, axis=0).T

    @pl.when(step == pl.num_programs(0) - 1)
    def _():
        for pair in range(n_heads // 2):
            out_ref[:, 384 * pair + 128 : 384 * pair + 256] = dk_scr[pair].astype(bf16)
            out_ref[:, 384 * pair + 256 : 384 * pair + 384] = dv_scr[pair].astype(bf16)
        offset = 256 - lax.broadcasted_iota(i32, (1, 512), 1)
        row, column = (lax.broadcasted_iota(i32, (NEAR, NEAR), at) for at in (0, 1))
        mirror = (row + column == NEAR - 1).astype(bf16)
        lane = lax.broadcasted_iota(i32, (n_keys, 128), 1)
        hots = [(box_cols[:, axis : axis + 1] == lane).astype(bf16) for axis in range(2)]
        sums = [jnp.zeros((1, 512), f32)] * 16
        for h in range(n_heads):
            high, rest = pieces(near_scr[h])[0:2]
            near = skew_sums(dot_tn(high.astype(bf16), mirror) + dot_tn(rest.astype(bf16), mirror), -128)
            left = jnp.sum(far_acc[h, 0], keepdims=True)
            right = jnp.sum(far_acc[h, 1], keepdims=True)
            alone = jnp.where(offset == 0, jnp.sum(self_acc[h : h + 1, :], keepdims=True), 0.0)
            far = jnp.where(offset == -255, left, 0.0) + jnp.where(offset == 255, right, 0.0)
            sums[h] = near + far + alone
            for axis in range(2):
                pairs = dot(part_scr[h, 128 * axis : 128 * axis + 128, :], hots[axis])
                sums[n_heads * (1 + axis) + h] = skew_sums(pairs.T, 0) + alone
        sums = jnp.concatenate(sums, axis=0)
        dtab_ref[...] = lax.dot_general(offset_hot(-1), sums, (((1,), (1,)), ((), ())), precision=lax.Precision.HIGHEST, preferred_element_type=f32)


def attend_back(ids, q, k, v, d_own, d_core, w_out, ctxt, rows, probs, lengths, box_cols, box_rows):
    n_keys, width = k.shape
    n_heads = width // HEAD
    qb = n_keys // 4
    model = w_out.shape[1]
    n_pairs = n_heads // 2
    at_rows = lambda i, ids, lens: (row_block(i, ids), 0)
    at_columns = lambda i, ids, lens: (0, row_block(i, ids))
    pieces_in = [(d, at) for at in range(2) for d in (d_own, d_core)]
    return pl.pallas_call(
        functools.partial(bwd_kernel, n_heads, qb),
        out_shape=[
            jax.ShapeDtypeStruct((n_keys, 384 * n_pairs), bf16),
            jax.ShapeDtypeStruct((NB, 16), f32),
            jax.ShapeDtypeStruct((n_keys, model), bf16),
        ],
        grid_spec=pltpu.PrefetchScalarGridSpec(
            num_scalar_prefetch=2,
            grid=(4,),
            in_specs=[
                whole(box_cols.shape), whole(box_rows.shape),
                pl.BlockSpec((qb, width), at_rows), whole(k.shape), whole(v.shape),
                *[pl.BlockSpec((qb, model), lambda i, ids, lens, at=at: (at, 0)) for _, at in pieces_in],
                whole(w_out.shape),
                pl.BlockSpec((width, qb), at_columns),
                pl.BlockSpec((8, qb), at_columns),
                pl.BlockSpec((n_heads, n_keys, qb), lambda i, ids, lens: (0, 0, row_block(i, ids))),
            ],
            out_specs=[whole((n_keys, 384 * n_pairs)), whole((NB, 16)), pl.BlockSpec((qb, model), at_rows)],
            scratch_shapes=[
                pltpu.VMEM((n_pairs, n_keys, 128 + EXTRA), bf16),
                pltpu.VMEM((n_pairs, 400, n_keys), bf16),
                pltpu.VMEM((n_heads, n_keys + 256, qb), bf16),
                pltpu.VMEM((n_pairs, n_keys, 128), f32),
                pltpu.VMEM((n_pairs, n_keys, 128), f32),
                pltpu.VMEM((n_heads, NEAR, COORD), f32),
                pltpu.VMEM((n_heads, 256, n_keys), bf16),
                pltpu.VMEM((n_heads, 2, 8, qb), f32),
                pltpu.VMEM((8, qb), f32),
            ],
        ),
        compiler_params=params(),
        cost_estimate=estimate(),
        name="attend_back",
    )(ids, lengths, box_cols, box_rows, q, k, v, *(d for d, _ in pieces_in), w_out, ctxt, rows, probs)


norm_eps = 1e-06
gelu_scale = 0.7978845608028654
gelu_cube = 0.044715


def scale_of(values):
    return lax.rsqrt(jnp.mean(values * values, axis=-1, keepdims=True) + norm_eps)


def anywhere():
    return pl.BlockSpec(memory_space=pl.ANY)


def estimate():
    return pl.CostEstimate(flops=1_000, bytes_accessed=1_000, transcendentals=0)


def qkv_kernel(ids, xa_ref, xb_ref, g_ref, wq_ref, wk_ref, wv_ref, *refs):
    xo_ref, n_ref, q_ref, k_ref, v_ref = refs[-5:]
    for at_step, piece in enumerate((xa_ref, xb_ref)):

        @pl.when(pl.program_id(0) == at_step)
        def _():
            xo_ref[...] = piece[...]

    x = xo_ref[...].astype(f32)
    normed = (x * scale_of(x) * g_ref[...]).astype(bf16)
    n_ref[...] = normed
    q_ref[...] = dot(normed, wq_ref[...]).astype(bf16)
    k_ref[...] = dot(normed, wk_ref[...]).astype(bf16)
    v_ref[...] = dot(normed, wv_ref[...]).astype(bf16)


def project(ids, far, pair, gain, weights, before, n_blocks):
    rows, model = pair[0].shape
    width = weights[0].shape[1]

    def row(i, ids):
        chip = 1 - ids[2] if far else ids[2]
        return (2 * chip + (i + ids[1]) % 2, 0)

    shapes = [jax.ShapeDtypeStruct((n_blocks * rows, n), bf16) for n in (model, model, width, width, width)]
    return pl.pallas_call(
        qkv_kernel,
        out_shape=shapes,
        grid_spec=pltpu.PrefetchScalarGridSpec(
            num_scalar_prefetch=1,
            grid=(2,),
            in_specs=[whole(pair[0].shape)] * 2 + [whole(gain.shape)] + [whole(w.shape) for w in weights] + [anywhere()] * len(before),
            out_specs=[pl.BlockSpec((rows, s.shape[1]), row) for s in shapes],
        ),
        input_output_aliases={7 + i: i for i in range(len(before))},
        compiler_params=params(),
        cost_estimate=estimate(),
        name="project",
    )(ids, *pair, gain, *weights, *before)


def assemble_kernel(ids, *refs):
    for at_step in range(4):

        @pl.when(pl.program_id(0) == at_step)
        def _():
            refs[4][...] = refs[at_step][...]


def assemble(ids, blocks):
    rows, model = blocks[0].shape

    def row(i, ids):
        chip = i // 2
        core = i % 2
        return (2 * ((ids[2] + chip) % 2) + (ids[1] + core) % 2, 0)

    return pl.pallas_call(
        assemble_kernel,
        out_shape=jax.ShapeDtypeStruct((4 * rows, model), bf16),
        grid_spec=pltpu.PrefetchScalarGridSpec(
            num_scalar_prefetch=1,
            grid=(4,),
            in_specs=[whole((rows, model))] * 4,
            out_specs=pl.BlockSpec((rows, model), row),
        ),
        compiler_params=params(),
        cost_estimate=estimate(),
        name="assemble",
    )(ids, *blocks)


def ffn_kernel(ids, a0, a1, a2, a3, b0, b1, b2, b3, x_ref, cot_ref, o0, o1, o2, o3, g_ref, wg_ref, wu_ref, wd_ref,
               mixed_ref, nf_ref, hid_ref, dg_ref, du_ref, dsend, dkeep, rsend, rkeep):
    first = pl.program_id(0) < 2
    mixed = x_ref[...].astype(f32)
    for a, b, o in ((a0, b0, o0), (a1, b1, o1), (a2, b2, o2), (a3, b3, o3)):
        mixed = mixed + dot(jnp.where(first, a[...], b[...]), o[...])
    normed = (mixed * scale_of(mixed) * g_ref[...]).astype(bf16)
    nf_ref[...] = normed
    gate = dot_nt(wg_ref[...], normed)
    up = dot_nt(wu_ref[...], normed)
    d_hidden = dot_nt(wd_ref[...], cot_ref[...])
    square = gate * gate
    t = jnp.tanh(gelu_scale * gate * (1.0 + gelu_cube * square))
    half = 0.5 * (1.0 + t)
    unit = gate * half
    slope = half + 0.5 * gate * (1.0 - t * t) * (gelu_scale * (1.0 + 3.0 * gelu_cube * square))
    hidden = (unit * up).astype(bf16)
    d_gate = (d_hidden * up * slope).astype(bf16)
    d_up = (d_hidden * unit).astype(bf16)
    hid_ref[...] = hidden
    dg_ref[...] = d_gate
    du_ref[...] = d_up
    d_normed = (dot_tn(d_gate, wg_ref[...]) + dot_tn(d_up, wu_ref[...])).astype(bf16)
    down = dot_tn(hidden, wd_ref[...]).astype(bf16)
    half = pl.program_id(0) % 2

    @pl.when(half == 0)
    def _():
        dsend[...] = d_normed
        rsend[...] = down

    @pl.when(half == 1)
    def _():
        dkeep[...] = d_normed
        rkeep[...] = down
        mixed_ref[...] = mixed


def ffn(ids, contexts, x_all, cot_all, w_outs, gain, w_gate_t, w_up_t, w_down):
    total, model = x_all.shape
    rows = total // 4
    width, hidden = contexts[0][0].shape[1], w_down.shape[0]

    def local_row(i, ids):
        return (i + 1 + ids[1]) % 2

    def row(i, ids):
        return i // 2 * 2 + local_row(i, ids)

    def part(chunk):
        return pl.BlockSpec((rows, width), lambda i, ids: (jnp.where(i // 2 == chunk, local_row(i, ids), ids[1] if chunk == 0 else 1 - ids[1]), 0))

    rows_spec = pl.BlockSpec((rows, model), lambda i, ids: (row(i, ids), 0))
    units_spec = pl.BlockSpec((hidden, rows), lambda i, ids: (0, row(i, ids)))
    half_spec = pl.BlockSpec((rows, model), lambda i, ids: (i // 2, 0))
    outs = [((2 * rows, model), f32, half_spec), ((total, model), bf16, rows_spec)]
    outs += [((hidden, total), bf16, units_spec)] * 3
    outs += [((2 * rows, model), bf16, half_spec)] * 4
    ins = [(a, part(chunk)) for chunk in range(2) for a in contexts[chunk]]
    ins += [(x_all, rows_spec), (cot_all, rows_spec)]
    ins += [(w, whole(w.shape)) for w in (*w_outs, gain, w_gate_t, w_up_t, w_down)]
    return call(ffn_kernel, ids, ins, outs, (4,), "ffn")


def norm_back(total, values, gain):
    r = scale_of(values)
    n = values * r
    e = gain * total
    return r * (e - n * jnp.mean(n * e, axis=-1, keepdims=True)), jnp.sum(total * n, axis=0, keepdims=True)


def mid_kernel(ids, a_ref, b_ref, mixed_ref, cot_ref, g_ref, dm_ref, da_ref, sum_ref):
    total = a_ref[...].astype(f32) + b_ref[...].astype(f32)
    grad, gain_sum = norm_back(total, mixed_ref[...], g_ref[...])
    d_mixed = cot_ref[...].astype(f32) + grad
    dm_ref[...] = d_mixed
    da_ref[...] = d_mixed.astype(bf16)
    step = pl.program_id(0)
    gain_sum = jnp.where(ids[2] == step // 2, gain_sum, 0.0)

    @pl.when(step == 0)
    def _():
        sum_ref[...] = gain_sum

    @pl.when(step > 0)
    def _():
        sum_ref[...] += gain_sum


def mid(ids, own, far, mixed, cot_all, gain):
    total, model = own.shape
    rows = total // 4
    spec = pl.BlockSpec((rows, model), lambda i, ids: (i, 0))
    cot_spec = pl.BlockSpec((rows, model), lambda i, ids: (i // 2 * 4 + 2 * ids[1] + i % 2, 0))
    ins = [(own, spec), (far, spec), (mixed, spec), (cot_all, cot_spec), (gain, whole(gain.shape))]
    outs = [((total, model), f32, spec), ((total, model), bf16, spec), ((1, model), f32, whole((1, model)))]
    return call(mid_kernel, ids, ins, outs, (4,), "mid")


def back_kernel(ids, a_ref, b_ref, wa_ref, wb_ref, *outs):
    total = dot_nt(a_ref[...], wa_ref[...]) + dot_nt(b_ref[...], wb_ref[...])
    for at_step, out in enumerate(outs):

        @pl.when(pl.program_id(0) == at_step)
        def _():
            out[...] = total.astype(out.dtype)


def project_back(ids, grads, weights):
    total = grads.shape[0]
    rows, (model, width) = total // 4, weights[0].shape

    def row(i, ids):
        return 2 * ((1 - i // 2 + ids[2]) % 2) + (i + 1 + ids[1]) % 2

    ins = [(grads, pl.BlockSpec((rows, width), lambda i, ids, at=at: (row(i, ids), at))) for at in range(2)]
    ins += [(w, whole(w.shape)) for w in weights]
    outs = [((rows, model), kind, whole((rows, model))) for kind in (bf16, f32, bf16, f32)]
    return call(back_kernel, ids, ins, outs, (4,), "project_back")


def last_kernel(ids, keep_ref, core_ref, y_ref, x_ref, g_ref, dm_ref, out_ref, sum_ref):
    total = keep_ref[...] + core_ref[...].astype(f32) + y_ref[...].astype(f32)
    grad, gain_sum = norm_back(total, x_ref[...].astype(f32), g_ref[...])
    out_ref[...] = dm_ref[...] + grad
    sum_ref[...] = gain_sum


def last(ids, keep, core, far, x, gain, d_mixed):
    ins = [(a, whole(a.shape)) for a in (keep, core, far, x, gain)]
    ins.append((d_mixed, pl.BlockSpec(keep.shape, lambda i, ids: (ids[2], 0))))
    outs = [(shape, f32, whole(shape)) for shape in (keep.shape, (1, keep.shape[1]))]
    return call(last_kernel, ids, ins, outs, (1,), "last")


def bit_orders(shards):
    bits = list(range(shards.bit_length() - 1))
    return bits, bits[1:] + bits[:1]


def slot_of(flip, order):
    place = 0
    for bit in order[1:]:
        place = 2 * place + (flip >> bit) % 2
    return (flip >> order[0]) % 2, place


def unit_parts_kernel(ids, *refs):
    n = 3
    kept_a, sent_a, kept_b, sent_b = refs[2 * n :]
    step = pl.program_id(0)
    low, high = step % 2, step // 2
    even = ids[3] % 2 == 0
    nears, fars = [], []
    for i in range(n):
        out = dot(refs[i][...], refs[n + i][...]).astype(bf16)
        width, cut = out.shape[1] // 2, out.shape[0] // 2
        first, second = out[:, :width], out[:, width:]
        nears.append(jnp.where(even, first, second))
        fars.append(jnp.where(even, second, first))
        kept_a[2 * low + high, i] = nears[i][:cut]
        sent_a[2 * low + high, i] = fars[i][:cut]

    @pl.when(low == 0)
    def _():
        for i in range(n):
            kept_b[2 * high, i] = nears[i][cut:]
            kept_b[2 * high + 1, i] = fars[i][cut:]

    @pl.when(low == 1)
    def _():
        for i in range(n):
            sent_b[2 * high, i] = nears[i][cut:]
            sent_b[2 * high + 1, i] = fars[i][cut:]


def unit_parts(ids, lefts, rights):
    n = len(lefts)
    total, model = rights[0].shape
    hidden = lefts[0].shape[0]
    shape = (4, n, hidden // 2, model // 8)
    return pl.pallas_call(
        unit_parts_kernel,
        out_shape=[jax.ShapeDtypeStruct(shape, bf16)] * 4,
        grid_spec=pltpu.PrefetchScalarGridSpec(
            num_scalar_prefetch=1,
            grid=(4,),
            in_specs=[whole(a.shape) for a in lefts] + [pl.BlockSpec((total, model // 4), lambda i, ids: (0, i ^ (ids[3] // 2)))] * n,
            out_specs=[whole(shape)] * 4,
        ),
        compiler_params=params(),
        cost_estimate=estimate(),
        name="unit_parts",
    )(ids, *lefts, *rights)


def unit_sums_kernel(n, split, *refs):
    out_ref = refs[-1]
    for i in range(n):
        out = dot(refs[i][...], refs[n + i][...]).astype(bf16)
        width = out.shape[1] // split
        for part in range(split):
            out_ref[part, i] = out[:, part * width : part * width + width]


def unit_sums(lefts, rights, shards):
    n = len(lefts)
    total, model = rights[0].shape
    hidden = lefts[0].shape[0]
    cut = model // shards
    step = 256
    split = step // cut if cut % 128 == 0 else 1
    out = pl.pallas_call(
        functools.partial(unit_sums_kernel, n, split),
        out_shape=jax.ShapeDtypeStruct((model // step * split, n, hidden, step // split), bf16),
        grid=(model // step,),
        in_specs=[whole(a.shape) for a in lefts] + [pl.BlockSpec((total, step), lambda i: (0, i))] * n,
        out_specs=pl.BlockSpec((split, n, hidden, step // split), lambda i: (i, 0, 0, 0)),
        compiler_params=params(),
        cost_estimate=estimate(),
        name="unit_sums",
    )(*lefts, *rights)
    if split == 1:
        out = out.reshape(model // step, n, hidden, step // cut, cut)
        out = out.transpose(0, 3, 1, 2, 4).reshape(shards, n, hidden, cut)
    return out


def head_sums_kernel(shards, ids, normed_ref, da_ref, g_ref, ctx_ref, ka_ref, sa_ref, kb_ref, sb_ref, acc, turned):
    outs = ((ka_ref, sa_ref), (kb_ref, sb_ref))
    cut = acc.shape[0] // shards
    turned[...] = normed_ref[...].T
    acc[:, 0:768] = dot(turned[...], g_ref[...])
    turned[...] = da_ref[...].T
    acc[:, 768:] = dot(turned[...], ctx_ref[...])
    for group, order in enumerate(bit_orders(shards)):
        for flip in range(shards):
            sent, place = slot_of(flip, order)
            at = (ids[3] ^ flip) * cut + group * (cut // 2)
            rows = pl.ds(pl.multiple_of(at, cut // 2), cut // 2)
            outs[group][sent][place] = acc[rows, :].astype(bf16)


def head_sums(ids, normed, d_attn, grads, context, shards):
    total, model = normed.shape
    columns = grads.shape[1] + context.shape[1]
    shape = (shards // 2, model // shards // 2, columns)
    ins = [(a, whole(a.shape)) for a in (normed, d_attn, grads, context)]
    return pl.pallas_call(
        functools.partial(head_sums_kernel, shards),
        out_shape=[jax.ShapeDtypeStruct(shape, bf16)] * 4,
        grid_spec=pltpu.PrefetchScalarGridSpec(
            num_scalar_prefetch=1,
            grid=(1,),
            in_specs=[spec for _, spec in ins],
            out_specs=[whole(shape)] * 4,
            scratch_shapes=[pltpu.VMEM((model, columns), f32), pltpu.VMEM((model, total), bf16)],
        ),
        compiler_params=params(),
        cost_estimate=estimate(),
        name="head_sums",
    )(ids, *(a for a, _ in ins))


def swap(sent, bit, n_dp):
    return lax.ppermute(sent, "dp", [(i, i ^ (1 << bit)) for i in range(n_dp)])


def call(kernel, ids, ins, outs, grid, name):
    return pl.pallas_call(
        kernel,
        out_shape=[jax.ShapeDtypeStruct(shape, kind) for shape, kind, _ in outs],
        grid_spec=pltpu.PrefetchScalarGridSpec(
            num_scalar_prefetch=1,
            grid=grid,
            in_specs=[spec for _, spec in ins],
            out_specs=[spec for _, _, spec in outs],
        ),
        compiler_params=params(),
        cost_estimate=estimate(),
        name=name,
    )(ids, *(array for array, _ in ins))


def out_kernel(ids, ka_ref, ca_ref, kb_ref, cb_ref, send_ref, own_ref):
    sum_a = ka_ref[...].astype(f32) + ca_ref[...].astype(f32)
    sum_b = kb_ref[...].astype(f32) + cb_ref[...].astype(f32)
    first = ids[2] == 0
    send_ref[...] = jnp.where(first, sum_b, sum_a).astype(bf16)
    own_ref[...] = jnp.where(first, sum_a, sum_b)


def out_sums(ids, keep, core):
    rows, model = keep.shape[0] // 2, keep.shape[1]
    low = pl.BlockSpec((rows // 2, model), lambda i, ids: (i, 0))
    high = pl.BlockSpec((rows // 2, model), lambda i, ids: (2 + i, 0))
    ins = [(keep, low), (core, low), (keep, high), (core, high)]
    return call(out_kernel, ids, ins, [((rows, model), bf16, low), ((rows, model), f32, low)], (2,), "out_sums")


def result_kernel(ids, mixed_ref, own_ref, far_ref, out_ref):
    out_ref[...] = mixed_ref[...] + own_ref[...] + far_ref[...].astype(f32)


def result_of(ids, mixed, own, far):
    rows, model = own.shape
    spec = pl.BlockSpec((rows // 2, model), lambda i, ids: (i, 0))
    ins = [(mixed, pl.BlockSpec((rows // 2, model), lambda i, ids: (2 * ids[2] + i, 0))), (own, spec), (far, spec)]
    return call(result_kernel, ids, ins, [(own.shape, f32, spec)], (2,), "result_of")[0]


def onward_kernel(n, ids, *refs):
    for i in range(n):
        low, high, came_low, came_high = refs[4 * i : 4 * i + 4]
        keep, send = refs[4 * n + 2 * i : 4 * n + 2 * i + 2]
        keep[...] = (low[...].astype(f32) + came_low[...].astype(f32)).astype(bf16)
        send[...] = (high[...].astype(f32) + came_high[...].astype(f32)).astype(bf16)


def onward(ids, kept, came):
    ins, outs = [], []
    half = kept[0].shape[0] // 2
    for k, c in zip(kept, came, strict=True):
        block = (1,) + k.shape[1:]
        rest = (0,) * (k.ndim - 1)
        low = pl.BlockSpec(block, lambda i, ids, rest=rest: (i,) + rest)
        high = pl.BlockSpec(block, lambda i, ids, rest=rest: (half + i,) + rest)
        ins += [(k, low), (k, high), (c, low), (c, high)]
        outs += [((half,) + k.shape[1:], bf16, low)] * 2
    got = call(functools.partial(onward_kernel, len(kept)), ids, ins, outs, (half,), "onward")
    return got[0::2], got[1::2]


def unit_last_kernel(ids, ka, ca, kb, cb, *outs):
    cut = ka.shape[2]
    for i, out in enumerate(outs):
        out[0:cut, :] = ka[0, i].astype(f32) + ca[0, i].astype(f32)
        out[cut:, :] = kb[0, i].astype(f32) + cb[0, i].astype(f32)


def unit_last(ids, kept, came):
    _, n, cut, columns = kept[0].shape
    ins = [(a, whole(a.shape)) for a in (kept[0], came[0], kept[1], came[1])]
    outs = [((2 * cut, columns), f32, whole((2 * cut, columns)))] * n
    return call(unit_last_kernel, ids, ins, outs, (1,), "unit_last")


def head_last_kernel(ids, ka, ca, kb, cb, *outs):
    rows = ka.shape[1]
    both = jnp.concatenate([k[0].astype(f32) + c[0].astype(f32) for k, c in ((ka, ca), (kb, cb))], axis=0)
    for i, out in enumerate(outs[:3]):
        out[:, 0:128] = both[:, 128 * i : 128 * i + 128]
        out[:, 128:256] = both[:, 384 + 128 * i : 512 + 128 * i]
    outs[3][...] = both[:, 768:].T


def head_last(ids, kept, came):
    _, rows, columns = kept[0].shape
    ins = [(a, whole(a.shape)) for a in (kept[0], came[0], kept[1], came[1])]
    outs = [((2 * rows, 256), f32, whole((2 * rows, 256)))] * 3 + [((256, 2 * rows), f32, whole((256, 2 * rows)))]
    return call(head_last_kernel, ids, ins, outs, (1,), "head_last")


def local(
    tokens, w_query, w_key, w_value, w_attn_out, w_gate, w_up, w_down, norm_attn, norm_ffn,
    rel_table, x_table, y_table, lengths, boxes, cotangent,
):
    n_mp, n_dp = lax.axis_size("mp"), lax.axis_size("dp")
    me = lax.axis_index("mp")
    core, chip = me % 2, me // 2
    ids = jnp.stack([me, core, chip, lax.axis_index("dp")]).astype(i32)
    rows, model = tokens.shape

    def by_core(a):
        return lax.ppermute(a, "mp", [(i, i ^ 1) for i in range(n_mp)])

    def by_chip(a):
        return lax.ppermute(a, "mp", [(i, i ^ 2) for i in range(n_mp)])

    def together(*arrays):
        return lax.optimization_barrier(arrays)

    def after(a, *earlier):
        return lax.optimization_barrier((a, *earlier))[0]

    def exchange_small(a):
        return lax.all_to_all(a, ("dp", "mp"), split_axis=0, concat_axis=0, tiled=True)

    n_heads = w_query.shape[1] // HEAD
    tables = jnp.concatenate([rel_table.T, x_table.T, y_table.T, jnp.zeros((16 - 3 * n_heads, NB), f32)], axis=0)
    box_cols = boxes.T
    gain_attn, gain_ffn = norm_attn.reshape(1, model), norm_ffn.reshape(1, model)
    weights = (w_query, w_key, w_value)
    w_gate_t, w_up_t = w_gate.T, w_up.T

    x_chip = by_chip(tokens)
    group = project(ids, False, (tokens, by_core(tokens)), gain_attn, weights, [], n_mp)
    w_pairs = [jnp.concatenate([w[:, at : at + 128] for w in weights], axis=1) for at in (0, 128)]
    x_chip, _, box_cols, tables, *w_pairs = together(x_chip, group[0], box_cols, tables, *w_pairs)
    x_both = by_core(x_chip)
    w_chip = by_chip(after(w_attn_out, x_chip))
    c_chip = by_chip(after(cotangent, x_chip))
    group = project(ids, True, (x_chip, x_both), gain_attn, weights, group, n_mp)
    x_all, normed, queries, keys_all, values_all = group

    *kept, own_a = attend(0, queries, keys_all, values_all, tables, lengths, box_cols, boxes, [])
    core_a, far_a = by_core(own_a), by_chip(own_a)
    *kept, own_b = attend(1, after(queries, own_a), keys_all, values_all, tables, lengths, box_cols, boxes, kept)
    context, ctxt, factors, probs = kept
    own_b, core_a, far_a, w_chip, c_chip = together(own_b, core_a, far_a, w_chip, c_chip)
    core_b, far_b = by_core(own_b), by_chip(own_b)
    w_outs = (w_attn_out, by_core(w_attn_out), w_chip, by_core(w_chip))
    cot_all = assemble(ids, (cotangent, by_core(cotangent), c_chip, by_core(c_chip)))
    both_a = by_core(far_a)
    cot_all, far_b = together(cot_all, far_b)
    contexts = ((own_a, core_a, far_a, both_a), (own_b, core_b, far_b, by_core(far_b)))

    out = ffn(ids, contexts, x_all, cot_all, w_outs, gain_ffn, w_gate_t, w_up_t, w_down)
    mixed, normed_ffn, hidden, d_gate, d_up, d_send, d_keep, r_send, r_keep = out
    d_core = by_core(d_send)
    sums = (d_keep.astype(f32) + d_core.astype(f32)).astype(bf16)
    far_sums = by_chip(sums)
    r_core = by_core(after(r_send, sums))

    orders = bit_orders(n_dp)
    pairwise = n_dp == 8 and model == 1024
    unit_args = ((d_gate, d_up, hidden), (normed_ffn, normed_ffn, after(cot_all, sums)))
    if pairwise:
        unit = list(unit_parts(ids, *unit_args))
        r_out, r_own = out_sums(ids, r_keep, r_core)
        unit[0], unit[2], far_sums, r_out = together(unit[0], unit[2], far_sums, r_out)
        unit_came = [swap(unit[2 * i + 1], order[0], n_dp) for i, order in enumerate(orders)]
    else:
        unit = [unit_sums(*unit_args, n_dp)]
        r_out, r_own = out_sums(ids, r_keep, r_core)
        *unit, far_sums, r_out = together(*unit, far_sums, r_out)
        ffn_sums = lax.psum_scatter(unit[0], "dp", scatter_dimension=0, tiled=True)[0].astype(f32)
    d_mixed, d_own, gain_mid = mid(ids, sums, far_sums, mixed, cot_all, gain_ffn)
    d_core = by_core(d_own)

    r_far = by_chip(r_out)
    d_heads, d_tab, d_attn = attend_back(
        ids, queries, keys_all, values_all, d_own, d_core, w_attn_out, ctxt, factors, probs, lengths, box_cols, boxes
    )
    d_heads, r_far = together(d_heads, r_far)

    def swaps(sends, step):
        return [swap(send, order[step], n_dp) for send, order in zip(sends, orders, strict=True)]

    d_first = d_heads
    if pairwise:
        unit_came = together(*unit_came, d_heads)[:2]
        unit_kept, sends = onward(ids, unit[0::2], unit_came)
        unit_came = swaps(sends, 1)
        d_first = after(d_heads, *sends)
    f_send, f_keep, n_send, n_keep = project_back(ids, d_first, w_pairs)
    f_core, n_core = by_core(f_send), by_core(n_send)
    if pairwise:
        attn = head_sums(ids, normed, d_attn, after(d_heads, f_keep), context, n_dp)
        f_core, n_core, *attn = together(f_core, n_core, *attn)
        unit_came = together(*unit_came, attn[0])[:2]
        unit_kept, sends = onward(ids, unit_kept, unit_came)
        unit_came = swaps(sends, 2)
        f_core = after(f_core, *sends)
        came = swaps(attn[1::2], 0)
    f_sum = (f_keep + f_core.astype(f32)).astype(bf16)
    far = by_chip(f_sum)
    if pairwise:
        came[0], came[1], f_sum = together(*came, f_sum)
        kept, sends = onward(ids, attn[0::2], came)
        came = swaps(sends, 1)
        far = after(far, *sends)
    d_tokens, gain_first = last(ids, n_keep, n_core, far, tokens, gain_attn, d_mixed)

    gains = jnp.concatenate([gain_first, gain_mid], axis=0).reshape(2, n_dp, n_mp, -1).transpose(1, 2, 0, 3)
    n_gain = gains.shape[3]
    tabs = d_tab[:, : 3 * n_heads].reshape(n_dp, 1, -1)
    tabs = jnp.where(lax.broadcasted_iota(i32, (1, n_mp, 1), 1) == me, tabs, 0.0)
    small = jnp.concatenate([gains.reshape(n_dp, n_mp, 2 * n_gain), tabs], axis=2).reshape(n_dp * n_mp, -1)
    if pairwise:
        unit_came[0], unit_came[1], small = together(*unit_came, small)
        small = exchange_small(small)
        ffn_sums = unit_last(ids, unit_kept, unit_came)
        came[0], came[1], *ffn_sums = together(*came, *ffn_sums)
        kept, sends = onward(ids, kept, came)
        came = swaps(sends, 2)
        small = after(small, *sends).sum(axis=0)
        result = result_of(ids, mixed, r_own, after(r_far, *sends))
        came[0], came[1], result = together(*came, result)
        attn_sums = head_last(ids, kept, came)
    else:
        result = result_of(ids, mixed, r_own, r_far)
        wide = dot_tn(normed, d_heads)
        parts = [wide[:, 384 * pair + 128 * i : 384 * pair + 128 * i + 128] for i in range(3) for pair in range(2)]
        wide = [*parts, dot_tn(d_attn, context)]
        wide = jnp.concatenate(wide, axis=1).astype(bf16)
        wide = lax.psum_scatter(wide, "dp", scatter_dimension=0, tiled=True).astype(f32)
        attn_sums = [wide[:, 256 * i : 256 * i + 256] for i in range(4)]
        attn_sums[3] = attn_sums[3].T
        small = exchange_small(small).sum(axis=0)
    tabs = small[2 * n_gain :].reshape(-1, 3, n_heads)
    return (
        result, d_tokens,
        *attn_sums,
        ffn_sums[0].T, ffn_sums[1].T, ffn_sums[2],
        small[:n_gain], small[n_gain : 2 * n_gain], tabs[:, 0], tabs[:, 1], tabs[:, 2],
    )


def solution(mesh):
    in_specs = (
        P(("dp", "mp"), None),
        P(None, "mp"),
        P(None, "mp"),
        P(None, "mp"),
        P("mp", None),
        P(None, "mp"),
        P(None, "mp"),
        P("mp", None),
        P(),
        P(),
        P(None, "mp"),
        P(None, "mp"),
        P(None, "mp"),
        P("dp", None),
        P(None, "dp"),
        P(("dp", "mp"), None),
    )
    out_specs = (
        P(("dp", "mp"), None),
        P(("dp", "mp"), None),
        P("dp", "mp"),
        P("dp", "mp"),
        P("dp", "mp"),
        P("mp", "dp"),
        P("dp", "mp"),
        P("dp", "mp"),
        P("mp", "dp"),
        P(("dp", "mp")),
        P(("dp", "mp")),
        P("dp", "mp"),
        P("dp", "mp"),
        P("dp", "mp"),
    )
    return jax.shard_map(local, mesh=mesh, in_specs=in_specs, out_specs=out_specs, check_vma=False)
```

profile of v0, /device:TPU:0, one launch (start us, length us, event | category | flops | bytes accessed | tf_op | source)
XLA Modules:
  0.0 231.1 jit_solution(1730616294884358341)
XLA Ops:
  1.2 2.6 %collective-permute-start = (bf16[256,1024]{1,0:T(8,128)(2,1)}, bf16[256,1024]{1,0:T(8,128)(2,1)}, u32[]{:S(2)}, u32[]{:S(2)}) collective-permute-start(bf16[256,1024]{1,0:T(8,128)(2,1)} %x_ref.1), channel_id=1, source_target_pairs={{0,2},{1,3},{2,0},{3,1},{4,6},{5,7},{6,4},{7,5},{8,10},{9,11},{10,... | collective-permute-start | bytes 1572872 | tf_op jit(solution)/shard_map/ppermute | solution.py:927
  3.8 1.1 fusion
  4.8 1.1 fusion.1
  6.0 1.0 copy.42
  7.1 0.6 pad_add_fusion.ids
  7.7 1.4 pad_maximum_fusion
  9.1 0.7 maximum_maximum_fusion.tab_ref
  9.8 0.8 copy-done.11
  10.6 4.7 %project.2 = (bf16[1024,1024]{1,0:T(8,128)(2,1)}, bf16[1024,1024]{1,0:T(8,128)(2,1)}, bf16[1024,256]{1,0:T(8,128)(2,1)}, bf16[1024,256]{1,0:T(8,128)(2,1)}, bf16[1024,256]{1,0:T(8,128)(2,1)}) custom-call(s32[4]{0:T(128)} %pad_add_fusion.ids, bf16[256,1024]{1,0:T(8,128)(2,1)} %x_ref.1, bf16[256,1024]{1,0:T(8,128)(2,1)} %copy-done.11, f32[1,1024]{1,0:T(1,128)} %bitcast.34, ...), custom_call_target="tpu_custom_call" | custom-call | flops 1000 | bytes 1000 | tf_op jit(solution)/shard_map/project/pallas_call | solution.py:503
  15.3 1.3 collective-permute-done.xa_ref
  16.6 1.8 collective-permute-start.5
  18.9 4.7 %project.3 = (bf16[1024,1024]{1,0:T(8,128)(2,1)}, bf16[1024,1024]{1,0:T(8,128)(2,1)}, bf16[1024,256]{1,0:T(8,128)(2,1)}, bf16[1024,256]{1,0:T(8,128)(2,1)}, bf16[1024,256]{1,0:T(8,128)(2,1)}) custom-call(s32[4]{0:T(128)} %pad_add_fusion.ids, ...), custom_call_target="tpu_custom_call", output_to_operand_aliasing={{0}: (7, {}), {1}: (8, {}), {2}: (9, {}), {3}: (10, {}), {4... | custom-call | flops 1000 | bytes 1000 | tf_op jit(solution)/shard_map/project/pallas_call | solution.py:503
  23.6 11.8 %attend.2 = (bf16[1024,256]{1,0:T(8,128)(2,1)}, f32[256,1024]{1,0:T(8,128)}, f32[8,1024]{1,0:T(8,128)}, bf16[4,1024,1024]{2,1,0:T(8,128)(2,1)}, bf16[512,256]{1,0:T(8,128)(2,1)}) custom-call(s32[1,2]{1,0:T(1,128)} %lens.5, f32[16,32]{1,0:T(8,128)} %maximum_maximum_fusion.tab_ref, s32[1024,2]{1,0:T(8,128)} %bitcast.26, s32[2,1024]{1,0:T(2,128)} %box_rows.5, ...), custom_call_target="tpu_custom_call" | custom-call | flops 1000 | bytes 1000 | tf_op jit(solution)/shard_map/attend/pallas_call | solution.py:236
  35.3 1.8 collective-permute-start.4
  37.6 11.8 %attend.3 = (bf16[1024,256]{1,0:T(8,128)(2,1)}, f32[256,1024]{1,0:T(8,128)}, f32[8,1024]{1,0:T(8,128)}, bf16[4,1024,1024]{2,1,0:T(8,128)(2,1)}, bf16[512,256]{1,0:T(8,128)(2,1)}) custom-call(s32[1,2]{1,0:T(1,128)} %lens.5, f32[16,32]{1,0:T(8,128)} %maximum_maximum_fusion.tab_ref, ...), custom_call_target="tpu_custom_call", output_to_operand_aliasing={{0}: (7, {}), {1}: (8, {}), {2}: (9, {}), {3}: (10, {})} | custom-call | flops 1000 | bytes 1000 | tf_op jit(solution)/shard_map/attend/pallas_call | solution.py:236
  50.6 1.2 collective-permute-done.10.refs_3_
  51.9 4.3 %assemble.1.cot_ref.refs_5_ = bf16[1024,1024]{1,0:T(8,128)(2,1)} custom-call(s32[4]{0:T(128)} %pad_add_fusion.ids, bf16[256,1024]{1,0:T(8,128)(2,1)} %refs_0_.1, bf16[256,1024]{1,0:T(8,128)(2,1)} %collective-permute-done.9.refs_1_, bf16[256,1024]{1,0:T(8,128)(2,1)} %collective-permute-done.6.refs_2_, bf16[256,1024]{1,0:T(8,128)(2,1)} %collective-permute-done.10.refs_3_), custom_call_target="tpu_custom_call" | custom-call | flops 1000 | bytes 1000 | tf_op jit(solution)/shard_map/assemble/pallas_call | solution.py:535
  56.3 2.3 %collective-permute-done.11.b2 = bf16[512,256]{1,0:T(8,128)(2,1)} collective-permute-done((bf16[512,256]{1,0:T(8,128)(2,1)}, bf16[512,256]{1,0:T(8,128)(2,1)}, u32[]{:S(2)}, u32[]{:S(2)}) %collective-permute-start.11) | collective-permute-done | bytes 262176 | tf_op jit(solution)/shard_map/ppermute | solution.py:927
  58.6 1.8 collective-permute-done.12.b3
  60.5 25.2 %ffn.1 = (f32[512,1024]{1,0:T(8,128)}, bf16[1024,1024]{1,0:T(8,128)(2,1)}, bf16[704,1024]{1,0:T(8,128)(2,1)}, bf16[704,1024]{1,0:T(8,128)(2,1)}, bf16[704,1024]{...) custom-call(s32[4]{0:T(128)} %pad_add_fusion.ids, ...), custom_call_target="tpu_custom_call" | custom-call | flops 1000 | bytes 1000 | tf_op jit(solution)/shard_map/ffn/pallas_call | solution.py:819
  85.9 2.7 %collective-permute-done.15 = bf16[512,1024]{1,0:T(8,128)(2,1)S(1)} collective-permute-done((bf16[512,1024]{1,0:T(8,128)(2,1)}, bf16[512,1024]{1,0:T(8,128)(2,1)S(1)}, u32[]{:S(2)}, u32[]{:S(2)}) %collective-permute-start.15) | collective-permute-done | bytes 1048608 | tf_op jit(solution)/shard_map/ppermute | solution.py:924
  88.6 2.6 %add_convert_fusion.a_ref = bf16[512,1024]{1,0:T(8,128)(2,1)} fusion(bf16[512,1024]{1,0:T(8,128)(2,1)S(1)} %collective-permute-done.15, bf16[512,1024]{1,0:T(8,128)(2,1)} %get-tuple-element.168), kind=kLoop, calls=%fused_computation | loop fusion | flops 2097152 | bytes 3145728 | tf_op jit(solution)/shard_map/convert_element_type | solution.py:970
  91.6 11.3 %unit_parts.1 = (bf16[4,3,352,128]{3,2,1,0:T(8,128)(2,1)}, bf16[4,3,352,128]{3,2,1,0:T(8,128)(2,1)}, bf16[4,3,352,128]{3,2,1,0:T(8,128)(2,1)}, bf16[4,3,352,128]{3,2,1,0:T(8,128)(2,1)}) custom-call(s32[4]{0:T(128)} %pad_add_fusion.ids, bf16[704,1024]{1,0:T(8,128)(2,1)} %get-tuple-element.170.refs_0_, bf16[704,1024]{1,0:T(8,128)(2,1)} %get-tuple-element.171.refs_1_, ...), custom_call_target="tpu_custom_call" | custom-call | flops 1000 | bytes 1000 | tf_op jit(solution)/shard_map/unit_parts/pallas_call | solution.py:731
  102.9 2.0 collective-permute-start.20
  104.9 1.6 collective-permute-start.21
  106.5 3.2 %out_sums.1 = (bf16[256,1024]{1,0:T(8,128)(2,1)}, f32[256,1024]{1,0:T(8,128)}) custom-call(s32[4]{0:T(128)} %pad_add_fusion.ids, bf16[512,1024]{1,0:T(8,128)(2,1)} %get-tuple-element.177.ka_ref.kb_ref, bf16[512,1024]{1,0:T(8,128)(2,1)} %collective-permute-done.17.ca_ref.cb_ref, bf16[512,1024]{1,0:T(8,128)(2,1)} %get-tuple-element.177.ka_ref.kb_ref, ...), custom_call_target="tpu_custom_call" | custom-call | flops 1000 | bytes 1000 | tf_op jit(solution)/shard_map/out_sums/pallas_call | solution.py:819
  109.7 7.3 %collective-permute-done.16.b_ref = bf16[512,1024]{1,0:T(8,128)(2,1)} collective-permute-done((bf16[512,1024]{1,0:T(8,128)(2,1)}, bf16[512,1024]{1,0:T(8,128)(2,1)}, u32[]{:S(2)}, u32[]{:S(2)}) %collective-permute-start.16) | collective-permute-done | bytes 1048608 | tf_op jit(solution)/shard_map/ppermute | solution.py:927
  117.1 5.8 %mid.1 = (f32[512,1024]{1,0:T(8,128)}, bf16[512,1024]{1,0:T(8,128)(2,1)}, f32[1,1024]{1,0:T(1,128)}) custom-call(s32[4]{0:T(128)} %pad_add_fusion.ids, bf16[512,1024]{1,0:T(8,128)(2,1)} %add_convert_fusion.a_ref, bf16[512,1024]{1,0:T(8,128)(2,1)} %collective-permute-done.16.b_ref, f32[512,1024]{1,0:T(8,128)} %get-tuple-element.182.mixed_ref, ...), custom_call_target="tpu_custom_call" | custom-call | flops 1000 | bytes 1000 | tf_op jit(solution)/shard_map/mid/pallas_call | solution.py:819
  123.3 2.6 %collective-permute-done.18.d1_ref.d3_ref = bf16[512,1024]{1,0:T(8,128)(2,1)} collective-permute-done((bf16[512,1024]{1,0:T(8,128)(2,1)}, bf16[512,1024]{1,0:T(8,128)(2,1)}, u32[]{:S(2)}, u32[]{:S(2)}) %collective-permute-start.18) | collective-permute-done | bytes 1048608 | tf_op jit(solution)/shard_map/ppermute | solution.py:924
  125.9 21.9 %attend_back.1 = (bf16[1024,768]{1,0:T(8,128)(2,1)}, f32[32,16]{1,0:T(8,128)}, bf16[1024,1024]{1,0:T(8,128)(2,1)}) custom-call(s32[4]{0:T(128)} %pad_add_fusion.ids, s32[1,2]{1,0:T(1,128)} %lens.5, s32[1024,2]{1,0:T(8,128)} %bitcast.28, s32[2,1024]{1,0:T(2,128)} %box_rows.5, bf16[1024,256]{1,0:T(8,128)(2,1)} %get-tuple-element.152.q_ref, ...), custom_call_target="tpu_custom_call" | custom-call | flops 1000 | bytes 1000 | tf_op jit(solution)/shard_map/attend_back/pallas_call | solution.py:423
  147.9 1.0 copy-done.1
  148.9 4.1 %onward.4 = (bf16[2,3,352,128]{3,2,1,0:T(8,128)(2,1)}, bf16[2,3,352,128]{3,2,1,0:T(8,128)(2,1)}, bf16[2,3,352,128]{3,2,1,0:T(8,128)(2,1)}, bf16[2,3,352,128]{3,2,1,0:T(8,128)(2,1)}) custom-call(s32[4]{0:T(128)} %pad_add_fusion.ids, bf16[4,3,352,128]{3,2,1,0:T(8,128)(2,1)} %get-tuple-element.190.refs_0_.refs_1_, ...), custom_call_target="tpu_custom_call" | custom-call | flops 1000 | bytes 1000 | tf_op jit(solution)/shard_map/onward/pallas_call | solution.py:819
  153.0 2.5 %collective-permute-start.26 = (bf16[2,3,352,128]{3,2,1,0:T(8,128)(2,1)}, bf16[2,3,352,128]{3,2,1,0:T(8,128)(2,1)S(1)}, u32[]{:S(2)}, u32[]{:S(2)}) collective-permute-start(bf16[2,3,352,128]{3,2,1,0:T(8,128)(2,1)} %get-tuple-element.196), channel_id=1, source_target_pairs={{0,8},{4,12},{8,0},{12,4},{16,24},{20,28},{24,16},{28,20},{1,9},{5... | collective-permute-start | bytes 1622024 | tf_op jit(solution)/shard_map/ppermute | solution.py:815
  155.5 3.4 %collective-permute-start.27 = (bf16[2,3,352,128]{3,2,1,0:T(8,128)(2,1)}, bf16[2,3,352,128]{3,2,1,0:T(8,128)(2,1)S(1)}, u32[]{:S(2)}, u32[]{:S(2)}) collective-permute-start(bf16[2,3,352,128]{3,2,1,0:T(8,128)(2,1)} %get-tuple-element.197), channel_id=1, source_target_pairs={{0,16},{4,20},{8,24},{12,28},{16,0},{20,4},{24,8},{28,12},{1,17},{... | collective-permute-start | bytes 1622024 | tf_op jit(solution)/shard_map/ppermute | solution.py:815
  158.9 7.5 %project_back.1 = (bf16[256,1024]{1,0:T(8,128)(2,1)}, f32[256,1024]{1,0:T(8,128)}, bf16[256,1024]{1,0:T(8,128)(2,1)}, f32[256,1024]{1,0:T(8,128)}) custom-call(s32[4]{0:T(128)} %pad_add_fusion.ids, bf16[1024,768]{1,0:T(8,128)(2,1)} %get-tuple-element.206.a_ref.b_ref.g_ref, bf16[1024,768]{1,0:T(8,128)(2,1)} %get-tuple-element.206.a_ref.b_ref.g_ref, ...), custom_call_target="tpu_custom_call" | custom-call | flops 1000 | bytes 1000 | tf_op jit(solution)/shard_map/project_back/pallas_call | solution.py:819
  166.9 7.3 %head_sums.1 = (bf16[4,64,1024]{2,1,0:T(8,128)(2,1)}, bf16[4,64,1024]{2,1,0:T(8,128)(2,1)}, bf16[4,64,1024]{2,1,0:T(8,128)(2,1)}, bf16[4,64,1024]{2,1,0:T(8,128)(2,1)}) custom-call(s32[4]{0:T(128)} %pad_add_fusion.ids, bf16[1024,1024]{1,0:T(8,128)(2,1)} %get-tuple-element.203.normed_ref, bf16[1024,1024]{1,0:T(8,128)(2,1)} %get-tuple-element.204.da_ref, ...), custom_call_target="tpu_custom_call" | custom-call | flops 1000 | bytes 1000 | tf_op jit(solution)/shard_map/head_sums/pallas_call | solution.py:798
  174.3 0.8 copy-done.12
  175.1 1.5 collective-permute-start.24
  176.7 3.3 %collective-permute-done.26.refs_2_.refs_3_ = bf16[2,3,352,128]{3,2,1,0:T(8,128)(2,1)S(1)} collective-permute-done((bf16[2,3,352,128]{3,2,1,0:T(8,128)(2,1)}, bf16[2,3,352,128]{3,2,1,0:T(8,128)(2,1)S(1)}, u32[]{:S(2)}, u32[]{:S(2)}) %collective-permute-start.26) | collective-permute-done | bytes 540704 | tf_op jit(solution)/shard_map/ppermute | solution.py:815
  180.0 2.8 %collective-permute-done.27.refs_6_.refs_7_ = bf16[2,3,352,128]{3,2,1,0:T(8,128)(2,1)S(1)} collective-permute-done((bf16[2,3,352,128]{3,2,1,0:T(8,128)(2,1)}, bf16[2,3,352,128]{3,2,1,0:T(8,128)(2,1)S(1)}, u32[]{:S(2)}, u32[]{:S(2)}) %collective-permute-start.27) | collective-permute-done | bytes 540704 | tf_op jit(solution)/shard_map/ppermute | solution.py:815
  182.8 0.8 copy-done.3
  183.6 3.2 %onward.5 = (bf16[1,3,352,128]{3,2,1,0:T(8,128)(2,1)}, bf16[1,3,352,128]{3,2,1,0:T(8,128)(2,1)}, bf16[1,3,352,128]{3,2,1,0:T(8,128)(2,1)}, bf16[1,3,352,128]{3,2,1,0:T(8,128)(2,1)}) custom-call(s32[4]{0:T(128)} %pad_add_fusion.ids, bf16[2,3,352,128]{3,2,1,0:T(8,128)(2,1)} %get-tuple-element.216.refs_0_.refs_1_, ...), custom_call_target="tpu_custom_call" | custom-call | flops 1000 | bytes 1000 | tf_op jit(solution)/shard_map/onward/pallas_call | solution.py:819
  186.8 1.5 add_convert_fusion.1
  188.4 0.6 collective-permute-start.32
  189.7 1.5 collective-permute-start.31
  191.1 3.1 %collective-permute-done.25.refs_6_.refs_7_ = bf16[4,64,1024]{2,1,0:T(8,128)(2,1)} collective-permute-done((bf16[4,64,1024]{2,1,0:T(8,128)(2,1)}, bf16[4,64,1024]{2,1,0:T(8,128)(2,1)}, u32[]{:S(2)}, u32[]{:S(2)}) %collective-permute-start.25) | collective-permute-done | bytes 524320 | tf_op jit(solution)/shard_map/ppermute | solution.py:815
  194.2 3.1 %onward.6 = (bf16[2,64,1024]{2,1,0:T(8,128)(2,1)}, bf16[2,64,1024]{2,1,0:T(8,128)(2,1)}, bf16[2,64,1024]{2,1,0:T(8,128)(2,1)}, bf16[2,64,1024]{2,1,0:T(8,128)(2,1)}) custom-call(s32[4]{0:T(128)} %pad_add_fusion.ids, bf16[4,64,1024]{2,1,0:T(8,128)(2,1)} %get-tuple-element.212.refs_0_.refs_1_, bf16[4,64,1024]{2,1,0:T(8,128)(2,1)} %get-tuple-element.212.refs_0_.refs_1_, ...), custom_call_target="tpu_custom_call" | custom-call | flops 1000 | bytes 1000 | tf_op jit(solution)/shard_map/onward/pallas_call | solution.py:819
  197.4 0.6 collective-permute-start.28
  198.0 2.2 collective-permute-start.29
  200.2 4.5 %last.1 = (f32[256,1024]{1,0:T(8,128)}, f32[1,1024]{1,0:T(1,128)}) custom-call(s32[4]{0:T(128)} %pad_add_fusion.ids, f32[256,1024]{1,0:T(8,128)} %get-tuple-element.230.keep_ref, bf16[256,1024]{1,0:T(8,128)(2,1)} %collective-permute-done.23.core_ref, bf16[256,1024]{1,0:T(8,128)(2,1)} %collective-permute-done.32.y_ref, bf16[256,1024]{1,0:T(8,128)(2,1)} %x_ref.1, ...), custom_call_target="tpu_custom_call" | custom-call | flops 1000 | bytes 1000 | tf_op jit(solution)/shard_map/last/pallas_call | solution.py:819
  204.7 0.7 pad_maximum_fusion.3
  205.6 0.7 pad_maximum_fusion.2
  206.3 5.4 %all-to-all-start = ((f32[32,1,112]{2,1,0:T(1,128)}), f32[32,1,112]{2,1,0:T(1,128)S(1)}, u32[]{:S(2)}, u32[]{:S(2)}) async-start(f32[32,1,112]{2,1,0:T(1,128)} %bitcast.17), calls=%async_computation | async-start | bytes 32768 | tf_op jit(solution)/shard_map/all_to_all | solution.py:936
  211.7 2.9 %unit_last.1 = (f32[704,128]{1,0:T(8,128)}, f32[704,128]{1,0:T(8,128)}, f32[704,128]{1,0:T(8,128)}) custom-call(s32[4]{0:T(128)} %pad_add_fusion.ids, bf16[1,3,352,128]{3,2,1,0:T(8,128)(2,1)} %get-tuple-element.229.ka, bf16[1,3,352,128]{3,2,1,0:T(8,128)(2,1)} %copy-done.13, bf16[1,3,352,128]{3,2,1,0:T(8,128)(2,1)} %get-tuple-element.238.kb, ...), custom_call_target="tpu_custom_call" | custom-call | flops 1000 | bytes 1000 | tf_op jit(solution)/shard_map/unit_last/pallas_call | solution.py:819
  214.6 0.7 copy-done.6
  215.4 2.8 %onward.7 = (bf16[1,64,1024]{2,1,0:T(8,128)(2,1)}, bf16[1,64,1024]{2,1,0:T(8,128)(2,1)}, bf16[1,64,1024]{2,1,0:T(8,128)(2,1)}, bf16[1,64,1024]{2,1,0:T(8,128)(2,1)}) custom-call(s32[4]{0:T(128)} %pad_add_fusion.ids, bf16[2,64,1024]{2,1,0:T(8,128)(2,1)} %get-tuple-element.226.refs_0_.refs_1_, bf16[2,64,1024]{2,1,0:T(8,128)(2,1)} %get-tuple-element.226.refs_0_.refs_1_, ...), custom_call_target="tpu_custom_call" | custom-call | flops 1000 | bytes 1000 | tf_op jit(solution)/shard_map/onward/pallas_call | solution.py:819
  218.2 2.7 %collective-permute-start.33 = (bf16[1,64,1024]{2,1,0:T(8,128)(2,1)}, bf16[1,64,1024]{2,1,0:T(8,128)(2,1)S(1)}, u32[]{:S(2)}, u32[]{:S(2)}) collective-permute-start(bf16[1,64,1024]{2,1,0:T(8,128)(2,1)} %get-tuple-element.246), channel_id=1, source_target_pairs={{0,16},{4,20},{8,24},{12,28},{16,0},{20,4},{24,8},{28,12},{1,17},{... | collective-permute-start | bytes 393224 | tf_op jit(solution)/shard_map/ppermute | solution.py:815
  220.9 1.5 collective-permute-start.34
  222.5 0.6 fusion.3
  223.1 3.2 %result_of.1 = f32[256,1024]{1,0:T(8,128)} custom-call(s32[4]{0:T(128)} %pad_add_fusion.ids, f32[512,1024]{1,0:T(8,128)} %get-tuple-element.182.mixed_ref, f32[256,1024]{1,0:T(8,128)} %get-tuple-element.248.own_ref, bf16[256,1024]{1,0:T(8,128)(2,1)} %copy-done.9), custom_call_target="tpu_custom_call" | custom-call | flops 1000 | bytes 1000 | tf_op jit(solution)/shard_map/result_of/pallas_call | solution.py:819
  226.3 0.6 fusion.4
  226.9 0.9 collective-permute-done.33.ca
  227.8 0.6 copy-done.18
  228.5 2.6 %head_last.1 = (f32[128,256]{1,0:T(8,128)}, f32[128,256]{1,0:T(8,128)}, f32[128,256]{1,0:T(8,128)}, f32[256,128]{1,0:T(8,128)}) custom-call(s32[4]{0:T(128)} %pad_add_fusion.ids, bf16[1,64,1024]{2,1,0:T(8,128)(2,1)} %get-tuple-element.253.ka, bf16[1,64,1024]{2,1,0:T(8,128)(2,1)} %copy-done.18, bf16[1,64,1024]{2,1,0:T(8,128)(2,1)} %get-tuple-element.255.kb, ...), custom_call_target="tpu_custom_call" | custom-call | flops 1000 | bytes 1000 | tf_op jit(solution)/shard_map/head_last/pallas_call | solution.py:819
  (105 shorter events, 6.0 us)
Async XLA Ops:
  0.6 5.3 %copy-start = (bf16[1024,256]{1,0:T(8,128)(2,1)S(1)}, bf16[1024,256]{1,0:T(8,128)(2,1)}, u32[]{:S(2)}) copy-start(bf16[1024,256]{1,0:T(8,128)(2,1)} %wv_ref.3) | copy-start | bytes 1572868
  0.7 5.3 %copy-start.17 = (s32[2,1024]{1,0:T(2,128)S(1)}, s32[2,1024]{1,0:T(2,128)}, u32[]{:S(2)}) copy-start(s32[2,1024]{1,0:T(2,128)} %box_rows.5) | copy-start | bytes 24580
  0.7 9.1 %collective-permute-start.1 = (bf16[256,1024]{1,0:T(8,128)(2,1)}, bf16[256,1024]{1,0:T(8,128)(2,1)S(1)}, u32[]{:S(2)}, u32[]{:S(2)}) collective-permute-start(bf16[256,1024]{1,0:T(8,128)(2,1)} %x_ref.1), channel_id=1, source_target_pairs={{0,1},{1,0},{2,3},{3,2},{4,5},{5,4},{6,7},{7,6},{8,9},{9,8},{10,11... | collective-permute-start | bytes 1572872 | tf_op jit(solution)/shard_map/ppermute | solution.py:924
  1.2 15.4 %collective-permute-start = (bf16[256,1024]{1,0:T(8,128)(2,1)}, bf16[256,1024]{1,0:T(8,128)(2,1)}, u32[]{:S(2)}, u32[]{:S(2)}) collective-permute-start(bf16[256,1024]{1,0:T(8,128)(2,1)} %x_ref.1), channel_id=1, source_target_pairs={{0,2},{1,3},{2,0},{3,1},{4,6},{5,7},{6,4},{7,5},{8,10},{9,11},{10,... | collective-permute-start | bytes 1572872 | tf_op jit(solution)/shard_map/ppermute | solution.py:927
  7.7 1.4 copy-start.22
  7.7 1.4 copy-start.23
  7.7 1.4 copy-start.24
  9.1 7.6 %copy-start.5 = (bf16[256,1024]{1,0:T(8,128)(2,1)S(1)}, bf16[256,1024]{1,0:T(8,128)(2,1)}, u32[]{:S(2)}) copy-start(bf16[256,1024]{1,0:T(8,128)(2,1)} %wo_ref.1) | copy-start | bytes 1572868
  9.1 9.3 %copy-start.8 = (bf16[256,1024]{1,0:T(8,128)(2,1)S(1)}, bf16[256,1024]{1,0:T(8,128)(2,1)}, u32[]{:S(2)}) copy-start(bf16[256,1024]{1,0:T(8,128)(2,1)} %refs_0_.1) | copy-start | bytes 1572868
  9.8 0.8 copy-start.11
  16.6 2.3 collective-permute-start.2
  16.6 32.8 %collective-permute-start.5 = (bf16[256,1024]{1,0:T(8,128)(2,1)S(1)}, bf16[256,1024]{1,0:T(8,128)(2,1)S(1)}, u32[]{:S(2)}, u32[]{:S(2)}) collective-permute-start(bf16[256,1024]{1,0:T(8,128)(2,1)S(1)} %copy-done.5), channel_id=1, source_target_pairs={{0,2},{1,3},{2,0},{3,1},{4,6},{5,7},{6,4},{7,5},{8,10},{9,11},{10,... | collective-permute-start | bytes 1572872 | tf_op jit(solution)/shard_map/ppermute | solution.py:927
  18.4 31.1 %collective-permute-start.6 = (bf16[256,1024]{1,0:T(8,128)(2,1)S(1)}, bf16[256,1024]{1,0:T(8,128)(2,1)}, u32[]{:S(2)}, u32[]{:S(2)}) collective-permute-start(bf16[256,1024]{1,0:T(8,128)(2,1)S(1)} %copy-done.8), channel_id=1, source_target_pairs={{0,2},{1,3},{2,0},{3,1},{4,6},{5,7},{6,4},{7,5},{8,10},{9,11},{10,... | collective-permute-start | bytes 1572872 | tf_op jit(solution)/shard_map/ppermute | solution.py:927
  35.3 14.1 %collective-permute-start.4 = (bf16[512,256]{1,0:T(8,128)(2,1)}, bf16[512,256]{1,0:T(8,128)(2,1)S(1)}, u32[]{:S(2)}, u32[]{:S(2)}) collective-permute-start(bf16[512,256]{1,0:T(8,128)(2,1)} %get-tuple-element.151.a0), channel_id=1, source_target_pairs={{0,2},{1,3},{2,0},{3,1},{4,6},{5,7},{6,4},{7,5},{8,10},{9,11},{10,... | collective-permute-start | bytes 786440 | tf_op jit(solution)/shard_map/ppermute | solution.py:927
  37.1 12.4 %collective-permute-start.3 = (bf16[512,256]{1,0:T(8,128)(2,1)}, bf16[512,256]{1,0:T(8,128)(2,1)}, u32[]{:S(2)}, u32[]{:S(2)}) collective-permute-start(bf16[512,256]{1,0:T(8,128)(2,1)} %get-tuple-element.151.a0), channel_id=1, source_target_pairs={{0,1},{1,0},{2,3},{3,2},{4,5},{5,4},{6,7},{7,6},{8,9},{9,8},{10,11... | collective-permute-start | bytes 786440 | tf_op jit(solution)/shard_map/ppermute | solution.py:924
  37.1 13.3 %collective-permute-start.9 = (bf16[256,1024]{1,0:T(8,128)(2,1)S(1)}, bf16[256,1024]{1,0:T(8,128)(2,1)}, u32[]{:S(2)}, u32[]{:S(2)}) collective-permute-start(bf16[256,1024]{1,0:T(8,128)(2,1)S(1)} %copy-done.8), channel_id=1, source_target_pairs={{0,1},{1,0},{2,3},{3,2},{4,5},{5,4},{6,7},{7,6},{8,9},{9,8},{10,11... | collective-permute-start | bytes 1572872 | tf_op jit(solution)/shard_map/ppermute | solution.py:924
  49.4 6.9 %copy-start.10 = (bf16[256,1024]{1,0:T(8,128)(2,1)}, bf16[256,1024]{1,0:T(8,128)(2,1)S(1)}, u32[]{:S(2)}) copy-start(bf16[256,1024]{1,0:T(8,128)(2,1)S(1)} %collective-permute-done.5.o2) | copy-start | bytes 1572868
  49.5 6.8 %copy-start.14 = (bf16[512,256]{1,0:T(8,128)(2,1)}, bf16[512,256]{1,0:T(8,128)(2,1)S(1)}, u32[]{:S(2)}) copy-start(bf16[512,256]{1,0:T(8,128)(2,1)S(1)} %collective-permute-done.4.a2) | copy-start | bytes 786436
  49.5 2.3 %collective-permute-start.10 = (bf16[256,1024]{1,0:T(8,128)(2,1)}, bf16[256,1024]{1,0:T(8,128)(2,1)}, u32[]{:S(2)}, u32[]{:S(2)}) collective-permute-start(bf16[256,1024]{1,0:T(8,128)(2,1)} %collective-permute-done.6.refs_2_), channel_id=1, source_target_pairs={{0,1},{1,0},{2,3},{3,2},{4,5},{5,4},{6,7},{7,6},{8,9},{9,8},{10,11... | collective-permute-start | bytes 1572872 | tf_op jit(solution)/shard_map/ppermute | solution.py:924
  49.6 9.0 %collective-permute-start.11 = (bf16[512,256]{1,0:T(8,128)(2,1)}, bf16[512,256]{1,0:T(8,128)(2,1)}, u32[]{:S(2)}, u32[]{:S(2)}) collective-permute-start(bf16[512,256]{1,0:T(8,128)(2,1)} %get-tuple-element.162.b0), channel_id=1, source_target_pairs={{0,2},{1,3},{2,0},{3,1},{4,6},{5,7},{6,4},{7,5},{8,10},{9,11},{10,... | collective-permute-start | bytes 786440 | tf_op jit(solution)/shard_map/ppermute | solution.py:927
  49.9 8.7 %collective-permute-start.13 = (bf16[256,1024]{1,0:T(8,128)(2,1)S(1)}, bf16[256,1024]{1,0:T(8,128)(2,1)}, u32[]{:S(2)}, u32[]{:S(2)}) collective-permute-start(bf16[256,1024]{1,0:T(8,128)(2,1)S(1)} %copy-done.5), channel_id=1, source_target_pairs={{0,1},{1,0},{2,3},{3,2},{4,5},{5,4},{6,7},{7,6},{8,9},{9,8},{10,11... | collective-permute-start | bytes 1572872 | tf_op jit(solution)/shard_map/ppermute | solution.py:924
  50.1 8.6 %collective-permute-start.14 = (bf16[256,1024]{1,0:T(8,128)(2,1)S(1)}, bf16[256,1024]{1,0:T(8,128)(2,1)}, u32[]{:S(2)}, u32[]{:S(2)}) collective-permute-start(bf16[256,1024]{1,0:T(8,128)(2,1)S(1)} %collective-permute-done.5.o2), channel_id=1, source_target_pairs={{0,1},{1,0},{2,3},{3,2},{4,5},{5,4},{6,7},{7,6},{8,9},{9,8},{10,11... | collective-permute-start | bytes 1572872 | tf_op jit(solution)/shard_map/ppermute | solution.py:924
  50.4 8.2 %collective-permute-start.8 = (bf16[512,256]{1,0:T(8,128)(2,1)}, bf16[512,256]{1,0:T(8,128)(2,1)S(1)}, u32[]{:S(2)}, u32[]{:S(2)}) collective-permute-start(bf16[512,256]{1,0:T(8,128)(2,1)} %get-tuple-element.162.b0), channel_id=1, source_target_pairs={{0,1},{1,0},{2,3},{3,2},{4,5},{5,4},{6,7},{7,6},{8,9},{9,8},{10,11... | collective-permute-start | bytes 786440 | tf_op jit(solution)/shard_map/ppermute | solution.py:924
  51.8 6.8 %collective-permute-start.7 = (bf16[512,256]{1,0:T(8,128)(2,1)S(1)}, bf16[512,256]{1,0:T(8,128)(2,1)S(1)}, u32[]{:S(2)}, u32[]{:S(2)}) collective-permute-start(bf16[512,256]{1,0:T(8,128)(2,1)S(1)} %collective-permute-done.4.a2), channel_id=1, source_target_pairs={{0,1},{1,0},{2,3},{3,2},{4,5},{5,4},{6,7},{7,6},{8,9},{9,8},{10,11... | collective-permute-start | bytes 786440 | tf_op jit(solution)/shard_map/ppermute | solution.py:924
  58.6 1.9 collective-permute-start.12
  58.6 1.9 copy-start.16
  58.6 1.8 copy-start.15
  85.7 2.9 %collective-permute-start.15 = (bf16[512,1024]{1,0:T(8,128)(2,1)}, bf16[512,1024]{1,0:T(8,128)(2,1)S(1)}, u32[]{:S(2)}, u32[]{:S(2)}) collective-permute-start(bf16[512,1024]{1,0:T(8,128)(2,1)} %get-tuple-element.169), channel_id=1, source_target_pairs={{0,1},{1,0},{2,3},{3,2},{4,5},{5,4},{6,7},{7,6},{8,9},{9,8},{10,11... | collective-permute-start | bytes 3145736 | tf_op jit(solution)/shard_map/ppermute | solution.py:924
  91.2 15.3 %collective-permute-start.17 = (bf16[512,1024]{1,0:T(8,128)(2,1)}, bf16[512,1024]{1,0:T(8,128)(2,1)}, u32[]{:S(2)}, u32[]{:S(2)}) collective-permute-start(bf16[512,1024]{1,0:T(8,128)(2,1)} %get-tuple-element.179), channel_id=1, source_target_pairs={{0,1},{1,0},{2,3},{3,2},{4,5},{5,4},{6,7},{7,6},{8,9},{9,8},{10,11... | collective-permute-start | bytes 3145736 | tf_op jit(solution)/shard_map/ppermute | solution.py:924
  91.4 25.7 %collective-permute-start.16 = (bf16[512,1024]{1,0:T(8,128)(2,1)}, bf16[512,1024]{1,0:T(8,128)(2,1)}, u32[]{:S(2)}, u32[]{:S(2)}) collective-permute-start(bf16[512,1024]{1,0:T(8,128)(2,1)} %add_convert_fusion.a_ref), channel_id=1, source_target_pairs={{0,2},{1,3},{2,0},{3,1},{4,6},{5,7},{6,4},{7,5},{8,10},{9,11},{10,... | collective-permute-start | bytes 3145736 | tf_op jit(solution)/shard_map/ppermute | solution.py:927
  102.9 44.9 %collective-permute-start.20 = (bf16[4,3,352,128]{3,2,1,0:T(8,128)(2,1)}, bf16[4,3,352,128]{3,2,1,0:T(8,128)(2,1)S(1)}, u32[]{:S(2)}, u32[]{:S(2)}) collective-permute-start(bf16[4,3,352,128]{3,2,1,0:T(8,128)(2,1)} %get-tuple-element.191), channel_id=1, source_target_pairs={{0,4},{4,0},{8,12},{12,8},{16,20},{20,16},{24,28},{28,24},{1,5},{5... | collective-permute-start | bytes 3244040 | tf_op jit(solution)/shard_map/ppermute | solution.py:815
  104.9 43.0 %collective-permute-start.21 = (bf16[4,3,352,128]{3,2,1,0:T(8,128)(2,1)}, bf16[4,3,352,128]{3,2,1,0:T(8,128)(2,1)}, u32[]{:S(2)}, u32[]{:S(2)}) collective-permute-start(bf16[4,3,352,128]{3,2,1,0:T(8,128)(2,1)} %get-tuple-element.192), channel_id=1, source_target_pairs={{0,8},{4,12},{8,0},{12,4},{16,24},{20,28},{24,16},{28,20},{1,9},{5... | collective-permute-start | bytes 3244040 | tf_op jit(solution)/shard_map/ppermute | solution.py:815
  122.8 3.0 %collective-permute-start.18 = (bf16[512,1024]{1,0:T(8,128)(2,1)}, bf16[512,1024]{1,0:T(8,128)(2,1)}, u32[]{:S(2)}, u32[]{:S(2)}) collective-permute-start(bf16[512,1024]{1,0:T(8,128)(2,1)} %get-tuple-element.183.d0_ref.d2_ref), channel_id=1, source_target_pairs={{0,1},{1,0},{2,3},{3,2},{4,5},{5,4},{6,7},{7,6},{8,9},{9,8},{10,11... | collective-permute-start | bytes 3145736 | tf_op jit(solution)/shard_map/ppermute | solution.py:924
  122.9 24.9 %collective-permute-start.19 = (bf16[256,1024]{1,0:T(8,128)(2,1)}, bf16[256,1024]{1,0:T(8,128)(2,1)S(1)}, u32[]{:S(2)}, u32[]{:S(2)}) collective-permute-start(bf16[256,1024]{1,0:T(8,128)(2,1)} %get-tuple-element.188), channel_id=1, source_target_pairs={{0,2},{1,3},{2,0},{3,1},{4,6},{5,7},{6,4},{7,5},{8,10},{9,11},{10,... | collective-permute-start | bytes 1572872 | tf_op jit(solution)/shard_map/ppermute | solution.py:927
  147.8 18.6 %copy-start.9 = (bf16[256,1024]{1,0:T(8,128)(2,1)}, bf16[256,1024]{1,0:T(8,128)(2,1)S(1)}, u32[]{:S(2)}) copy-start(bf16[256,1024]{1,0:T(8,128)(2,1)S(1)} %collective-permute-done.19.far_ref) | copy-start | bytes 1572868
  147.9 1.0 copy-start.1
  153.0 27.0 %collective-permute-start.26 = (bf16[2,3,352,128]{3,2,1,0:T(8,128)(2,1)}, bf16[2,3,352,128]{3,2,1,0:T(8,128)(2,1)S(1)}, u32[]{:S(2)}, u32[]{:S(2)}) collective-permute-start(bf16[2,3,352,128]{3,2,1,0:T(8,128)(2,1)} %get-tuple-element.196), channel_id=1, source_target_pairs={{0,8},{4,12},{8,0},{12,4},{16,24},{20,28},{24,16},{28,20},{1,9},{5... | collective-permute-start | bytes 1622024 | tf_op jit(solution)/shard_map/ppermute | solution.py:815
  155.5 27.3 %collective-permute-start.27 = (bf16[2,3,352,128]{3,2,1,0:T(8,128)(2,1)}, bf16[2,3,352,128]{3,2,1,0:T(8,128)(2,1)S(1)}, u32[]{:S(2)}, u32[]{:S(2)}) collective-permute-start(bf16[2,3,352,128]{3,2,1,0:T(8,128)(2,1)} %get-tuple-element.197), channel_id=1, source_target_pairs={{0,16},{4,20},{8,24},{12,28},{16,0},{20,4},{24,8},{28,12},{1,17},{... | collective-permute-start | bytes 1622024 | tf_op jit(solution)/shard_map/ppermute | solution.py:815
  166.4 7.8 %collective-permute-start.22 = (bf16[256,1024]{1,0:T(8,128)(2,1)}, bf16[256,1024]{1,0:T(8,128)(2,1)S(1)}, u32[]{:S(2)}, u32[]{:S(2)}) collective-permute-start(bf16[256,1024]{1,0:T(8,128)(2,1)} %get-tuple-element.201), channel_id=1, source_target_pairs={{0,1},{1,0},{2,3},{3,2},{4,5},{5,4},{6,7},{7,6},{8,9},{9,8},{10,11... | collective-permute-start | bytes 1572872 | tf_op jit(solution)/shard_map/ppermute | solution.py:924
  166.4 7.8 %collective-permute-start.23 = (bf16[256,1024]{1,0:T(8,128)(2,1)}, bf16[256,1024]{1,0:T(8,128)(2,1)}, u32[]{:S(2)}, u32[]{:S(2)}) collective-permute-start(bf16[256,1024]{1,0:T(8,128)(2,1)} %get-tuple-element.202), channel_id=1, source_target_pairs={{0,1},{1,0},{2,3},{3,2},{4,5},{5,4},{6,7},{7,6},{8,9},{9,8},{10,11... | collective-permute-start | bytes 1572872 | tf_op jit(solution)/shard_map/ppermute | solution.py:924
  174.3 0.8 copy-start.12
  175.1 16.1 %collective-permute-start.24 = (bf16[4,64,1024]{2,1,0:T(8,128)(2,1)}, bf16[4,64,1024]{2,1,0:T(8,128)(2,1)S(1)}, u32[]{:S(2)}, u32[]{:S(2)}) collective-permute-start(bf16[4,64,1024]{2,1,0:T(8,128)(2,1)} %get-tuple-element.213), channel_id=1, source_target_pairs={{0,4},{4,0},{8,12},{12,8},{16,20},{20,16},{24,28},{28,24},{1,5},{5... | collective-permute-start | bytes 1572872 | tf_op jit(solution)/shard_map/ppermute | solution.py:815
  176.6 17.6 %collective-permute-start.25 = (bf16[4,64,1024]{2,1,0:T(8,128)(2,1)}, bf16[4,64,1024]{2,1,0:T(8,128)(2,1)}, u32[]{:S(2)}, u32[]{:S(2)}) collective-permute-start(bf16[4,64,1024]{2,1,0:T(8,128)(2,1)} %get-tuple-element.214), channel_id=1, source_target_pairs={{0,8},{4,12},{8,0},{12,4},{16,24},{20,28},{24,16},{28,20},{1,9},{5... | collective-permute-start | bytes 1572872 | tf_op jit(solution)/shard_map/ppermute | solution.py:815
  180.0 2.9 %copy-start.2 = (bf16[2,3,352,128]{3,2,1,0:T(8,128)(2,1)}, bf16[2,3,352,128]{3,2,1,0:T(8,128)(2,1)S(1)}, u32[]{:S(2)}) copy-start(bf16[2,3,352,128]{3,2,1,0:T(8,128)(2,1)S(1)} %collective-permute-done.26.refs_2_.refs_3_) | copy-start | bytes 1622020
  182.8 0.8 copy-start.3
  186.8 2.2 copy-start.20
  188.4 11.9 %collective-permute-start.32 = (bf16[256,1024]{1,0:T(8,128)(2,1)S(1)}, bf16[256,1024]{1,0:T(8,128)(2,1)}, u32[]{:S(2)}, u32[]{:S(2)}) collective-permute-start(bf16[256,1024]{1,0:T(8,128)(2,1)S(1)} %add_convert_fusion.1), channel_id=1, source_target_pairs={{0,2},{1,3},{2,0},{3,1},{4,6},{5,7},{6,4},{7,5},{8,10},{9,11},{10,... | collective-permute-start | bytes 1572872 | tf_op jit(solution)/shard_map/ppermute | solution.py:927
  189.1 17.2 %collective-permute-start.30 = (bf16[1,3,352,128]{3,2,1,0:T(8,128)(2,1)}, bf16[1,3,352,128]{3,2,1,0:T(8,128)(2,1)S(1)}, u32[]{:S(2)}, u32[]{:S(2)}) collective-permute-start(bf16[1,3,352,128]{3,2,1,0:T(8,128)(2,1)} %get-tuple-element.220), channel_id=1, source_target_pairs={{0,16},{4,20},{8,24},{12,28},{16,0},{20,4},{24,8},{28,12},{1,17},{... | collective-permute-start | bytes 811016 | tf_op jit(solution)/shard_map/ppermute | solution.py:815
  189.7 16.7 %collective-permute-start.31 = (bf16[1,3,352,128]{3,2,1,0:T(8,128)(2,1)}, bf16[1,3,352,128]{3,2,1,0:T(8,128)(2,1)}, u32[]{:S(2)}, u32[]{:S(2)}) collective-permute-start(bf16[1,3,352,128]{3,2,1,0:T(8,128)(2,1)} %get-tuple-element.221), channel_id=1, source_target_pairs={{0,4},{4,0},{8,12},{12,8},{16,20},{20,16},{24,28},{28,24},{1,5},{5... | collective-permute-start | bytes 811016 | tf_op jit(solution)/shard_map/ppermute | solution.py:815
  191.1 3.1 %copy-start.4 = (bf16[4,64,1024]{2,1,0:T(8,128)(2,1)}, bf16[4,64,1024]{2,1,0:T(8,128)(2,1)S(1)}, u32[]{:S(2)}) copy-start(bf16[4,64,1024]{2,1,0:T(8,128)(2,1)S(1)} %collective-permute-done.24.refs_2_.refs_3_) | copy-start | bytes 1572868
  197.4 17.2 %collective-permute-start.28 = (bf16[2,64,1024]{2,1,0:T(8,128)(2,1)}, bf16[2,64,1024]{2,1,0:T(8,128)(2,1)S(1)}, u32[]{:S(2)}, u32[]{:S(2)}) collective-permute-start(bf16[2,64,1024]{2,1,0:T(8,128)(2,1)} %get-tuple-element.227), channel_id=1, source_target_pairs={{0,8},{4,12},{8,0},{12,4},{16,24},{20,28},{24,16},{28,20},{1,9},{5... | collective-permute-start | bytes 786440 | tf_op jit(solution)/shard_map/ppermute | solution.py:815
  198.0 16.7 %collective-permute-start.29 = (bf16[2,64,1024]{2,1,0:T(8,128)(2,1)}, bf16[2,64,1024]{2,1,0:T(8,128)(2,1)S(1)}, u32[]{:S(2)}, u32[]{:S(2)}) collective-permute-start(bf16[2,64,1024]{2,1,0:T(8,128)(2,1)} %get-tuple-element.228), channel_id=1, source_target_pairs={{0,16},{4,20},{8,24},{12,28},{16,0},{20,4},{24,8},{28,12},{1,17},{... | collective-permute-start | bytes 786440 | tf_op jit(solution)/shard_map/ppermute | solution.py:815
  200.2 4.5 %copy-start.21 = (f32[1,1024]{1,0:T(1,128)S(1)}, f32[1,1024]{1,0:T(1,128)}, u32[]{:S(2)}) copy-start(f32[1,1024]{1,0:T(1,128)} %get-tuple-element.235) | copy-start | bytes 12292
  206.3 5.4 %copy-start.13 = (bf16[1,3,352,128]{3,2,1,0:T(8,128)(2,1)}, bf16[1,3,352,128]{3,2,1,0:T(8,128)(2,1)S(1)}, u32[]{:S(2)}) copy-start(bf16[1,3,352,128]{3,2,1,0:T(8,128)(2,1)S(1)} %collective-permute-done.30.ca) | copy-start | bytes 811012
  206.3 16.0 %all-to-all-start = ((f32[32,1,112]{2,1,0:T(1,128)}), f32[32,1,112]{2,1,0:T(1,128)S(1)}, u32[]{:S(2)}, u32[]{:S(2)}) async-start(f32[32,1,112]{2,1,0:T(1,128)} %bitcast.17), calls=%async_computation | async-start | bytes 32768 | tf_op jit(solution)/shard_map/all_to_all | solution.py:936
  214.6 0.7 copy-start.6
  214.6 0.8 copy-start.7
  218.2 9.6 %collective-permute-start.33 = (bf16[1,64,1024]{2,1,0:T(8,128)(2,1)}, bf16[1,64,1024]{2,1,0:T(8,128)(2,1)S(1)}, u32[]{:S(2)}, u32[]{:S(2)}) collective-permute-start(bf16[1,64,1024]{2,1,0:T(8,128)(2,1)} %get-tuple-element.246), channel_id=1, source_target_pairs={{0,16},{4,20},{8,24},{12,28},{16,0},{20,4},{24,8},{28,12},{1,17},{... | collective-permute-start | bytes 393224 | tf_op jit(solution)/shard_map/ppermute | solution.py:815
  220.9 6.9 %collective-permute-start.34 = (bf16[1,64,1024]{2,1,0:T(8,128)(2,1)}, bf16[1,64,1024]{2,1,0:T(8,128)(2,1)S(1)}, u32[]{:S(2)}, u32[]{:S(2)}) collective-permute-start(bf16[1,64,1024]{2,1,0:T(8,128)(2,1)} %get-tuple-element.247), channel_id=1, source_target_pairs={{0,4},{4,0},{8,12},{12,8},{16,20},{20,16},{24,28},{28,24},{1,5},{5... | collective-permute-start | bytes 393224 | tf_op jit(solution)/shard_map/ppermute | solution.py:815
  227.8 0.7 copy-start.18
  227.8 0.7 copy-start.19
where the time goes:
time: 232 us; the launch traced here: 231 us
  Pallas kernels  146 us (63%)
  starting transfers between devices  36.3 us (16%)
  waiting for transfers between devices  29.8 us (13%)
  local copies, waits for them, and re-layouts  10 us (4%)
  other arithmetic  8.2 us (4%)
    pallas_call x12, Pallas kernels, call(): pl.pallas_call(kernel, out_shape=[jax.ShapeDtypeStruct(shape, kind) for s...  68 us
    pallas_call x2, Pallas kernels, attend(): pl.pallas_call(functools.partial(fwd_kernel, n_heads, qb, 2 * chunk), out...  23.5 us
    pallas_call x1, Pallas kernels, attend_back(): pl.pallas_call(functools.partial(bwd_kernel, n_heads, qb), out_shape=[jax...  21.9 us
    ppermute x12, starting transfers between devices, swap(): return lax.ppermute(sent, 'dp', [(i, i ^ 1 << bit) for i in range(n_dp)])  20 us
    pallas_call x1, Pallas kernels, unit_parts(): pl.pallas_call(unit_parts_kernel, out_shape=[jax.ShapeDtypeStruct(shape,...  11.3 us
    ppermute x8, waiting for transfers between devices, by_chip(): return lax.ppermute(a, 'mp', [(i, i ^ 2) for i in range(n_mp)])  11 us
    ppermute x12, waiting for transfers between devices, swap(): return lax.ppermute(sent, 'dp', [(i, i ^ 1 << bit) for i in range(n_dp)])  10.1 us
    pallas_call x2, Pallas kernels, project(): pl.pallas_call(qkv_kernel, out_shape=shapes, grid_spec=pltpu.PrefetchScal...  9.4 us
  transfers between devices with their start and end apart: 36, of which 12 were waited for; matrix products, arithmetic and copies ran while one was open for 5% of the time, Pallas kernels for 49%

commit v1 on v0

--- a/solution.py
+++ b/solution.py
@@ -222,7 +222,7 @@
 
 
 def params():
-    return pltpu.CompilerParams(dimension_semantics=("arbitrary",), vmem_limit_bytes=62 << 20)
+    return pltpu.CompilerParams(dimension_semantics=("arbitrary",), vmem_limit_bytes=255 << 18)
 
 
 def row_block(step, ids):
@@ -549,7 +549,7 @@
 
 def ffn_kernel(ids, a0, a1, a2, a3, b0, b1, b2, b3, x_ref, cot_ref, o0, o1, o2, o3, g_ref, wg_ref, wu_ref, wd_ref,
                mixed_ref, nf_ref, hid_ref, dg_ref, du_ref, dsend, dkeep, rsend, rkeep):
-    first = pl.program_id(0) < 2
+    first = pl.program_id(0) == 0
     mixed = x_ref[...].astype(f32)
     for a, b, o in ((a0, b0, o0), (a1, b1, o1), (a2, b2, o2), (a3, b3, o3)):
         mixed = mixed + dot(jnp.where(first, a[...], b[...]), o[...])
@@ -571,44 +571,28 @@
     du_ref[...] = d_up
     d_normed = (dot_tn(d_gate, wg_ref[...]) + dot_tn(d_up, wu_ref[...])).astype(bf16)
     down = dot_tn(hidden, wd_ref[...]).astype(bf16)
-    half = pl.program_id(0) % 2
-
-    @pl.when(half == 0)
-    def _():
-        dsend[...] = d_normed
-        rsend[...] = down
-
-    @pl.when(half == 1)
-    def _():
-        dkeep[...] = d_normed
-        rkeep[...] = down
-        mixed_ref[...] = mixed
+    rows = mixed.shape[0] // 2
+    lower = ids[1] == 0
+    for value, other, own in ((d_normed, dsend, dkeep), (down, rsend, rkeep)):
+        other[...] = jnp.where(lower, value[rows:], value[:rows])
+        own[...] = jnp.where(lower, value[:rows], value[rows:])
+    mixed_ref[...] = jnp.where(lower, mixed[:rows], mixed[rows:])
 
 
 def ffn(ids, contexts, x_all, cot_all, w_outs, gain, w_gate_t, w_up_t, w_down):
     total, model = x_all.shape
     rows = total // 4
-    width, hidden = contexts[0][0].shape[1], w_down.shape[0]
-
-    def local_row(i, ids):
-        return (i + 1 + ids[1]) % 2
-
-    def row(i, ids):
-        return i // 2 * 2 + local_row(i, ids)
-
-    def part(chunk):
-        return pl.BlockSpec((rows, width), lambda i, ids: (jnp.where(i // 2 == chunk, local_row(i, ids), ids[1] if chunk == 0 else 1 - ids[1]), 0))
-
-    rows_spec = pl.BlockSpec((rows, model), lambda i, ids: (row(i, ids), 0))
-    units_spec = pl.BlockSpec((hidden, rows), lambda i, ids: (0, row(i, ids)))
-    half_spec = pl.BlockSpec((rows, model), lambda i, ids: (i // 2, 0))
+    hidden = w_down.shape[0]
+    rows_spec = pl.BlockSpec((2 * rows, model), lambda i, ids: (i, 0))
+    units_spec = pl.BlockSpec((hidden, 2 * rows), lambda i, ids: (0, i))
+    half_spec = pl.BlockSpec((rows, model), lambda i, ids: (i, 0))
     outs = [((2 * rows, model), f32, half_spec), ((total, model), bf16, rows_spec)]
     outs += [((hidden, total), bf16, units_spec)] * 3
     outs += [((2 * rows, model), bf16, half_spec)] * 4
-    ins = [(a, part(chunk)) for chunk in range(2) for a in contexts[chunk]]
+    ins = [(a, whole(a.shape)) for chunk in range(2) for a in contexts[chunk]]
     ins += [(x_all, rows_spec), (cot_all, rows_spec)]
     ins += [(w, whole(w.shape)) for w in (*w_outs, gain, w_gate_t, w_up_t, w_down)]
-    return call(ffn_kernel, ids, ins, outs, (4,), "ffn")
+    return call(ffn_kernel, ids, ins, outs, (2,), "ffn")
 
 
 def norm_back(total, values, gain):
@@ -648,24 +632,25 @@
 
 def back_kernel(ids, a_ref, b_ref, wa_ref, wb_ref, *outs):
     total = dot_nt(a_ref[...], wa_ref[...]) + dot_nt(b_ref[...], wb_ref[...])
-    for at_step, out in enumerate(outs):
+    rows = total.shape[0] // 2
+    first = ids[1] == 0
+    other = jnp.where(first, total[rows:], total[:rows]).astype(bf16)
+    own = jnp.where(first, total[:rows], total[rows:])
+    for at_step in range(2):
 
         @pl.when(pl.program_id(0) == at_step)
         def _():
-            out[...] = total.astype(out.dtype)
+            outs[2 * at_step][...] = other
+            outs[2 * at_step + 1][...] = own
 
 
 def project_back(ids, grads, weights):
     total = grads.shape[0]
     rows, (model, width) = total // 4, weights[0].shape
-
-    def row(i, ids):
-        return 2 * ((1 - i // 2 + ids[2]) % 2) + (i + 1 + ids[1]) % 2
-
-    ins = [(grads, pl.BlockSpec((rows, width), lambda i, ids, at=at: (row(i, ids), at))) for at in range(2)]
+    ins = [(grads, pl.BlockSpec((2 * rows, width), lambda i, ids, at=at: ((1 - i + ids[2]) % 2, at))) for at in range(2)]
     ins += [(w, whole(w.shape)) for w in weights]
     outs = [((rows, model), kind, whole((rows, model))) for kind in (bf16, f32, bf16, f32)]
-    return call(back_kernel, ids, ins, outs, (4,), "project_back")
+    return call(back_kernel, ids, ins, outs, (2,), "project_back")
 
 
 def last_kernel(ids, keep_ref, core_ref, y_ref, x_ref, g_ref, dm_ref, out_ref, sum_ref):
@@ -1007,7 +992,8 @@
     if pairwise:
         attn = head_sums(ids, normed, d_attn, after(d_heads, f_keep), context, n_dp)
         f_core, n_core, *attn = together(f_core, n_core, *attn)
-        unit_came = together(*unit_came, attn[0])[:2]
+        result = result_of(ids, mixed, r_own, after(r_far, attn[0]))
+        *unit_came, result = together(*unit_came, result)
         unit_kept, sends = onward(ids, unit_kept, unit_came)
         unit_came = swaps(sends, 2)
         f_core = after(f_core, *sends)
@@ -1034,8 +1020,6 @@
         kept, sends = onward(ids, kept, came)
         came = swaps(sends, 2)
         small = after(small, *sends).sum(axis=0)
-        result = result_of(ids, mixed, r_own, after(r_far, *sends))
-        came[0], came[1], result = together(*came, result)
         attn_sums = head_last(ids, kept, came)
     else:
         result = result_of(ids, mixed, r_own, r_far)

time: 232 us -> 225 us (0.970)
  Pallas kernels: 146 us -> 140 us
  local copies, waits for them, and re-layouts: 10 us -> 5.71 us
  waiting for transfers between devices: 29.8 us -> 32.2 us
    pallas_call x12, Pallas kernels: 68 us -> 61.7 us  [call(): pl.pallas_call(kernel, out_shape=[jax.ShapeDtypeStruct(shape, kind) for s...]
    unnamed x51 -> x17, local copies, waits for them, and re-layouts: 6.03 us -> 1.74 us
  transfers between devices with their start and end apart: 36 -> 36, of which waited for: 12 -> 12; matrix products, arithmetic and copies ran while one was open for 5% -> 5% of each run, Pallas kernels for 49% -> 51%
where the time goes in v1:
time: 225 us; the launch traced here: 224 us
  Pallas kernels  140 us (62%)
  starting transfers between devices  36.1 us (16%)
  waiting for transfers between devices  32.2 us (14%)
  other arithmetic  9.06 us (4%)
  local copies, waits for them, and re-layouts  5.71 us (3%)
    pallas_call x12, Pallas kernels, call(): pl.pallas_call(kernel, out_shape=[jax.ShapeDtypeStruct(shape, kind) for s...  61.7 us
    pallas_call x2, Pallas kernels, attend(): pl.pallas_call(functools.partial(fwd_kernel, n_heads, qb, 2 * chunk), out...  23.6 us
    pallas_call x1, Pallas kernels, attend_back(): pl.pallas_call(functools.partial(bwd_kernel, n_heads, qb), out_shape=[jax...  22.2 us
    ppermute x12, starting transfers between devices, swap(): return lax.ppermute(sent, 'dp', [(i, i ^ 1 << bit) for i in range(n_dp)])  21.3 us
    ppermute x12, waiting for transfers between devices, swap(): return lax.ppermute(sent, 'dp', [(i, i ^ 1 << bit) for i in range(n_dp)])  12.2 us
    ppermute x8, waiting for transfers between devices, by_chip(): return lax.ppermute(a, 'mp', [(i, i ^ 2) for i in range(n_mp)])  11.4 us
    pallas_call x1, Pallas kernels, unit_parts(): pl.pallas_call(unit_parts_kernel, out_shape=[jax.ShapeDtypeStruct(shape,...  11.3 us
    pallas_call x2, Pallas kernels, project(): pl.pallas_call(qkv_kernel, out_shape=shapes, grid_spec=pltpu.PrefetchScal...  9.44 us
  transfers between devices with their start and end apart: 36, of which 12 were waited for; matrix products, arithmetic and copies ran while one was open for 5% of the time, Pallas kernels for 51%

profile of v1, /device:TPU:0, one launch (start us, length us, event | category | flops | bytes accessed | tf_op | source)
XLA Modules:
  0.0 223.5 jit_solution(14510112678130676317)
XLA Ops:
  0.7 0.5 collective-permute-start.1
  1.2 2.6 %collective-permute-start = (bf16[256,1024]{1,0:T(8,128)(2,1)}, bf16[256,1024]{1,0:T(8,128)(2,1)}, u32[]{:S(2)}, u32[]{:S(2)}) collective-permute-start(bf16[256,1024]{1,0:T(8,128)(2,1)} %x_ref.1), channel_id=1, source_target_pairs={{0,2},{1,3},{2,0},{3,1},{4,6},{5,7},{6,4},{7,5},{8,10},{9,11},{10,... | collective-permute-start | bytes 1572872 | tf_op jit(solution)/shard_map/ppermute | solution.py:912
  3.8 1.1 fusion
  4.8 1.1 fusion.1
  6.0 1.1 copy.42
  7.1 0.6 pad_add_fusion.ids
  7.8 1.3 pad_maximum_fusion
  9.1 0.7 maximum_maximum_fusion.tab_ref
  9.8 4.8 %project.2 = (bf16[1024,1024]{1,0:T(8,128)(2,1)}, bf16[1024,1024]{1,0:T(8,128)(2,1)}, bf16[1024,256]{1,0:T(8,128)(2,1)}, bf16[1024,256]{1,0:T(8,128)(2,1)}, bf16[1024,256]{1,0:T(8,128)(2,1)}) custom-call(s32[4]{0:T(128)} %pad_add_fusion.ids, bf16[256,1024]{1,0:T(8,128)(2,1)} %x_ref.1, bf16[256,1024]{1,0:T(8,128)(2,1)} %collective-permute-done.1.xb_ref, ...), custom_call_target="tpu_custom_call" | custom-call | flops 1000 | bytes 1000 | tf_op jit(solution)/shard_map/project/pallas_call | solution.py:503
  14.6 2.0 collective-permute-done.xa_ref
  16.6 1.8 collective-permute-start.5
  18.9 4.7 %project.3 = (bf16[1024,1024]{1,0:T(8,128)(2,1)}, bf16[1024,1024]{1,0:T(8,128)(2,1)}, bf16[1024,256]{1,0:T(8,128)(2,1)}, bf16[1024,256]{1,0:T(8,128)(2,1)}, bf16[1024,256]{1,0:T(8,128)(2,1)}) custom-call(s32[4]{0:T(128)} %pad_add_fusion.ids, ...), custom_call_target="tpu_custom_call", output_to_operand_aliasing={{0}: (7, {}), {1}: (8, {}), {2}: (9, {}), {3}: (10, {}), {4... | custom-call | flops 1000 | bytes 1000 | tf_op jit(solution)/shard_map/project/pallas_call | solution.py:503
  23.5 11.8 %attend.2 = (bf16[1024,256]{1,0:T(8,128)(2,1)}, f32[256,1024]{1,0:T(8,128)}, f32[8,1024]{1,0:T(8,128)}, bf16[4,1024,1024]{2,1,0:T(8,128)(2,1)}, bf16[512,256]{1,0:T(8,128)(2,1)}) custom-call(s32[1,2]{1,0:T(1,128)} %lens.5, f32[16,32]{1,0:T(8,128)} %maximum_maximum_fusion.tab_ref, s32[1024,2]{1,0:T(8,128)} %bitcast.26, s32[2,1024]{1,0:T(2,128)} %box_rows.5, ...), custom_call_target="tpu_custom_call" | custom-call | flops 1000 | bytes 1000 | tf_op jit(solution)/shard_map/attend/pallas_call | solution.py:236
  35.3 1.8 collective-permute-start.4
  37.1 0.5 collective-permute-start.9
  37.6 11.8 %attend.3 = (bf16[1024,256]{1,0:T(8,128)(2,1)}, f32[256,1024]{1,0:T(8,128)}, f32[8,1024]{1,0:T(8,128)}, bf16[4,1024,1024]{2,1,0:T(8,128)(2,1)}, bf16[512,256]{1,0:T(8,128)(2,1)}) custom-call(s32[1,2]{1,0:T(1,128)} %lens.5, f32[16,32]{1,0:T(8,128)} %maximum_maximum_fusion.tab_ref, ...), custom_call_target="tpu_custom_call", output_to_operand_aliasing={{0}: (7, {}), {1}: (8, {}), {2}: (9, {}), {3}: (10, {})} | custom-call | flops 1000 | bytes 1000 | tf_op jit(solution)/shard_map/attend/pallas_call | solution.py:236
  50.6 1.2 collective-permute-done.10.refs_3_
  51.9 4.3 %assemble.1.cot_ref.refs_5_ = bf16[1024,1024]{1,0:T(8,128)(2,1)} custom-call(s32[4]{0:T(128)} %pad_add_fusion.ids, bf16[256,1024]{1,0:T(8,128)(2,1)} %refs_0_.1, bf16[256,1024]{1,0:T(8,128)(2,1)} %collective-permute-done.9.refs_1_, bf16[256,1024]{1,0:T(8,128)(2,1)} %collective-permute-done.6.refs_2_, bf16[256,1024]{1,0:T(8,128)(2,1)} %collective-permute-done.10.refs_3_), custom_call_target="tpu_custom_call" | custom-call | flops 1000 | bytes 1000 | tf_op jit(solution)/shard_map/assemble/pallas_call | solution.py:535
  56.3 2.3 %collective-permute-done.11.b2 = bf16[512,256]{1,0:T(8,128)(2,1)} collective-permute-done((bf16[512,256]{1,0:T(8,128)(2,1)}, bf16[512,256]{1,0:T(8,128)(2,1)}, u32[]{:S(2)}, u32[]{:S(2)}) %collective-permute-start.11) | collective-permute-done | bytes 262176 | tf_op jit(solution)/shard_map/ppermute | solution.py:912
  58.6 1.8 collective-permute-done.12.b3
  60.5 19.5 %ffn.1 = (f32[512,1024]{1,0:T(8,128)}, bf16[1024,1024]{1,0:T(8,128)(2,1)}, bf16[704,1024]{1,0:T(8,128)(2,1)}, bf16[704,1024]{1,0:T(8,128)(2,1)}, bf16[704,1024]{...) custom-call(s32[4]{0:T(128)} %pad_add_fusion.ids, ...), custom_call_target="tpu_custom_call" | custom-call | flops 1000 | bytes 1000 | tf_op jit(solution)/shard_map/ffn/pallas_call | solution.py:804
  80.2 2.7 %collective-permute-done.15 = bf16[512,1024]{1,0:T(8,128)(2,1)S(1)} collective-permute-done((bf16[512,1024]{1,0:T(8,128)(2,1)}, bf16[512,1024]{1,0:T(8,128)(2,1)S(1)}, u32[]{:S(2)}, u32[]{:S(2)}) %collective-permute-start.15) | collective-permute-done | bytes 1048608 | tf_op jit(solution)/shard_map/ppermute | solution.py:909
  82.9 2.6 %add_convert_fusion.a_ref = bf16[512,1024]{1,0:T(8,128)(2,1)} fusion(bf16[512,1024]{1,0:T(8,128)(2,1)S(1)} %collective-permute-done.15, bf16[512,1024]{1,0:T(8,128)(2,1)} %get-tuple-element.170), kind=kLoop, calls=%fused_computation | loop fusion | flops 2097152 | bytes 3145728 | tf_op jit(solution)/shard_map/convert_element_type | solution.py:955
  85.7 0.3 collective-permute-start.16
  86.0 11.3 %unit_parts.1 = (bf16[4,3,352,128]{3,2,1,0:T(8,128)(2,1)}, bf16[4,3,352,128]{3,2,1,0:T(8,128)(2,1)}, bf16[4,3,352,128]{3,2,1,0:T(8,128)(2,1)}, bf16[4,3,352,128]{3,2,1,0:T(8,128)(2,1)}) custom-call(s32[4]{0:T(128)} %pad_add_fusion.ids, bf16[704,1024]{1,0:T(8,128)(2,1)} %get-tuple-element.166.refs_0_, bf16[704,1024]{1,0:T(8,128)(2,1)} %get-tuple-element.167.refs_1_, ...), custom_call_target="tpu_custom_call" | custom-call | flops 1000 | bytes 1000 | tf_op jit(solution)/shard_map/unit_parts/pallas_call | solution.py:716
  97.3 1.9 collective-permute-start.18
  99.2 1.9 collective-permute-start.19
  101.1 3.2 %out_sums.1 = (bf16[256,1024]{1,0:T(8,128)(2,1)}, f32[256,1024]{1,0:T(8,128)}) custom-call(s32[4]{0:T(128)} %pad_add_fusion.ids, bf16[512,1024]{1,0:T(8,128)(2,1)} %get-tuple-element.175.ka_ref.kb_ref, bf16[512,1024]{1,0:T(8,128)(2,1)} %collective-permute-done.17.ca_ref.cb_ref, bf16[512,1024]{1,0:T(8,128)(2,1)} %get-tuple-element.175.ka_ref.kb_ref, ...), custom_call_target="tpu_custom_call" | custom-call | flops 1000 | bytes 1000 | tf_op jit(solution)/shard_map/out_sums/pallas_call | solution.py:804
  104.4 7.0 %collective-permute-done.16.b_ref = bf16[512,1024]{1,0:T(8,128)(2,1)} collective-permute-done((bf16[512,1024]{1,0:T(8,128)(2,1)}, bf16[512,1024]{1,0:T(8,128)(2,1)}, u32[]{:S(2)}, u32[]{:S(2)}) %collective-permute-start.16) | collective-permute-done | bytes 1048608 | tf_op jit(solution)/shard_map/ppermute | solution.py:912
  111.4 5.8 %mid.1 = (f32[512,1024]{1,0:T(8,128)}, bf16[512,1024]{1,0:T(8,128)(2,1)}, f32[1,1024]{1,0:T(1,128)}) custom-call(s32[4]{0:T(128)} %pad_add_fusion.ids, bf16[512,1024]{1,0:T(8,128)(2,1)} %add_convert_fusion.a_ref, bf16[512,1024]{1,0:T(8,128)(2,1)} %collective-permute-done.16.b_ref, f32[512,1024]{1,0:T(8,128)} %get-tuple-element.183.mixed_ref, ...), custom_call_target="tpu_custom_call" | custom-call | flops 1000 | bytes 1000 | tf_op jit(solution)/shard_map/mid/pallas_call | solution.py:804
  117.2 0.4 collective-permute-start.21
  117.6 2.6 %collective-permute-done.20.d1_ref.d3_ref = bf16[512,1024]{1,0:T(8,128)(2,1)} collective-permute-done((bf16[512,1024]{1,0:T(8,128)(2,1)}, bf16[512,1024]{1,0:T(8,128)(2,1)}, u32[]{:S(2)}, u32[]{:S(2)}) %collective-permute-start.20) | collective-permute-done | bytes 1048608 | tf_op jit(solution)/shard_map/ppermute | solution.py:909
  120.2 22.2 %attend_back.1 = (bf16[1024,768]{1,0:T(8,128)(2,1)}, f32[32,16]{1,0:T(8,128)}, bf16[1024,1024]{1,0:T(8,128)(2,1)}) custom-call(s32[4]{0:T(128)} %pad_add_fusion.ids, s32[1,2]{1,0:T(1,128)} %lens.5, s32[1024,2]{1,0:T(8,128)} %bitcast.28, s32[2,1024]{1,0:T(2,128)} %box_rows.5, bf16[1024,256]{1,0:T(8,128)(2,1)} %get-tuple-element.150.q_ref, ...), custom_call_target="tpu_custom_call" | custom-call | flops 1000 | bytes 1000 | tf_op jit(solution)/shard_map/attend_back/pallas_call | solution.py:423
  142.4 4.0 %onward.4 = (bf16[2,3,352,128]{3,2,1,0:T(8,128)(2,1)}, bf16[2,3,352,128]{3,2,1,0:T(8,128)(2,1)}, bf16[2,3,352,128]{3,2,1,0:T(8,128)(2,1)}, bf16[2,3,352,128]{3,2,1,0:T(8,128)(2,1)}) custom-call(s32[4]{0:T(128)} %pad_add_fusion.ids, bf16[4,3,352,128]{3,2,1,0:T(8,128)(2,1)} %get-tuple-element.179.refs_0_.refs_1_, ...), custom_call_target="tpu_custom_call" | custom-call | flops 1000 | bytes 1000 | tf_op jit(solution)/shard_map/onward/pallas_call | solution.py:804
  146.5 3.4 %collective-permute-start.22 = (bf16[2,3,352,128]{3,2,1,0:T(8,128)(2,1)}, bf16[2,3,352,128]{3,2,1,0:T(8,128)(2,1)}, u32[]{:S(2)}, u32[]{:S(2)}) collective-permute-start(bf16[2,3,352,128]{3,2,1,0:T(8,128)(2,1)} %get-tuple-element.194), channel_id=1, source_target_pairs={{0,8},{4,12},{8,0},{12,4},{16,24},{20,28},{24,16},{28,20},{1,9},{5... | collective-permute-start | bytes 1622024 | tf_op jit(solution)/shard_map/ppermute | solution.py:800
  149.8 2.6 %collective-permute-start.23 = (bf16[2,3,352,128]{3,2,1,0:T(8,128)(2,1)}, bf16[2,3,352,128]{3,2,1,0:T(8,128)(2,1)}, u32[]{:S(2)}, u32[]{:S(2)}) collective-permute-start(bf16[2,3,352,128]{3,2,1,0:T(8,128)(2,1)} %get-tuple-element.195), channel_id=1, source_target_pairs={{0,16},{4,20},{8,24},{12,28},{16,0},{20,4},{24,8},{28,12},{1,17},{... | collective-permute-start | bytes 1622024 | tf_op jit(solution)/shard_map/ppermute | solution.py:800
  152.4 6.8 %project_back.1 = (bf16[256,1024]{1,0:T(8,128)(2,1)}, f32[256,1024]{1,0:T(8,128)}, bf16[256,1024]{1,0:T(8,128)(2,1)}, f32[256,1024]{1,0:T(8,128)}) custom-call(s32[4]{0:T(128)} %pad_add_fusion.ids, bf16[1024,768]{1,0:T(8,128)(2,1)} %get-tuple-element.206.a_ref.b_ref.g_ref, bf16[1024,768]{1,0:T(8,128)(2,1)} %get-tuple-element.206.a_ref.b_ref.g_ref, ...), custom_call_target="tpu_custom_call" | custom-call | flops 1000 | bytes 1000 | tf_op jit(solution)/shard_map/project_back/pallas_call | solution.py:804
  159.2 0.5 collective-permute-start.25
  159.7 7.1 %head_sums.1 = (bf16[4,64,1024]{2,1,0:T(8,128)(2,1)}, bf16[4,64,1024]{2,1,0:T(8,128)(2,1)}, bf16[4,64,1024]{2,1,0:T(8,128)(2,1)}, bf16[4,64,1024]{2,1,0:T(8,128)(2,1)}) custom-call(s32[4]{0:T(128)} %pad_add_fusion.ids, bf16[1024,1024]{1,0:T(8,128)(2,1)} %get-tuple-element.203.normed_ref, bf16[1024,1024]{1,0:T(8,128)(2,1)} %get-tuple-element.204.da_ref, ...), custom_call_target="tpu_custom_call" | custom-call | flops 1000 | bytes 1000 | tf_op jit(solution)/shard_map/head_sums/pallas_call | solution.py:783
  166.9 1.6 collective-permute-start.27
  168.5 3.2 %result_of.1 = f32[256,1024]{1,0:T(8,128)} custom-call(s32[4]{0:T(128)} %pad_add_fusion.ids, f32[512,1024]{1,0:T(8,128)} %get-tuple-element.183.mixed_ref, f32[256,1024]{1,0:T(8,128)} %get-tuple-element.196.own_ref, bf16[256,1024]{1,0:T(8,128)(2,1)} %collective-permute-done.21.far_ref), custom_call_target="tpu_custom_call" | custom-call | flops 1000 | bytes 1000 | tf_op jit(solution)/shard_map/result_of/pallas_call | solution.py:804
  171.7 3.0 %collective-permute-done.22.refs_2_.refs_3_ = bf16[2,3,352,128]{3,2,1,0:T(8,128)(2,1)} collective-permute-done((bf16[2,3,352,128]{3,2,1,0:T(8,128)(2,1)}, bf16[2,3,352,128]{3,2,1,0:T(8,128)(2,1)}, u32[]{:S(2)}, u32[]{:S(2)}) %collective-permute-start.22) | collective-permute-done | bytes 540704 | tf_op jit(solution)/shard_map/ppermute | solution.py:800
  174.7 1.3 collective-permute-done.23.refs_6_.refs_7_
  176.0 3.2 %onward.5 = (bf16[1,3,352,128]{3,2,1,0:T(8,128)(2,1)}, bf16[1,3,352,128]{3,2,1,0:T(8,128)(2,1)}, bf16[1,3,352,128]{3,2,1,0:T(8,128)(2,1)}, bf16[1,3,352,128]{3,2,1,0:T(8,128)(2,1)}) custom-call(s32[4]{0:T(128)} %pad_add_fusion.ids, bf16[2,3,352,128]{3,2,1,0:T(8,128)(2,1)} %get-tuple-element.218.refs_0_.refs_1_, ...), custom_call_target="tpu_custom_call" | custom-call | flops 1000 | bytes 1000 | tf_op jit(solution)/shard_map/onward/pallas_call | solution.py:804
  179.3 2.3 %add_convert_fusion.1 = bf16[256,1024]{1,0:T(8,128)(2,1)} fusion(f32[256,1024]{1,0:T(8,128)} %get-tuple-element.205, bf16[256,1024]{1,0:T(8,128)(2,1)} %collective-permute-done.24), kind=kLoop, calls=%fused_computation.1 | loop fusion | flops 786432 | bytes 2097152 | tf_op jit(solution)/shard_map/convert_element_type | solution.py:1001
  181.6 0.5 collective-permute-start.26
  182.3 1.7 collective-permute-start.31
  184.0 1.5 collective-permute-start.32
  185.5 3.8 %collective-permute-done.28.refs_6_.refs_7_ = bf16[4,64,1024]{2,1,0:T(8,128)(2,1)} collective-permute-done((bf16[4,64,1024]{2,1,0:T(8,128)(2,1)}, bf16[4,64,1024]{2,1,0:T(8,128)(2,1)}, u32[]{:S(2)}, u32[]{:S(2)}) %collective-permute-start.28) | collective-permute-done | bytes 524320 | tf_op jit(solution)/shard_map/ppermute | solution.py:800
  189.3 3.1 %onward.6 = (bf16[2,64,1024]{2,1,0:T(8,128)(2,1)}, bf16[2,64,1024]{2,1,0:T(8,128)(2,1)}, bf16[2,64,1024]{2,1,0:T(8,128)(2,1)}, bf16[2,64,1024]{2,1,0:T(8,128)(2,1)}) custom-call(s32[4]{0:T(128)} %pad_add_fusion.ids, bf16[4,64,1024]{2,1,0:T(8,128)(2,1)} %get-tuple-element.212.refs_0_.refs_1_, bf16[4,64,1024]{2,1,0:T(8,128)(2,1)} %get-tuple-element.212.refs_0_.refs_1_, ...), custom_call_target="tpu_custom_call" | custom-call | flops 1000 | bytes 1000 | tf_op jit(solution)/shard_map/onward/pallas_call | solution.py:804
  192.5 2.4 %collective-permute-start.30 = (bf16[2,64,1024]{2,1,0:T(8,128)(2,1)}, bf16[2,64,1024]{2,1,0:T(8,128)(2,1)}, u32[]{:S(2)}, u32[]{:S(2)}) collective-permute-start(bf16[2,64,1024]{2,1,0:T(8,128)(2,1)} %get-tuple-element.231), channel_id=1, source_target_pairs={{0,16},{4,20},{8,24},{12,28},{16,0},{20,4},{24,8},{28,12},{1,17},{... | collective-permute-start | bytes 786440 | tf_op jit(solution)/shard_map/ppermute | solution.py:800
  195.0 4.5 %last.1 = (f32[256,1024]{1,0:T(8,128)}, f32[1,1024]{1,0:T(1,128)}) custom-call(s32[4]{0:T(128)} %pad_add_fusion.ids, f32[256,1024]{1,0:T(8,128)} %get-tuple-element.215.keep_ref, bf16[256,1024]{1,0:T(8,128)(2,1)} %collective-permute-done.25.core_ref, bf16[256,1024]{1,0:T(8,128)(2,1)} %collective-permute-done.26.y_ref, bf16[256,1024]{1,0:T(8,128)(2,1)} %x_ref.1, ...), custom_call_target="tpu_custom_call" | custom-call | flops 1000 | bytes 1000 | tf_op jit(solution)/shard_map/last/pallas_call | solution.py:804
  199.5 0.7 pad_maximum_fusion.3
  200.4 0.7 pad_maximum_fusion.2
  201.1 3.9 %all-to-all-start = ((f32[32,1,112]{2,1,0:T(1,128)}), f32[32,1,112]{2,1,0:T(1,128)S(1)}, u32[]{:S(2)}, u32[]{:S(2)}) async-start(f32[32,1,112]{2,1,0:T(1,128)} %bitcast.17), calls=%async_computation | async-start | bytes 32768 | tf_op jit(solution)/shard_map/all_to_all | solution.py:921
  205.1 2.9 %unit_last.1 = (f32[704,128]{1,0:T(8,128)}, f32[704,128]{1,0:T(8,128)}, f32[704,128]{1,0:T(8,128)}) custom-call(s32[4]{0:T(128)} %pad_add_fusion.ids, bf16[1,3,352,128]{3,2,1,0:T(8,128)(2,1)} %get-tuple-element.236.ka, bf16[1,3,352,128]{3,2,1,0:T(8,128)(2,1)} %collective-permute-done.31.ca, bf16[1,3,352,128]{3,2,1,0:T(8,128)(2,1)} %get-tuple-element.241.kb, ...), custom_call_target="tpu_custom_call" | custom-call | flops 1000 | bytes 1000 | tf_op jit(solution)/shard_map/unit_last/pallas_call | solution.py:804
  207.9 2.8 %onward.7 = (bf16[1,64,1024]{2,1,0:T(8,128)(2,1)}, bf16[1,64,1024]{2,1,0:T(8,128)(2,1)}, bf16[1,64,1024]{2,1,0:T(8,128)(2,1)}, bf16[1,64,1024]{2,1,0:T(8,128)(2,1)}) custom-call(s32[4]{0:T(128)} %pad_add_fusion.ids, bf16[2,64,1024]{2,1,0:T(8,128)(2,1)} %get-tuple-element.235.refs_0_.refs_1_, bf16[2,64,1024]{2,1,0:T(8,128)(2,1)} %get-tuple-element.235.refs_0_.refs_1_, ...), custom_call_target="tpu_custom_call" | custom-call | flops 1000 | bytes 1000 | tf_op jit(solution)/shard_map/onward/pallas_call | solution.py:804
  210.7 2.7 %collective-permute-start.33 = (bf16[1,64,1024]{2,1,0:T(8,128)(2,1)}, bf16[1,64,1024]{2,1,0:T(8,128)(2,1)S(1)}, u32[]{:S(2)}, u32[]{:S(2)}) collective-permute-start(bf16[1,64,1024]{2,1,0:T(8,128)(2,1)} %get-tuple-element.250), channel_id=1, source_target_pairs={{0,16},{4,20},{8,24},{12,28},{16,0},{20,4},{24,8},{28,12},{1,17},{... | collective-permute-start | bytes 393224 | tf_op jit(solution)/shard_map/ppermute | solution.py:800
  213.4 1.5 collective-permute-start.34
  215.0 0.6 fusion.3
  215.6 0.6 fusion.4
  216.2 4.1 %collective-permute-done.33.ca = bf16[1,64,1024]{2,1,0:T(8,128)(2,1)S(1)} collective-permute-done((bf16[1,64,1024]{2,1,0:T(8,128)(2,1)}, bf16[1,64,1024]{2,1,0:T(8,128)(2,1)S(1)}, u32[]{:S(2)}, u32[]{:S(2)}) %collective-permute-start.33) | collective-permute-done | bytes 131104 | tf_op jit(solution)/shard_map/ppermute | solution.py:800
  220.3 0.6 copy-done.2
  220.9 2.6 %head_last.1 = (f32[128,256]{1,0:T(8,128)}, f32[128,256]{1,0:T(8,128)}, f32[128,256]{1,0:T(8,128)}, f32[256,128]{1,0:T(8,128)}) custom-call(s32[4]{0:T(128)} %pad_add_fusion.ids, bf16[1,64,1024]{2,1,0:T(8,128)(2,1)} %get-tuple-element.249.ka, bf16[1,64,1024]{2,1,0:T(8,128)(2,1)} %copy-done.2, bf16[1,64,1024]{2,1,0:T(8,128)(2,1)} %get-tuple-element.251.kb, ...), custom_call_target="tpu_custom_call" | custom-call | flops 1000 | bytes 1000 | tf_op jit(solution)/shard_map/head_last/pallas_call | solution.py:804
  (71 shorter events, 3.2 us)
Async XLA Ops:
  0.6 5.3 %copy-start = (bf16[1024,256]{1,0:T(8,128)(2,1)S(1)}, bf16[1024,256]{1,0:T(8,128)(2,1)}, u32[]{:S(2)}) copy-start(bf16[1024,256]{1,0:T(8,128)(2,1)} %wv_ref.3) | copy-start | bytes 1572868
  0.7 5.3 %copy-start.1 = (s32[2,1024]{1,0:T(2,128)S(1)}, s32[2,1024]{1,0:T(2,128)}, u32[]{:S(2)}) copy-start(s32[2,1024]{1,0:T(2,128)} %box_rows.5) | copy-start | bytes 24580
  0.7 9.2 %collective-permute-start.1 = (bf16[256,1024]{1,0:T(8,128)(2,1)}, bf16[256,1024]{1,0:T(8,128)(2,1)}, u32[]{:S(2)}, u32[]{:S(2)}) collective-permute-start(bf16[256,1024]{1,0:T(8,128)(2,1)} %x_ref.1), channel_id=1, source_target_pairs={{0,1},{1,0},{2,3},{3,2},{4,5},{5,4},{6,7},{7,6},{8,9},{9,8},{10,11... | collective-permute-start | bytes 1572872 | tf_op jit(solution)/shard_map/ppermute | solution.py:909
  1.2 15.4 %collective-permute-start = (bf16[256,1024]{1,0:T(8,128)(2,1)}, bf16[256,1024]{1,0:T(8,128)(2,1)}, u32[]{:S(2)}, u32[]{:S(2)}) collective-permute-start(bf16[256,1024]{1,0:T(8,128)(2,1)} %x_ref.1), channel_id=1, source_target_pairs={{0,2},{1,3},{2,0},{3,1},{4,6},{5,7},{6,4},{7,5},{8,10},{9,11},{10,... | collective-permute-start | bytes 1572872 | tf_op jit(solution)/shard_map/ppermute | solution.py:912
  7.8 1.4 copy-start.5
  7.8 1.4 copy-start.6
  7.8 1.4 copy-start.7
  16.6 2.3 %collective-permute-start.2 = (bf16[256,1024]{1,0:T(8,128)(2,1)}, bf16[256,1024]{1,0:T(8,128)(2,1)}, u32[]{:S(2)}, u32[]{:S(2)}) collective-permute-start(bf16[256,1024]{1,0:T(8,128)(2,1)} %collective-permute-done.xa_ref), channel_id=1, source_target_pairs={{0,1},{1,0},{2,3},{3,2},{4,5},{5,4},{6,7},{7,6},{8,9},{9,8},{10,11... | collective-permute-start | bytes 1572872 | tf_op jit(solution)/shard_map/ppermute | solution.py:909
  16.6 32.8 %collective-permute-start.5 = (bf16[256,1024]{1,0:T(8,128)(2,1)}, bf16[256,1024]{1,0:T(8,128)(2,1)}, u32[]{:S(2)}, u32[]{:S(2)}) collective-permute-start(bf16[256,1024]{1,0:T(8,128)(2,1)} %wo_ref.1), channel_id=1, source_target_pairs={{0,2},{1,3},{2,0},{3,1},{4,6},{5,7},{6,4},{7,5},{8,10},{9,11},{10,... | collective-permute-start | bytes 1572872 | tf_op jit(solution)/shard_map/ppermute | solution.py:912
  18.4 31.1 %collective-permute-start.6 = (bf16[256,1024]{1,0:T(8,128)(2,1)}, bf16[256,1024]{1,0:T(8,128)(2,1)}, u32[]{:S(2)}, u32[]{:S(2)}) collective-permute-start(bf16[256,1024]{1,0:T(8,128)(2,1)} %refs_0_.1), channel_id=1, source_target_pairs={{0,2},{1,3},{2,0},{3,1},{4,6},{5,7},{6,4},{7,5},{8,10},{9,11},{10,... | collective-permute-start | bytes 1572872 | tf_op jit(solution)/shard_map/ppermute | solution.py:912
  35.3 14.2 %collective-permute-start.4 = (bf16[512,256]{1,0:T(8,128)(2,1)}, bf16[512,256]{1,0:T(8,128)(2,1)}, u32[]{:S(2)}, u32[]{:S(2)}) collective-permute-start(bf16[512,256]{1,0:T(8,128)(2,1)} %get-tuple-element.149.a0), channel_id=1, source_target_pairs={{0,2},{1,3},{2,0},{3,1},{4,6},{5,7},{6,4},{7,5},{8,10},{9,11},{10,... | collective-permute-start | bytes 786440 | tf_op jit(solution)/shard_map/ppermute | solution.py:912
  37.1 12.4 %collective-permute-start.3 = (bf16[512,256]{1,0:T(8,128)(2,1)}, bf16[512,256]{1,0:T(8,128)(2,1)}, u32[]{:S(2)}, u32[]{:S(2)}) collective-permute-start(bf16[512,256]{1,0:T(8,128)(2,1)} %get-tuple-element.149.a0), channel_id=1, source_target_pairs={{0,1},{1,0},{2,3},{3,2},{4,5},{5,4},{6,7},{7,6},{8,9},{9,8},{10,11... | collective-permute-start | bytes 786440 | tf_op jit(solution)/shard_map/ppermute | solution.py:909
  37.1 13.3 %collective-permute-start.9 = (bf16[256,1024]{1,0:T(8,128)(2,1)}, bf16[256,1024]{1,0:T(8,128)(2,1)}, u32[]{:S(2)}, u32[]{:S(2)}) collective-permute-start(bf16[256,1024]{1,0:T(8,128)(2,1)} %refs_0_.1), channel_id=1, source_target_pairs={{0,1},{1,0},{2,3},{3,2},{4,5},{5,4},{6,7},{7,6},{8,9},{9,8},{10,11... | collective-permute-start | bytes 1572872 | tf_op jit(solution)/shard_map/ppermute | solution.py:909
  49.5 2.3 %collective-permute-start.10 = (bf16[256,1024]{1,0:T(8,128)(2,1)}, bf16[256,1024]{1,0:T(8,128)(2,1)}, u32[]{:S(2)}, u32[]{:S(2)}) collective-permute-start(bf16[256,1024]{1,0:T(8,128)(2,1)} %collective-permute-done.6.refs_2_), channel_id=1, source_target_pairs={{0,1},{1,0},{2,3},{3,2},{4,5},{5,4},{6,7},{7,6},{8,9},{9,8},{10,11... | collective-permute-start | bytes 1572872 | tf_op jit(solution)/shard_map/ppermute | solution.py:909
  49.6 9.0 %collective-permute-start.11 = (bf16[512,256]{1,0:T(8,128)(2,1)}, bf16[512,256]{1,0:T(8,128)(2,1)}, u32[]{:S(2)}, u32[]{:S(2)}) collective-permute-start(bf16[512,256]{1,0:T(8,128)(2,1)} %get-tuple-element.160.b0), channel_id=1, source_target_pairs={{0,2},{1,3},{2,0},{3,1},{4,6},{5,7},{6,4},{7,5},{8,10},{9,11},{10,... | collective-permute-start | bytes 786440 | tf_op jit(solution)/shard_map/ppermute | solution.py:912
  49.9 8.7 %collective-permute-start.13 = (bf16[256,1024]{1,0:T(8,128)(2,1)}, bf16[256,1024]{1,0:T(8,128)(2,1)}, u32[]{:S(2)}, u32[]{:S(2)}) collective-permute-start(bf16[256,1024]{1,0:T(8,128)(2,1)} %wo_ref.1), channel_id=1, source_target_pairs={{0,1},{1,0},{2,3},{3,2},{4,5},{5,4},{6,7},{7,6},{8,9},{9,8},{10,11... | collective-permute-start | bytes 1572872 | tf_op jit(solution)/shard_map/ppermute | solution.py:909
  50.1 8.5 %collective-permute-start.14 = (bf16[256,1024]{1,0:T(8,128)(2,1)}, bf16[256,1024]{1,0:T(8,128)(2,1)}, u32[]{:S(2)}, u32[]{:S(2)}) collective-permute-start(bf16[256,1024]{1,0:T(8,128)(2,1)} %collective-permute-done.5.o2), channel_id=1, source_target_pairs={{0,1},{1,0},{2,3},{3,2},{4,5},{5,4},{6,7},{7,6},{8,9},{9,8},{10,11... | collective-permute-start | bytes 1572872 | tf_op jit(solution)/shard_map/ppermute | solution.py:909
  50.4 8.2 %collective-permute-start.8 = (bf16[512,256]{1,0:T(8,128)(2,1)}, bf16[512,256]{1,0:T(8,128)(2,1)}, u32[]{:S(2)}, u32[]{:S(2)}) collective-permute-start(bf16[512,256]{1,0:T(8,128)(2,1)} %get-tuple-element.160.b0), channel_id=1, source_target_pairs={{0,1},{1,0},{2,3},{3,2},{4,5},{5,4},{6,7},{7,6},{8,9},{9,8},{10,11... | collective-permute-start | bytes 786440 | tf_op jit(solution)/shard_map/ppermute | solution.py:909
  51.8 6.8 %collective-permute-start.7 = (bf16[512,256]{1,0:T(8,128)(2,1)}, bf16[512,256]{1,0:T(8,128)(2,1)}, u32[]{:S(2)}, u32[]{:S(2)}) collective-permute-start(bf16[512,256]{1,0:T(8,128)(2,1)} %collective-permute-done.4.a2), channel_id=1, source_target_pairs={{0,1},{1,0},{2,3},{3,2},{4,5},{5,4},{6,7},{7,6},{8,9},{9,8},{10,11... | collective-permute-start | bytes 786440 | tf_op jit(solution)/shard_map/ppermute | solution.py:909
  58.6 1.9 collective-permute-start.12
  80.0 2.9 %collective-permute-start.15 = (bf16[512,1024]{1,0:T(8,128)(2,1)}, bf16[512,1024]{1,0:T(8,128)(2,1)S(1)}, u32[]{:S(2)}, u32[]{:S(2)}) collective-permute-start(bf16[512,1024]{1,0:T(8,128)(2,1)} %get-tuple-element.171), channel_id=1, source_target_pairs={{0,1},{1,0},{2,3},{3,2},{4,5},{5,4},{6,7},{7,6},{8,9},{9,8},{10,11... | collective-permute-start | bytes 3145736 | tf_op jit(solution)/shard_map/ppermute | solution.py:909
  85.5 15.6 %collective-permute-start.17 = (bf16[512,1024]{1,0:T(8,128)(2,1)}, bf16[512,1024]{1,0:T(8,128)(2,1)}, u32[]{:S(2)}, u32[]{:S(2)}) collective-permute-start(bf16[512,1024]{1,0:T(8,128)(2,1)} %get-tuple-element.177), channel_id=1, source_target_pairs={{0,1},{1,0},{2,3},{3,2},{4,5},{5,4},{6,7},{7,6},{8,9},{9,8},{10,11... | collective-permute-start | bytes 3145736 | tf_op jit(solution)/shard_map/ppermute | solution.py:909
  85.7 25.7 %collective-permute-start.16 = (bf16[512,1024]{1,0:T(8,128)(2,1)}, bf16[512,1024]{1,0:T(8,128)(2,1)}, u32[]{:S(2)}, u32[]{:S(2)}) collective-permute-start(bf16[512,1024]{1,0:T(8,128)(2,1)} %add_convert_fusion.a_ref), channel_id=1, source_target_pairs={{0,2},{1,3},{2,0},{3,1},{4,6},{5,7},{6,4},{7,5},{8,10},{9,11},{10,... | collective-permute-start | bytes 3145736 | tf_op jit(solution)/shard_map/ppermute | solution.py:912
  97.3 45.1 %collective-permute-start.18 = (bf16[4,3,352,128]{3,2,1,0:T(8,128)(2,1)}, bf16[4,3,352,128]{3,2,1,0:T(8,128)(2,1)}, u32[]{:S(2)}, u32[]{:S(2)}) collective-permute-start(bf16[4,3,352,128]{3,2,1,0:T(8,128)(2,1)} %get-tuple-element.180), channel_id=1, source_target_pairs={{0,4},{4,0},{8,12},{12,8},{16,20},{20,16},{24,28},{28,24},{1,5},{5... | collective-permute-start | bytes 3244040 | tf_op jit(solution)/shard_map/ppermute | solution.py:800
  99.2 43.2 %collective-permute-start.19 = (bf16[4,3,352,128]{3,2,1,0:T(8,128)(2,1)}, bf16[4,3,352,128]{3,2,1,0:T(8,128)(2,1)}, u32[]{:S(2)}, u32[]{:S(2)}) collective-permute-start(bf16[4,3,352,128]{3,2,1,0:T(8,128)(2,1)} %get-tuple-element.181), channel_id=1, source_target_pairs={{0,8},{4,12},{8,0},{12,4},{16,24},{20,28},{24,16},{28,20},{1,9},{5... | collective-permute-start | bytes 3244040 | tf_op jit(solution)/shard_map/ppermute | solution.py:800
  117.2 3.0 %collective-permute-start.20 = (bf16[512,1024]{1,0:T(8,128)(2,1)}, bf16[512,1024]{1,0:T(8,128)(2,1)}, u32[]{:S(2)}, u32[]{:S(2)}) collective-permute-start(bf16[512,1024]{1,0:T(8,128)(2,1)} %get-tuple-element.184.d0_ref.d2_ref), channel_id=1, source_target_pairs={{0,1},{1,0},{2,3},{3,2},{4,5},{5,4},{6,7},{7,6},{8,9},{9,8},{10,11... | collective-permute-start | bytes 3145736 | tf_op jit(solution)/shard_map/ppermute | solution.py:909
  117.2 25.2 %collective-permute-start.21 = (bf16[256,1024]{1,0:T(8,128)(2,1)}, bf16[256,1024]{1,0:T(8,128)(2,1)}, u32[]{:S(2)}, u32[]{:S(2)}) collective-permute-start(bf16[256,1024]{1,0:T(8,128)(2,1)} %get-tuple-element.189), channel_id=1, source_target_pairs={{0,2},{1,3},{2,0},{3,1},{4,6},{5,7},{6,4},{7,5},{8,10},{9,11},{10,... | collective-permute-start | bytes 1572872 | tf_op jit(solution)/shard_map/ppermute | solution.py:912
  146.5 28.2 %collective-permute-start.22 = (bf16[2,3,352,128]{3,2,1,0:T(8,128)(2,1)}, bf16[2,3,352,128]{3,2,1,0:T(8,128)(2,1)}, u32[]{:S(2)}, u32[]{:S(2)}) collective-permute-start(bf16[2,3,352,128]{3,2,1,0:T(8,128)(2,1)} %get-tuple-element.194), channel_id=1, source_target_pairs={{0,8},{4,12},{8,0},{12,4},{16,24},{20,28},{24,16},{28,20},{1,9},{5... | collective-permute-start | bytes 1622024 | tf_op jit(solution)/shard_map/ppermute | solution.py:800
  149.8 26.2 %collective-permute-start.23 = (bf16[2,3,352,128]{3,2,1,0:T(8,128)(2,1)}, bf16[2,3,352,128]{3,2,1,0:T(8,128)(2,1)}, u32[]{:S(2)}, u32[]{:S(2)}) collective-permute-start(bf16[2,3,352,128]{3,2,1,0:T(8,128)(2,1)} %get-tuple-element.195), channel_id=1, source_target_pairs={{0,16},{4,20},{8,24},{12,28},{16,0},{20,4},{24,8},{28,12},{1,17},{... | collective-permute-start | bytes 1622024 | tf_op jit(solution)/shard_map/ppermute | solution.py:800
  159.2 7.7 %collective-permute-start.24 = (bf16[256,1024]{1,0:T(8,128)(2,1)}, bf16[256,1024]{1,0:T(8,128)(2,1)}, u32[]{:S(2)}, u32[]{:S(2)}) collective-permute-start(bf16[256,1024]{1,0:T(8,128)(2,1)} %get-tuple-element.201), channel_id=1, source_target_pairs={{0,1},{1,0},{2,3},{3,2},{4,5},{5,4},{6,7},{7,6},{8,9},{9,8},{10,11... | collective-permute-start | bytes 1572872 | tf_op jit(solution)/shard_map/ppermute | solution.py:909
  159.2 7.7 %collective-permute-start.25 = (bf16[256,1024]{1,0:T(8,128)(2,1)}, bf16[256,1024]{1,0:T(8,128)(2,1)}, u32[]{:S(2)}, u32[]{:S(2)}) collective-permute-start(bf16[256,1024]{1,0:T(8,128)(2,1)} %get-tuple-element.202), channel_id=1, source_target_pairs={{0,1},{1,0},{2,3},{3,2},{4,5},{5,4},{6,7},{7,6},{8,9},{9,8},{10,11... | collective-permute-start | bytes 1572872 | tf_op jit(solution)/shard_map/ppermute | solution.py:909
  166.9 18.6 %collective-permute-start.27 = (bf16[4,64,1024]{2,1,0:T(8,128)(2,1)}, bf16[4,64,1024]{2,1,0:T(8,128)(2,1)}, u32[]{:S(2)}, u32[]{:S(2)}) collective-permute-start(bf16[4,64,1024]{2,1,0:T(8,128)(2,1)} %get-tuple-element.225), channel_id=1, source_target_pairs={{0,4},{4,0},{8,12},{12,8},{16,20},{20,16},{24,28},{28,24},{1,5},{5... | collective-permute-start | bytes 1572872 | tf_op jit(solution)/shard_map/ppermute | solution.py:800
  168.4 20.9 %collective-permute-start.28 = (bf16[4,64,1024]{2,1,0:T(8,128)(2,1)}, bf16[4,64,1024]{2,1,0:T(8,128)(2,1)}, u32[]{:S(2)}, u32[]{:S(2)}) collective-permute-start(bf16[4,64,1024]{2,1,0:T(8,128)(2,1)} %get-tuple-element.226), channel_id=1, source_target_pairs={{0,8},{4,12},{8,0},{12,4},{16,24},{20,28},{24,16},{28,20},{1,9},{5... | collective-permute-start | bytes 1572872 | tf_op jit(solution)/shard_map/ppermute | solution.py:800
  179.3 3.0 %copy-start.3 = (f32[32,16]{1,0:T(8,128)S(1)}, f32[32,16]{1,0:T(8,128)}, u32[]{:S(2)}) copy-start(f32[32,16]{1,0:T(8,128)} %get-tuple-element.239) | copy-start | bytes 6148
  181.6 13.5 %collective-permute-start.26 = (bf16[256,1024]{1,0:T(8,128)(2,1)}, bf16[256,1024]{1,0:T(8,128)(2,1)}, u32[]{:S(2)}, u32[]{:S(2)}) collective-permute-start(bf16[256,1024]{1,0:T(8,128)(2,1)} %add_convert_fusion.1), channel_id=1, source_target_pairs={{0,2},{1,3},{2,0},{3,1},{4,6},{5,7},{6,4},{7,5},{8,10},{9,11},{10,... | collective-permute-start | bytes 1572872 | tf_op jit(solution)/shard_map/ppermute | solution.py:912
  182.3 18.8 %collective-permute-start.31 = (bf16[1,3,352,128]{3,2,1,0:T(8,128)(2,1)}, bf16[1,3,352,128]{3,2,1,0:T(8,128)(2,1)}, u32[]{:S(2)}, u32[]{:S(2)}) collective-permute-start(bf16[1,3,352,128]{3,2,1,0:T(8,128)(2,1)} %get-tuple-element.222), channel_id=1, source_target_pairs={{0,16},{4,20},{8,24},{12,28},{16,0},{20,4},{24,8},{28,12},{1,17},{... | collective-permute-start | bytes 811016 | tf_op jit(solution)/shard_map/ppermute | solution.py:800
  184.0 17.1 %collective-permute-start.32 = (bf16[1,3,352,128]{3,2,1,0:T(8,128)(2,1)}, bf16[1,3,352,128]{3,2,1,0:T(8,128)(2,1)}, u32[]{:S(2)}, u32[]{:S(2)}) collective-permute-start(bf16[1,3,352,128]{3,2,1,0:T(8,128)(2,1)} %get-tuple-element.223), channel_id=1, source_target_pairs={{0,4},{4,0},{8,12},{12,8},{16,20},{20,16},{24,28},{28,24},{1,5},{5... | collective-permute-start | bytes 811016 | tf_op jit(solution)/shard_map/ppermute | solution.py:800
  192.4 15.5 %collective-permute-start.29 = (bf16[2,64,1024]{2,1,0:T(8,128)(2,1)}, bf16[2,64,1024]{2,1,0:T(8,128)(2,1)}, u32[]{:S(2)}, u32[]{:S(2)}) collective-permute-start(bf16[2,64,1024]{2,1,0:T(8,128)(2,1)} %get-tuple-element.230), channel_id=1, source_target_pairs={{0,8},{4,12},{8,0},{12,4},{16,24},{20,28},{24,16},{28,20},{1,9},{5... | collective-permute-start | bytes 786440 | tf_op jit(solution)/shard_map/ppermute | solution.py:800
  192.5 15.4 %collective-permute-start.30 = (bf16[2,64,1024]{2,1,0:T(8,128)(2,1)}, bf16[2,64,1024]{2,1,0:T(8,128)(2,1)}, u32[]{:S(2)}, u32[]{:S(2)}) collective-permute-start(bf16[2,64,1024]{2,1,0:T(8,128)(2,1)} %get-tuple-element.231), channel_id=1, source_target_pairs={{0,16},{4,20},{8,24},{12,28},{16,0},{20,4},{24,8},{28,12},{1,17},{... | collective-permute-start | bytes 786440 | tf_op jit(solution)/shard_map/ppermute | solution.py:800
  195.0 4.5 %copy-start.4 = (f32[1,1024]{1,0:T(1,128)S(1)}, f32[1,1024]{1,0:T(1,128)}, u32[]{:S(2)}) copy-start(f32[1,1024]{1,0:T(1,128)} %get-tuple-element.238) | copy-start | bytes 12292
  201.1 13.7 %all-to-all-start = ((f32[32,1,112]{2,1,0:T(1,128)}), f32[32,1,112]{2,1,0:T(1,128)S(1)}, u32[]{:S(2)}, u32[]{:S(2)}) async-start(f32[32,1,112]{2,1,0:T(1,128)} %bitcast.17), calls=%async_computation | async-start | bytes 32768 | tf_op jit(solution)/shard_map/all_to_all | solution.py:921
  210.7 9.6 %collective-permute-start.33 = (bf16[1,64,1024]{2,1,0:T(8,128)(2,1)}, bf16[1,64,1024]{2,1,0:T(8,128)(2,1)S(1)}, u32[]{:S(2)}, u32[]{:S(2)}) collective-permute-start(bf16[1,64,1024]{2,1,0:T(8,128)(2,1)} %get-tuple-element.250), channel_id=1, source_target_pairs={{0,16},{4,20},{8,24},{12,28},{16,0},{20,4},{24,8},{28,12},{1,17},{... | collective-permute-start | bytes 393224 | tf_op jit(solution)/shard_map/ppermute | solution.py:800
  213.4 6.9 %collective-permute-start.34 = (bf16[1,64,1024]{2,1,0:T(8,128)(2,1)}, bf16[1,64,1024]{2,1,0:T(8,128)(2,1)}, u32[]{:S(2)}, u32[]{:S(2)}) collective-permute-start(bf16[1,64,1024]{2,1,0:T(8,128)(2,1)} %get-tuple-element.252), channel_id=1, source_target_pairs={{0,4},{4,0},{8,12},{12,8},{16,20},{20,16},{24,28},{28,24},{1,5},{5... | collective-permute-start | bytes 393224 | tf_op jit(solution)/shard_map/ppermute | solution.py:800
  220.3 0.7 copy-start.2

commit v2 on v1

--- a/solution.py
+++ b/solution.py
@@ -225,10 +225,6 @@
     return pltpu.CompilerParams(dimension_semantics=("arbitrary",), vmem_limit_bytes=255 << 18)
 
 
-def row_block(step, ids):
-    return step // 2 * 2 + (step + ids[1]) % 2
-
-
 def attend(chunk, q, k, v, tables, lengths, box_cols, box_rows, before):
     n_keys, width = k.shape
     qb = n_keys // 4
@@ -275,10 +271,9 @@
     return jnp.sum(wide, axis=0, keepdims=True)
 
 
-def bwd_kernel(n_heads, qb, ids, lens, box_cols, box_rows, q_ref, k_ref, v_ref, d0_ref, d1_ref, d2_ref, d3_ref, wo_ref, ctxt_ref, rows_ref, p_ref,
-               out_ref, dtab_ref, da_ref, v_scr, kt_scr, ds_scr, dk_scr, dv_scr, near_scr, part_scr, far_acc, self_acc):
-    step = pl.program_id(0)
-    block = row_block(step, ids)
+def bwd_kernel(n_heads, qb, ids, lens, box_cols, box_rows, q_ref, k_ref, v_ref, own_ref, core_ref, wo_ref, ctxt_ref, rows_ref, p_ref,
+               out_ref, dtab_ref, da_ref, v_scr, kt_scr, ds_scr, dk_scr, dv_scr, near_scr, part_scr, far_acc, self_acc, ctx_scr):
+    step = block = pl.program_id(0)
     n_keys = k_ref.shape[0]
     blocks = qb // COORD
 
@@ -307,13 +302,11 @@
 
     rows_q = pl.ds(pl.multiple_of(block * qb, qb), qb)
     lane_half = lax.broadcasted_iota(i32, (qb, 128), 1) >= HEAD
-    for at_step, piece in enumerate((d0_ref, d1_ref, d2_ref, d3_ref)):
-
-        @pl.when(step == at_step)
-        def _():
-            da_ref[...] = piece[...]
-
+    lower = ids[1] == 0
+    da_ref[0 : qb // 2, :] = jnp.where(lower, own_ref[...], core_ref[...])
+    da_ref[qb // 2 :, :] = jnp.where(lower, core_ref[...], own_ref[...])
     d_ctx = dot_nt(wo_ref[...], da_ref[...])
+    ctx_scr[...] = d_ctx
     prod = d_ctx * ctxt_ref[...]
     scaled = []
     operands = []
@@ -364,7 +357,7 @@
 
     @pl.when(some)
     def _():
-        d_out = dot_nt(wo_ref[...], da_ref[...])
+        d_out = ctx_scr[...]
         product = d_out * ctxt_ref[...]
         for pair in range(n_heads // 2):
             cols = slice(pair * 128, pair * 128 + 128)
@@ -414,12 +407,11 @@
 def attend_back(ids, q, k, v, d_own, d_core, w_out, ctxt, rows, probs, lengths, box_cols, box_rows):
     n_keys, width = k.shape
     n_heads = width // HEAD
-    qb = n_keys // 4
+    qb = n_keys // 2
     model = w_out.shape[1]
     n_pairs = n_heads // 2
-    at_rows = lambda i, ids, lens: (row_block(i, ids), 0)
-    at_columns = lambda i, ids, lens: (0, row_block(i, ids))
-    pieces_in = [(d, at) for at in range(2) for d in (d_own, d_core)]
+    at_rows = lambda i, ids, lens: (i, 0)
+    at_columns = lambda i, ids, lens: (0, i)
     return pl.pallas_call(
         functools.partial(bwd_kernel, n_heads, qb),
         out_shape=[
@@ -429,15 +421,15 @@
         ],
         grid_spec=pltpu.PrefetchScalarGridSpec(
             num_scalar_prefetch=2,
-            grid=(4,),
+            grid=(2,),
             in_specs=[
                 whole(box_cols.shape), whole(box_rows.shape),
                 pl.BlockSpec((qb, width), at_rows), whole(k.shape), whole(v.shape),
-                *[pl.BlockSpec((qb, model), lambda i, ids, lens, at=at: (at, 0)) for _, at in pieces_in],
+                *[pl.BlockSpec((qb // 2, model), at_rows)] * 2,
                 whole(w_out.shape),
                 pl.BlockSpec((width, qb), at_columns),
                 pl.BlockSpec((8, qb), at_columns),
-                pl.BlockSpec((n_heads, n_keys, qb), lambda i, ids, lens: (0, 0, row_block(i, ids))),
+                pl.BlockSpec((n_heads, n_keys, qb), lambda i, ids, lens: (0, 0, i)),
             ],
             out_specs=[whole((n_keys, 384 * n_pairs)), whole((NB, 16)), pl.BlockSpec((qb, model), at_rows)],
             scratch_shapes=[
@@ -450,12 +442,13 @@
                 pltpu.VMEM((n_heads, 256, n_keys), bf16),
                 pltpu.VMEM((n_heads, 2, 8, qb), f32),
                 pltpu.VMEM((8, qb), f32),
+                pltpu.VMEM((width, qb), f32),
             ],
         ),
         compiler_params=params(),
         cost_estimate=estimate(),
         name="attend_back",
-    )(ids, lengths, box_cols, box_rows, q, k, v, *(d for d, _ in pieces_in), w_out, ctxt, rows, probs)
+    )(ids, lengths, box_cols, box_rows, q, k, v, d_own, d_core, w_out, ctxt, rows, probs)
 
 
 norm_eps = 1e-06
@@ -477,12 +470,10 @@
 
 def qkv_kernel(ids, xa_ref, xb_ref, g_ref, wq_ref, wk_ref, wv_ref, *refs):
     xo_ref, n_ref, q_ref, k_ref, v_ref = refs[-5:]
-    for at_step, piece in enumerate((xa_ref, xb_ref)):
-
-        @pl.when(pl.program_id(0) == at_step)
-        def _():
-            xo_ref[...] = piece[...]
-
+    rows = xa_ref.shape[0]
+    lower = ids[1] == 0
+    xo_ref[0:rows, :] = jnp.where(lower, xa_ref[...], xb_ref[...])
+    xo_ref[rows:, :] = jnp.where(lower, xb_ref[...], xa_ref[...])
     x = xo_ref[...].astype(f32)
     normed = (x * scale_of(x) * g_ref[...]).astype(bf16)
     n_ref[...] = normed
@@ -494,20 +485,15 @@
 def project(ids, far, pair, gain, weights, before, n_blocks):
     rows, model = pair[0].shape
     width = weights[0].shape[1]
-
-    def row(i, ids):
-        chip = 1 - ids[2] if far else ids[2]
-        return (2 * chip + (i + ids[1]) % 2, 0)
-
     shapes = [jax.ShapeDtypeStruct((n_blocks * rows, n), bf16) for n in (model, model, width, width, width)]
     return pl.pallas_call(
         qkv_kernel,
         out_shape=shapes,
         grid_spec=pltpu.PrefetchScalarGridSpec(
             num_scalar_prefetch=1,
-            grid=(2,),
+            grid=(1,),
             in_specs=[whole(pair[0].shape)] * 2 + [whole(gain.shape)] + [whole(w.shape) for w in weights] + [anywhere()] * len(before),
-            out_specs=[pl.BlockSpec((rows, s.shape[1]), row) for s in shapes],
+            out_specs=[pl.BlockSpec((2 * rows, s.shape[1]), lambda i, ids: (1 - ids[2] if far else ids[2], 0)) for s in shapes],
         ),
         input_output_aliases={7 + i: i for i in range(len(before))},
         compiler_params=params(),
@@ -609,7 +595,7 @@
     dm_ref[...] = d_mixed
     da_ref[...] = d_mixed.astype(bf16)
     step = pl.program_id(0)
-    gain_sum = jnp.where(ids[2] == step // 2, gain_sum, 0.0)
+    gain_sum = jnp.where(ids[2] == step, gain_sum, 0.0)
 
     @pl.when(step == 0)
     def _():
@@ -622,12 +608,12 @@
 
 def mid(ids, own, far, mixed, cot_all, gain):
     total, model = own.shape
-    rows = total // 4
+    rows = total // 2
     spec = pl.BlockSpec((rows, model), lambda i, ids: (i, 0))
-    cot_spec = pl.BlockSpec((rows, model), lambda i, ids: (i // 2 * 4 + 2 * ids[1] + i % 2, 0))
+    cot_spec = pl.BlockSpec((rows, model), lambda i, ids: (2 * i + ids[1], 0))
     ins = [(own, spec), (far, spec), (mixed, spec), (cot_all, cot_spec), (gain, whole(gain.shape))]
     outs = [((total, model), f32, spec), ((total, model), bf16, spec), ((1, model), f32, whole((1, model)))]
-    return call(mid_kernel, ids, ins, outs, (4,), "mid")
+    return call(mid_kernel, ids, ins, outs, (2,), "mid")
 
 
 def back_kernel(ids, a_ref, b_ref, wa_ref, wb_ref, *outs):
@@ -1013,13 +999,13 @@
     tabs = jnp.where(lax.broadcasted_iota(i32, (1, n_mp, 1), 1) == me, tabs, 0.0)
     small = jnp.concatenate([gains.reshape(n_dp, n_mp, 2 * n_gain), tabs], axis=2).reshape(n_dp * n_mp, -1)
     if pairwise:
-        unit_came[0], unit_came[1], small = together(*unit_came, small)
         small = exchange_small(small)
-        ffn_sums = unit_last(ids, unit_kept, unit_came)
-        came[0], came[1], *ffn_sums = together(*came, *ffn_sums)
         kept, sends = onward(ids, kept, came)
         came = swaps(sends, 2)
         small = after(small, *sends).sum(axis=0)
+        unit_came[0] = after(unit_came[0], small)
+        ffn_sums = unit_last(ids, unit_kept, unit_came)
+        came[0], came[1], *ffn_sums = together(*came, *ffn_sums)
         attn_sums = head_last(ids, kept, came)
     else:
         result = result_of(ids, mixed, r_own, r_far)

time: 225 us -> 224 us (level)
  transfers between devices with their start and end apart: 36 -> 36, of which waited for: 12 -> 14; matrix products, arithmetic and copies ran while one was open for 5% -> 5% of each run, Pallas kernels for 51% -> 50%
where the time goes in v2:
time: 224 us; the launch traced here: 221 us
  Pallas kernels  138 us (62%)
  starting transfers between devices  34.1 us (15%)
  waiting for transfers between devices  32.9 us (15%)
  other arithmetic  9.06 us (4%)
  local copies, waits for them, and re-layouts  5.73 us (3%)
    pallas_call x12, Pallas kernels, call(): pl.pallas_call(kernel, out_shape=[jax.ShapeDtypeStruct(shape, kind) for s...  61.1 us
    pallas_call x2, Pallas kernels, attend(): pl.pallas_call(functools.partial(fwd_kernel, n_heads, qb, 2 * chunk), out...  24.1 us
    pallas_call x1, Pallas kernels, attend_back(): pl.pallas_call(functools.partial(bwd_kernel, n_heads, qb), out_shape=[jax...  20.9 us
    ppermute x12, starting transfers between devices, swap(): return lax.ppermute(sent, 'dp', [(i, i ^ 1 << bit) for i in range(n_dp)])  19.2 us
    ppermute x12, waiting for transfers between devices, swap(): return lax.ppermute(sent, 'dp', [(i, i ^ 1 << bit) for i in range(n_dp)])  12.1 us
    ppermute x8, waiting for transfers between devices, by_chip(): return lax.ppermute(a, 'mp', [(i, i ^ 2) for i in range(n_mp)])  12 us
    pallas_call x1, Pallas kernels, unit_parts(): pl.pallas_call(unit_parts_kernel, out_shape=[jax.ShapeDtypeStruct(shape,...  11.3 us
    pallas_call x2, Pallas kernels, project(): pl.pallas_call(qkv_kernel, out_shape=shapes, grid_spec=pltpu.PrefetchScal...  8.78 us
  transfers between devices with their start and end apart: 36, of which 14 were waited for; matrix products, arithmetic and copies ran while one was open for 5% of the time, Pallas kernels for 50%

profile of v2, /device:TPU:0, one launch (start us, length us, event | category | flops | bytes accessed | tf_op | source)
XLA Modules:
  0.0 220.5 jit_solution(557086288648455241)
XLA Ops:
  0.7 0.5 collective-permute-start.1
  1.2 2.6 %collective-permute-start = (bf16[256,1024]{1,0:T(8,128)(2,1)}, bf16[256,1024]{1,0:T(8,128)(2,1)}, u32[]{:S(2)}, u32[]{:S(2)}) collective-permute-start(bf16[256,1024]{1,0:T(8,128)(2,1)} %x_ref.1), channel_id=1, source_target_pairs={{0,2},{1,3},{2,0},{3,1},{4,6},{5,7},{6,4},{7,5},{8,10},{9,11},{10,... | collective-permute-start | bytes 1572872 | tf_op jit(solution)/shard_map/ppermute | solution.py:898
  3.8 1.1 fusion
  4.8 1.1 fusion.1
  6.0 1.1 copy.42
  7.1 0.6 pad_add_fusion.ids
  7.8 1.3 pad_maximum_fusion
  9.1 0.7 maximum_maximum_fusion.tab_ref
  9.8 4.4 %project.2 = (bf16[1024,1024]{1,0:T(8,128)(2,1)}, bf16[1024,1024]{1,0:T(8,128)(2,1)}, bf16[1024,256]{1,0:T(8,128)(2,1)}, bf16[1024,256]{1,0:T(8,128)(2,1)}, bf16[1024,256]{1,0:T(8,128)(2,1)}) custom-call(s32[4]{0:T(128)} %pad_add_fusion.ids, bf16[256,1024]{1,0:T(8,128)(2,1)} %x_ref.1, bf16[256,1024]{1,0:T(8,128)(2,1)} %collective-permute-done.1.xb_ref, ...), custom_call_target="tpu_custom_call" | custom-call | flops 1000 | bytes 1000 | tf_op jit(solution)/shard_map/project/pallas_call | solution.py:489
  14.2 2.4 %collective-permute-done.xa_ref = bf16[256,1024]{1,0:T(8,128)(2,1)} collective-permute-done((bf16[256,1024]{1,0:T(8,128)(2,1)}, bf16[256,1024]{1,0:T(8,128)(2,1)}, u32[]{:S(2)}, u32[]{:S(2)}) %collective-permute-start) | collective-permute-done | bytes 524320 | tf_op jit(solution)/shard_map/ppermute | solution.py:898
  16.6 1.8 collective-permute-start.5
  18.9 4.4 %project.3 = (bf16[1024,1024]{1,0:T(8,128)(2,1)}, bf16[1024,1024]{1,0:T(8,128)(2,1)}, bf16[1024,256]{1,0:T(8,128)(2,1)}, bf16[1024,256]{1,0:T(8,128)(2,1)}, bf16[1024,256]{1,0:T(8,128)(2,1)}) custom-call(s32[4]{0:T(128)} %pad_add_fusion.ids, ...), custom_call_target="tpu_custom_call", output_to_operand_aliasing={{0}: (7, {}), {1}: (8, {}), {2}: (9, {}), {3}: (10, {}), {4... | custom-call | flops 1000 | bytes 1000 | tf_op jit(solution)/shard_map/project/pallas_call | solution.py:489
  23.3 12.3 %attend.2 = (bf16[1024,256]{1,0:T(8,128)(2,1)}, f32[256,1024]{1,0:T(8,128)}, f32[8,1024]{1,0:T(8,128)}, bf16[4,1024,1024]{2,1,0:T(8,128)(2,1)}, bf16[512,256]{1,0:T(8,128)(2,1)}) custom-call(s32[1,2]{1,0:T(1,128)} %lens.5, f32[16,32]{1,0:T(8,128)} %maximum_maximum_fusion.tab_ref, s32[1024,2]{1,0:T(8,128)} %bitcast.26, s32[2,1024]{1,0:T(2,128)} %box_rows.5, ...), custom_call_target="tpu_custom_call" | custom-call | flops 1000 | bytes 1000 | tf_op jit(solution)/shard_map/attend/pallas_call | solution.py:232
  35.5 1.8 collective-permute-start.4
  37.3 0.5 collective-permute-start.9
  37.8 11.8 %attend.3 = (bf16[1024,256]{1,0:T(8,128)(2,1)}, f32[256,1024]{1,0:T(8,128)}, f32[8,1024]{1,0:T(8,128)}, bf16[4,1024,1024]{2,1,0:T(8,128)(2,1)}, bf16[512,256]{1,0:T(8,128)(2,1)}) custom-call(s32[1,2]{1,0:T(1,128)} %lens.5, f32[16,32]{1,0:T(8,128)} %maximum_maximum_fusion.tab_ref, ...), custom_call_target="tpu_custom_call", output_to_operand_aliasing={{0}: (7, {}), {1}: (8, {}), {2}: (9, {}), {3}: (10, {})} | custom-call | flops 1000 | bytes 1000 | tf_op jit(solution)/shard_map/attend/pallas_call | solution.py:232
  50.8 1.2 collective-permute-done.10.refs_3_
  52.1 4.2 %assemble.1.cot_ref.refs_5_ = bf16[1024,1024]{1,0:T(8,128)(2,1)} custom-call(s32[4]{0:T(128)} %pad_add_fusion.ids, bf16[256,1024]{1,0:T(8,128)(2,1)} %refs_0_.1, bf16[256,1024]{1,0:T(8,128)(2,1)} %collective-permute-done.9.refs_1_, bf16[256,1024]{1,0:T(8,128)(2,1)} %collective-permute-done.6.refs_2_, bf16[256,1024]{1,0:T(8,128)(2,1)} %collective-permute-done.10.refs_3_), custom_call_target="tpu_custom_call" | custom-call | flops 1000 | bytes 1000 | tf_op jit(solution)/shard_map/assemble/pallas_call | solution.py:521
  56.3 2.5 %collective-permute-done.11.b2 = bf16[512,256]{1,0:T(8,128)(2,1)} collective-permute-done((bf16[512,256]{1,0:T(8,128)(2,1)}, bf16[512,256]{1,0:T(8,128)(2,1)}, u32[]{:S(2)}, u32[]{:S(2)}) %collective-permute-start.11) | collective-permute-done | bytes 262176 | tf_op jit(solution)/shard_map/ppermute | solution.py:898
  58.8 1.8 collective-permute-done.12.b3
  60.7 19.7 %ffn.1 = (f32[512,1024]{1,0:T(8,128)}, bf16[1024,1024]{1,0:T(8,128)(2,1)}, bf16[704,1024]{1,0:T(8,128)(2,1)}, bf16[704,1024]{1,0:T(8,128)(2,1)}, bf16[704,1024]{...) custom-call(s32[4]{0:T(128)} %pad_add_fusion.ids, ...), custom_call_target="tpu_custom_call" | custom-call | flops 1000 | bytes 1000 | tf_op jit(solution)/shard_map/ffn/pallas_call | solution.py:790
  80.5 2.7 %collective-permute-done.15 = bf16[512,1024]{1,0:T(8,128)(2,1)S(1)} collective-permute-done((bf16[512,1024]{1,0:T(8,128)(2,1)}, bf16[512,1024]{1,0:T(8,128)(2,1)S(1)}, u32[]{:S(2)}, u32[]{:S(2)}) %collective-permute-start.15) | collective-permute-done | bytes 1048608 | tf_op jit(solution)/shard_map/ppermute | solution.py:895
  83.3 2.6 %add_convert_fusion.a_ref = bf16[512,1024]{1,0:T(8,128)(2,1)} fusion(bf16[512,1024]{1,0:T(8,128)(2,1)S(1)} %collective-permute-done.15, bf16[512,1024]{1,0:T(8,128)(2,1)} %get-tuple-element.168), kind=kLoop, calls=%fused_computation | loop fusion | flops 2097152 | bytes 3145728 | tf_op jit(solution)/shard_map/convert_element_type | solution.py:941
  86.3 11.3 %unit_parts.1 = (bf16[4,3,352,128]{3,2,1,0:T(8,128)(2,1)}, bf16[4,3,352,128]{3,2,1,0:T(8,128)(2,1)}, bf16[4,3,352,128]{3,2,1,0:T(8,128)(2,1)}, bf16[4,3,352,128]{3,2,1,0:T(8,128)(2,1)}) custom-call(s32[4]{0:T(128)} %pad_add_fusion.ids, bf16[704,1024]{1,0:T(8,128)(2,1)} %get-tuple-element.164.refs_0_, bf16[704,1024]{1,0:T(8,128)(2,1)} %get-tuple-element.165.refs_1_, ...), custom_call_target="tpu_custom_call" | custom-call | flops 1000 | bytes 1000 | tf_op jit(solution)/shard_map/unit_parts/pallas_call | solution.py:702
  97.6 2.3 %collective-permute-start.18 = (bf16[4,3,352,128]{3,2,1,0:T(8,128)(2,1)}, bf16[4,3,352,128]{3,2,1,0:T(8,128)(2,1)}, u32[]{:S(2)}, u32[]{:S(2)}) collective-permute-start(bf16[4,3,352,128]{3,2,1,0:T(8,128)(2,1)} %get-tuple-element.178), channel_id=1, source_target_pairs={{0,4},{4,0},{8,12},{12,8},{16,20},{20,16},{24,28},{28,24},{1,5},{5... | collective-permute-start | bytes 3244040 | tf_op jit(solution)/shard_map/ppermute | solution.py:786
  99.9 1.6 collective-permute-start.19
  101.5 3.2 %out_sums.1 = (bf16[256,1024]{1,0:T(8,128)(2,1)}, f32[256,1024]{1,0:T(8,128)}) custom-call(s32[4]{0:T(128)} %pad_add_fusion.ids, bf16[512,1024]{1,0:T(8,128)(2,1)} %get-tuple-element.173.ka_ref.kb_ref, bf16[512,1024]{1,0:T(8,128)(2,1)} %collective-permute-done.17.ca_ref.cb_ref, bf16[512,1024]{1,0:T(8,128)(2,1)} %get-tuple-element.173.ka_ref.kb_ref, ...), custom_call_target="tpu_custom_call" | custom-call | flops 1000 | bytes 1000 | tf_op jit(solution)/shard_map/out_sums/pallas_call | solution.py:790
  104.7 7.1 %collective-permute-done.16.b_ref = bf16[512,1024]{1,0:T(8,128)(2,1)} collective-permute-done((bf16[512,1024]{1,0:T(8,128)(2,1)}, bf16[512,1024]{1,0:T(8,128)(2,1)}, u32[]{:S(2)}, u32[]{:S(2)}) %collective-permute-start.16) | collective-permute-done | bytes 1048608 | tf_op jit(solution)/shard_map/ppermute | solution.py:898
  111.8 5.0 %mid.1 = (f32[512,1024]{1,0:T(8,128)}, bf16[512,1024]{1,0:T(8,128)(2,1)}, f32[1,1024]{1,0:T(1,128)}) custom-call(s32[4]{0:T(128)} %pad_add_fusion.ids, bf16[512,1024]{1,0:T(8,128)(2,1)} %add_convert_fusion.a_ref, bf16[512,1024]{1,0:T(8,128)(2,1)} %collective-permute-done.16.b_ref, f32[512,1024]{1,0:T(8,128)} %get-tuple-element.181.mixed_ref, ...), custom_call_target="tpu_custom_call" | custom-call | flops 1000 | bytes 1000 | tf_op jit(solution)/shard_map/mid/pallas_call | solution.py:790
  116.8 0.3 collective-permute-start.21
  117.1 2.6 %collective-permute-done.20.core_ref = bf16[512,1024]{1,0:T(8,128)(2,1)} collective-permute-done((bf16[512,1024]{1,0:T(8,128)(2,1)}, bf16[512,1024]{1,0:T(8,128)(2,1)}, u32[]{:S(2)}, u32[]{:S(2)}) %collective-permute-start.20) | collective-permute-done | bytes 1048608 | tf_op jit(solution)/shard_map/ppermute | solution.py:895
  119.8 20.9 %attend_back.1 = (bf16[1024,768]{1,0:T(8,128)(2,1)}, f32[32,16]{1,0:T(8,128)}, bf16[1024,1024]{1,0:T(8,128)(2,1)}) custom-call(s32[4]{0:T(128)} %pad_add_fusion.ids, s32[1,2]{1,0:T(1,128)} %lens.5, s32[1024,2]{1,0:T(8,128)} %bitcast.28, s32[2,1024]{1,0:T(2,128)} %box_rows.5, bf16[1024,256]{1,0:T(8,128)(2,1)} %get-tuple-element.148.q_ref, ...), custom_call_target="tpu_custom_call" | custom-call | flops 1000 | bytes 1000 | tf_op jit(solution)/shard_map/attend_back/pallas_call | solution.py:415
  140.7 4.0 %onward.4 = (bf16[2,3,352,128]{3,2,1,0:T(8,128)(2,1)}, bf16[2,3,352,128]{3,2,1,0:T(8,128)(2,1)}, bf16[2,3,352,128]{3,2,1,0:T(8,128)(2,1)}, bf16[2,3,352,128]{3,2,1,0:T(8,128)(2,1)}) custom-call(s32[4]{0:T(128)} %pad_add_fusion.ids, bf16[4,3,352,128]{3,2,1,0:T(8,128)(2,1)} %get-tuple-element.177.refs_0_.refs_1_, ...), custom_call_target="tpu_custom_call" | custom-call | flops 1000 | bytes 1000 | tf_op jit(solution)/shard_map/onward/pallas_call | solution.py:790
  144.7 3.1 %collective-permute-start.22 = (bf16[2,3,352,128]{3,2,1,0:T(8,128)(2,1)}, bf16[2,3,352,128]{3,2,1,0:T(8,128)(2,1)}, u32[]{:S(2)}, u32[]{:S(2)}) collective-permute-start(bf16[2,3,352,128]{3,2,1,0:T(8,128)(2,1)} %get-tuple-element.192), channel_id=1, source_target_pairs={{0,8},{4,12},{8,0},{12,4},{16,24},{20,28},{24,16},{28,20},{1,9},{5... | collective-permute-start | bytes 1622024 | tf_op jit(solution)/shard_map/ppermute | solution.py:786
  147.8 3.4 %collective-permute-start.23 = (bf16[2,3,352,128]{3,2,1,0:T(8,128)(2,1)}, bf16[2,3,352,128]{3,2,1,0:T(8,128)(2,1)}, u32[]{:S(2)}, u32[]{:S(2)}) collective-permute-start(bf16[2,3,352,128]{3,2,1,0:T(8,128)(2,1)} %get-tuple-element.193), channel_id=1, source_target_pairs={{0,16},{4,20},{8,24},{12,28},{16,0},{20,4},{24,8},{28,12},{1,17},{... | collective-permute-start | bytes 1622024 | tf_op jit(solution)/shard_map/ppermute | solution.py:786
  151.2 7.0 %project_back.1 = (bf16[256,1024]{1,0:T(8,128)(2,1)}, f32[256,1024]{1,0:T(8,128)}, bf16[256,1024]{1,0:T(8,128)(2,1)}, f32[256,1024]{1,0:T(8,128)}) custom-call(s32[4]{0:T(128)} %pad_add_fusion.ids, bf16[1024,768]{1,0:T(8,128)(2,1)} %get-tuple-element.204.a_ref.b_ref.g_ref, bf16[1024,768]{1,0:T(8,128)(2,1)} %get-tuple-element.204.a_ref.b_ref.g_ref, ...), custom_call_target="tpu_custom_call" | custom-call | flops 1000 | bytes 1000 | tf_op jit(solution)/shard_map/project_back/pallas_call | solution.py:790
  158.3 0.5 collective-permute-start.25
  158.8 7.2 %head_sums.1 = (bf16[4,64,1024]{2,1,0:T(8,128)(2,1)}, bf16[4,64,1024]{2,1,0:T(8,128)(2,1)}, bf16[4,64,1024]{2,1,0:T(8,128)(2,1)}, bf16[4,64,1024]{2,1,0:T(8,128)(2,1)}) custom-call(s32[4]{0:T(128)} %pad_add_fusion.ids, bf16[1024,1024]{1,0:T(8,128)(2,1)} %get-tuple-element.201.normed_ref, bf16[1024,1024]{1,0:T(8,128)(2,1)} %get-tuple-element.202.da_ref, ...), custom_call_target="tpu_custom_call" | custom-call | flops 1000 | bytes 1000 | tf_op jit(solution)/shard_map/head_sums/pallas_call | solution.py:769
  166.1 1.6 collective-permute-start.27
  167.7 3.2 %result_of.1 = f32[256,1024]{1,0:T(8,128)} custom-call(s32[4]{0:T(128)} %pad_add_fusion.ids, f32[512,1024]{1,0:T(8,128)} %get-tuple-element.181.mixed_ref, f32[256,1024]{1,0:T(8,128)} %get-tuple-element.194.own_ref, bf16[256,1024]{1,0:T(8,128)(2,1)} %collective-permute-done.21.far_ref), custom_call_target="tpu_custom_call" | custom-call | flops 1000 | bytes 1000 | tf_op jit(solution)/shard_map/result_of/pallas_call | solution.py:790
  170.9 1.6 collective-permute-done.22.refs_2_.refs_3_
  172.5 2.7 %collective-permute-done.23.refs_6_.refs_7_ = bf16[2,3,352,128]{3,2,1,0:T(8,128)(2,1)} collective-permute-done((bf16[2,3,352,128]{3,2,1,0:T(8,128)(2,1)}, bf16[2,3,352,128]{3,2,1,0:T(8,128)(2,1)}, u32[]{:S(2)}, u32[]{:S(2)}) %collective-permute-start.23) | collective-permute-done | bytes 540704 | tf_op jit(solution)/shard_map/ppermute | solution.py:786
  175.3 3.2 %onward.5 = (bf16[1,3,352,128]{3,2,1,0:T(8,128)(2,1)}, bf16[1,3,352,128]{3,2,1,0:T(8,128)(2,1)}, bf16[1,3,352,128]{3,2,1,0:T(8,128)(2,1)}, bf16[1,3,352,128]{3,2,1,0:T(8,128)(2,1)}) custom-call(s32[4]{0:T(128)} %pad_add_fusion.ids, bf16[2,3,352,128]{3,2,1,0:T(8,128)(2,1)} %get-tuple-element.216.refs_0_.refs_1_, ...), custom_call_target="tpu_custom_call" | custom-call | flops 1000 | bytes 1000 | tf_op jit(solution)/shard_map/onward/pallas_call | solution.py:790
  178.5 2.3 %add_convert_fusion.1 = bf16[256,1024]{1,0:T(8,128)(2,1)} fusion(f32[256,1024]{1,0:T(8,128)} %get-tuple-element.203, bf16[256,1024]{1,0:T(8,128)(2,1)} %collective-permute-done.24), kind=kLoop, calls=%fused_computation.1 | loop fusion | flops 786432 | bytes 2097152 | tf_op jit(solution)/shard_map/convert_element_type | solution.py:987
  180.8 0.5 collective-permute-start.26
  181.5 0.5 collective-permute-start.33
  182.0 4.5 %collective-permute-done.28.refs_6_.refs_7_ = bf16[4,64,1024]{2,1,0:T(8,128)(2,1)} collective-permute-done((bf16[4,64,1024]{2,1,0:T(8,128)(2,1)}, bf16[4,64,1024]{2,1,0:T(8,128)(2,1)}, u32[]{:S(2)}, u32[]{:S(2)}) %collective-permute-start.28) | collective-permute-done | bytes 524320 | tf_op jit(solution)/shard_map/ppermute | solution.py:786
  186.5 3.1 %onward.6 = (bf16[2,64,1024]{2,1,0:T(8,128)(2,1)}, bf16[2,64,1024]{2,1,0:T(8,128)(2,1)}, bf16[2,64,1024]{2,1,0:T(8,128)(2,1)}, bf16[2,64,1024]{2,1,0:T(8,128)(2,1)}) custom-call(s32[4]{0:T(128)} %pad_add_fusion.ids, bf16[4,64,1024]{2,1,0:T(8,128)(2,1)} %get-tuple-element.210.refs_0_.refs_1_, bf16[4,64,1024]{2,1,0:T(8,128)(2,1)} %get-tuple-element.210.refs_0_.refs_1_, ...), custom_call_target="tpu_custom_call" | custom-call | flops 1000 | bytes 1000 | tf_op jit(solution)/shard_map/onward/pallas_call | solution.py:790
  189.7 2.7 %collective-permute-start.30 = (bf16[2,64,1024]{2,1,0:T(8,128)(2,1)}, bf16[2,64,1024]{2,1,0:T(8,128)(2,1)}, u32[]{:S(2)}, u32[]{:S(2)}) collective-permute-start(bf16[2,64,1024]{2,1,0:T(8,128)(2,1)} %get-tuple-element.229), channel_id=1, source_target_pairs={{0,16},{4,20},{8,24},{12,28},{16,0},{20,4},{24,8},{28,12},{1,17},{... | collective-permute-start | bytes 786440 | tf_op jit(solution)/shard_map/ppermute | solution.py:786
  192.5 1.5 collective-permute-start.34
  194.0 4.5 %last.1 = (f32[256,1024]{1,0:T(8,128)}, f32[1,1024]{1,0:T(1,128)}) custom-call(s32[4]{0:T(128)} %pad_add_fusion.ids, f32[256,1024]{1,0:T(8,128)} %get-tuple-element.213.keep_ref, bf16[256,1024]{1,0:T(8,128)(2,1)} %collective-permute-done.25.core_ref, bf16[256,1024]{1,0:T(8,128)(2,1)} %collective-permute-done.26.y_ref, bf16[256,1024]{1,0:T(8,128)(2,1)} %x_ref.1, ...), custom_call_target="tpu_custom_call" | custom-call | flops 1000 | bytes 1000 | tf_op jit(solution)/shard_map/last/pallas_call | solution.py:790
  198.5 0.7 pad_maximum_fusion.3
  199.4 0.7 pad_maximum_fusion.2
  200.1 4.2 %all-to-all-start = ((f32[32,1,112]{2,1,0:T(1,128)}), f32[32,1,112]{2,1,0:T(1,128)S(1)}, u32[]{:S(2)}, u32[]{:S(2)}) async-start(f32[32,1,112]{2,1,0:T(1,128)} %bitcast.15), calls=%async_computation | async-start | bytes 32768 | tf_op jit(solution)/shard_map/all_to_all | solution.py:907
  204.3 1.8 collective-permute-done.30.refs_6_.refs_7_
  206.1 2.8 %onward.7 = (bf16[1,64,1024]{2,1,0:T(8,128)(2,1)}, bf16[1,64,1024]{2,1,0:T(8,128)(2,1)}, bf16[1,64,1024]{2,1,0:T(8,128)(2,1)}, bf16[1,64,1024]{2,1,0:T(8,128)(2,1)}) custom-call(s32[4]{0:T(128)} %pad_add_fusion.ids, bf16[2,64,1024]{2,1,0:T(8,128)(2,1)} %get-tuple-element.233.refs_0_.refs_1_, bf16[2,64,1024]{2,1,0:T(8,128)(2,1)} %get-tuple-element.233.refs_0_.refs_1_, ...), custom_call_target="tpu_custom_call" | custom-call | flops 1000 | bytes 1000 | tf_op jit(solution)/shard_map/onward/pallas_call | solution.py:790
  208.8 0.9 collective-permute-start.31
  209.7 1.5 collective-permute-start.32
  211.5 0.6 fusion.3
  212.1 2.9 %unit_last.1 = (f32[704,128]{1,0:T(8,128)}, f32[704,128]{1,0:T(8,128)}, f32[704,128]{1,0:T(8,128)}) custom-call(s32[4]{0:T(128)} %pad_add_fusion.ids, bf16[1,3,352,128]{3,2,1,0:T(8,128)(2,1)} %get-tuple-element.238.ka, bf16[1,3,352,128]{3,2,1,0:T(8,128)(2,1)} %collective-permute-done.33.ca, bf16[1,3,352,128]{3,2,1,0:T(8,128)(2,1)} %get-tuple-element.244.kb, ...), custom_call_target="tpu_custom_call" | custom-call | flops 1000 | bytes 1000 | tf_op jit(solution)/shard_map/unit_last/pallas_call | solution.py:790
  215.0 0.6 fusion.4
  215.6 1.4 collective-permute-done.31.ca
  217.0 0.7 copy-done.2
  217.7 2.6 %head_last.1 = (f32[128,256]{1,0:T(8,128)}, f32[128,256]{1,0:T(8,128)}, f32[128,256]{1,0:T(8,128)}, f32[256,128]{1,0:T(8,128)}) custom-call(s32[4]{0:T(128)} %pad_add_fusion.ids, bf16[1,64,1024]{2,1,0:T(8,128)(2,1)} %get-tuple-element.235.ka, bf16[1,64,1024]{2,1,0:T(8,128)(2,1)} %copy-done.2, bf16[1,64,1024]{2,1,0:T(8,128)(2,1)} %get-tuple-element.249.kb, ...), custom_call_target="tpu_custom_call" | custom-call | flops 1000 | bytes 1000 | tf_op jit(solution)/shard_map/head_last/pallas_call | solution.py:790
  (71 shorter events, 3.6 us)
Async XLA Ops:
  0.6 5.3 %copy-start = (bf16[1024,256]{1,0:T(8,128)(2,1)S(1)}, bf16[1024,256]{1,0:T(8,128)(2,1)}, u32[]{:S(2)}) copy-start(bf16[1024,256]{1,0:T(8,128)(2,1)} %wv_ref.3) | copy-start | bytes 1572868
  0.7 5.3 %copy-start.1 = (s32[2,1024]{1,0:T(2,128)S(1)}, s32[2,1024]{1,0:T(2,128)}, u32[]{:S(2)}) copy-start(s32[2,1024]{1,0:T(2,128)} %box_rows.5) | copy-start | bytes 24580
  0.7 9.2 %collective-permute-start.1 = (bf16[256,1024]{1,0:T(8,128)(2,1)}, bf16[256,1024]{1,0:T(8,128)(2,1)}, u32[]{:S(2)}, u32[]{:S(2)}) collective-permute-start(bf16[256,1024]{1,0:T(8,128)(2,1)} %x_ref.1), channel_id=1, source_target_pairs={{0,1},{1,0},{2,3},{3,2},{4,5},{5,4},{6,7},{7,6},{8,9},{9,8},{10,11... | collective-permute-start | bytes 1572872 | tf_op jit(solution)/shard_map/ppermute | solution.py:895
  1.2 15.4 %collective-permute-start = (bf16[256,1024]{1,0:T(8,128)(2,1)}, bf16[256,1024]{1,0:T(8,128)(2,1)}, u32[]{:S(2)}, u32[]{:S(2)}) collective-permute-start(bf16[256,1024]{1,0:T(8,128)(2,1)} %x_ref.1), channel_id=1, source_target_pairs={{0,2},{1,3},{2,0},{3,1},{4,6},{5,7},{6,4},{7,5},{8,10},{9,11},{10,... | collective-permute-start | bytes 1572872 | tf_op jit(solution)/shard_map/ppermute | solution.py:898
  7.8 1.4 copy-start.5
  7.8 1.4 copy-start.6
  7.8 1.4 copy-start.7
  16.6 2.3 %collective-permute-start.2 = (bf16[256,1024]{1,0:T(8,128)(2,1)}, bf16[256,1024]{1,0:T(8,128)(2,1)}, u32[]{:S(2)}, u32[]{:S(2)}) collective-permute-start(bf16[256,1024]{1,0:T(8,128)(2,1)} %collective-permute-done.xa_ref), channel_id=1, source_target_pairs={{0,1},{1,0},{2,3},{3,2},{4,5},{5,4},{6,7},{7,6},{8,9},{9,8},{10,11... | collective-permute-start | bytes 1572872 | tf_op jit(solution)/shard_map/ppermute | solution.py:895
  16.6 33.0 %collective-permute-start.5 = (bf16[256,1024]{1,0:T(8,128)(2,1)}, bf16[256,1024]{1,0:T(8,128)(2,1)}, u32[]{:S(2)}, u32[]{:S(2)}) collective-permute-start(bf16[256,1024]{1,0:T(8,128)(2,1)} %wo_ref.1), channel_id=1, source_target_pairs={{0,2},{1,3},{2,0},{3,1},{4,6},{5,7},{6,4},{7,5},{8,10},{9,11},{10,... | collective-permute-start | bytes 1572872 | tf_op jit(solution)/shard_map/ppermute | solution.py:898
  18.4 31.3 %collective-permute-start.6 = (bf16[256,1024]{1,0:T(8,128)(2,1)}, bf16[256,1024]{1,0:T(8,128)(2,1)}, u32[]{:S(2)}, u32[]{:S(2)}) collective-permute-start(bf16[256,1024]{1,0:T(8,128)(2,1)} %refs_0_.1), channel_id=1, source_target_pairs={{0,2},{1,3},{2,0},{3,1},{4,6},{5,7},{6,4},{7,5},{8,10},{9,11},{10,... | collective-permute-start | bytes 1572872 | tf_op jit(solution)/shard_map/ppermute | solution.py:898
  35.5 14.1 %collective-permute-start.4 = (bf16[512,256]{1,0:T(8,128)(2,1)}, bf16[512,256]{1,0:T(8,128)(2,1)}, u32[]{:S(2)}, u32[]{:S(2)}) collective-permute-start(bf16[512,256]{1,0:T(8,128)(2,1)} %get-tuple-element.147.a0), channel_id=1, source_target_pairs={{0,2},{1,3},{2,0},{3,1},{4,6},{5,7},{6,4},{7,5},{8,10},{9,11},{10,... | collective-permute-start | bytes 786440 | tf_op jit(solution)/shard_map/ppermute | solution.py:898
  37.3 12.4 %collective-permute-start.3 = (bf16[512,256]{1,0:T(8,128)(2,1)}, bf16[512,256]{1,0:T(8,128)(2,1)}, u32[]{:S(2)}, u32[]{:S(2)}) collective-permute-start(bf16[512,256]{1,0:T(8,128)(2,1)} %get-tuple-element.147.a0), channel_id=1, source_target_pairs={{0,1},{1,0},{2,3},{3,2},{4,5},{5,4},{6,7},{7,6},{8,9},{9,8},{10,11... | collective-permute-start | bytes 786440 | tf_op jit(solution)/shard_map/ppermute | solution.py:895
  37.3 13.3 %collective-permute-start.9 = (bf16[256,1024]{1,0:T(8,128)(2,1)}, bf16[256,1024]{1,0:T(8,128)(2,1)}, u32[]{:S(2)}, u32[]{:S(2)}) collective-permute-start(bf16[256,1024]{1,0:T(8,128)(2,1)} %refs_0_.1), channel_id=1, source_target_pairs={{0,1},{1,0},{2,3},{3,2},{4,5},{5,4},{6,7},{7,6},{8,9},{9,8},{10,11... | collective-permute-start | bytes 1572872 | tf_op jit(solution)/shard_map/ppermute | solution.py:895
  49.7 2.3 %collective-permute-start.10 = (bf16[256,1024]{1,0:T(8,128)(2,1)}, bf16[256,1024]{1,0:T(8,128)(2,1)}, u32[]{:S(2)}, u32[]{:S(2)}) collective-permute-start(bf16[256,1024]{1,0:T(8,128)(2,1)} %collective-permute-done.6.refs_2_), channel_id=1, source_target_pairs={{0,1},{1,0},{2,3},{3,2},{4,5},{5,4},{6,7},{7,6},{8,9},{9,8},{10,11... | collective-permute-start | bytes 1572872 | tf_op jit(solution)/shard_map/ppermute | solution.py:895
  49.8 9.0 %collective-permute-start.11 = (bf16[512,256]{1,0:T(8,128)(2,1)}, bf16[512,256]{1,0:T(8,128)(2,1)}, u32[]{:S(2)}, u32[]{:S(2)}) collective-permute-start(bf16[512,256]{1,0:T(8,128)(2,1)} %get-tuple-element.158.b0), channel_id=1, source_target_pairs={{0,2},{1,3},{2,0},{3,1},{4,6},{5,7},{6,4},{7,5},{8,10},{9,11},{10,... | collective-permute-start | bytes 786440 | tf_op jit(solution)/shard_map/ppermute | solution.py:898
  50.1 8.7 %collective-permute-start.13 = (bf16[256,1024]{1,0:T(8,128)(2,1)}, bf16[256,1024]{1,0:T(8,128)(2,1)}, u32[]{:S(2)}, u32[]{:S(2)}) collective-permute-start(bf16[256,1024]{1,0:T(8,128)(2,1)} %wo_ref.1), channel_id=1, source_target_pairs={{0,1},{1,0},{2,3},{3,2},{4,5},{5,4},{6,7},{7,6},{8,9},{9,8},{10,11... | collective-permute-start | bytes 1572872 | tf_op jit(solution)/shard_map/ppermute | solution.py:895
  50.3 8.6 %collective-permute-start.14 = (bf16[256,1024]{1,0:T(8,128)(2,1)}, bf16[256,1024]{1,0:T(8,128)(2,1)}, u32[]{:S(2)}, u32[]{:S(2)}) collective-permute-start(bf16[256,1024]{1,0:T(8,128)(2,1)} %collective-permute-done.5.o2), channel_id=1, source_target_pairs={{0,1},{1,0},{2,3},{3,2},{4,5},{5,4},{6,7},{7,6},{8,9},{9,8},{10,11... | collective-permute-start | bytes 1572872 | tf_op jit(solution)/shard_map/ppermute | solution.py:895
  50.6 8.2 %collective-permute-start.8 = (bf16[512,256]{1,0:T(8,128)(2,1)}, bf16[512,256]{1,0:T(8,128)(2,1)}, u32[]{:S(2)}, u32[]{:S(2)}) collective-permute-start(bf16[512,256]{1,0:T(8,128)(2,1)} %get-tuple-element.158.b0), channel_id=1, source_target_pairs={{0,1},{1,0},{2,3},{3,2},{4,5},{5,4},{6,7},{7,6},{8,9},{9,8},{10,11... | collective-permute-start | bytes 786440 | tf_op jit(solution)/shard_map/ppermute | solution.py:895
  52.0 6.8 %collective-permute-start.7 = (bf16[512,256]{1,0:T(8,128)(2,1)}, bf16[512,256]{1,0:T(8,128)(2,1)}, u32[]{:S(2)}, u32[]{:S(2)}) collective-permute-start(bf16[512,256]{1,0:T(8,128)(2,1)} %collective-permute-done.4.a2), channel_id=1, source_target_pairs={{0,1},{1,0},{2,3},{3,2},{4,5},{5,4},{6,7},{7,6},{8,9},{9,8},{10,11... | collective-permute-start | bytes 786440 | tf_op jit(solution)/shard_map/ppermute | solution.py:895
  58.8 1.9 collective-permute-start.12
  80.4 2.9 %collective-permute-start.15 = (bf16[512,1024]{1,0:T(8,128)(2,1)}, bf16[512,1024]{1,0:T(8,128)(2,1)S(1)}, u32[]{:S(2)}, u32[]{:S(2)}) collective-permute-start(bf16[512,1024]{1,0:T(8,128)(2,1)} %get-tuple-element.169), channel_id=1, source_target_pairs={{0,1},{1,0},{2,3},{3,2},{4,5},{5,4},{6,7},{7,6},{8,9},{9,8},{10,11... | collective-permute-start | bytes 3145736 | tf_op jit(solution)/shard_map/ppermute | solution.py:895
  85.9 15.6 %collective-permute-start.17 = (bf16[512,1024]{1,0:T(8,128)(2,1)}, bf16[512,1024]{1,0:T(8,128)(2,1)}, u32[]{:S(2)}, u32[]{:S(2)}) collective-permute-start(bf16[512,1024]{1,0:T(8,128)(2,1)} %get-tuple-element.175), channel_id=1, source_target_pairs={{0,1},{1,0},{2,3},{3,2},{4,5},{5,4},{6,7},{7,6},{8,9},{9,8},{10,11... | collective-permute-start | bytes 3145736 | tf_op jit(solution)/shard_map/ppermute | solution.py:895
  86.0 25.8 %collective-permute-start.16 = (bf16[512,1024]{1,0:T(8,128)(2,1)}, bf16[512,1024]{1,0:T(8,128)(2,1)}, u32[]{:S(2)}, u32[]{:S(2)}) collective-permute-start(bf16[512,1024]{1,0:T(8,128)(2,1)} %add_convert_fusion.a_ref), channel_id=1, source_target_pairs={{0,2},{1,3},{2,0},{3,1},{4,6},{5,7},{6,4},{7,5},{8,10},{9,11},{10,... | collective-permute-start | bytes 3145736 | tf_op jit(solution)/shard_map/ppermute | solution.py:898
  97.6 43.0 %collective-permute-start.18 = (bf16[4,3,352,128]{3,2,1,0:T(8,128)(2,1)}, bf16[4,3,352,128]{3,2,1,0:T(8,128)(2,1)}, u32[]{:S(2)}, u32[]{:S(2)}) collective-permute-start(bf16[4,3,352,128]{3,2,1,0:T(8,128)(2,1)} %get-tuple-element.178), channel_id=1, source_target_pairs={{0,4},{4,0},{8,12},{12,8},{16,20},{20,16},{24,28},{28,24},{1,5},{5... | collective-permute-start | bytes 3244040 | tf_op jit(solution)/shard_map/ppermute | solution.py:786
  99.9 40.7 %collective-permute-start.19 = (bf16[4,3,352,128]{3,2,1,0:T(8,128)(2,1)}, bf16[4,3,352,128]{3,2,1,0:T(8,128)(2,1)}, u32[]{:S(2)}, u32[]{:S(2)}) collective-permute-start(bf16[4,3,352,128]{3,2,1,0:T(8,128)(2,1)} %get-tuple-element.179), channel_id=1, source_target_pairs={{0,8},{4,12},{8,0},{12,4},{16,24},{20,28},{24,16},{28,20},{1,9},{5... | collective-permute-start | bytes 3244040 | tf_op jit(solution)/shard_map/ppermute | solution.py:786
  116.7 3.0 %collective-permute-start.20 = (bf16[512,1024]{1,0:T(8,128)(2,1)}, bf16[512,1024]{1,0:T(8,128)(2,1)}, u32[]{:S(2)}, u32[]{:S(2)}) collective-permute-start(bf16[512,1024]{1,0:T(8,128)(2,1)} %get-tuple-element.182.own_ref), channel_id=1, source_target_pairs={{0,1},{1,0},{2,3},{3,2},{4,5},{5,4},{6,7},{7,6},{8,9},{9,8},{10,11... | collective-permute-start | bytes 3145736 | tf_op jit(solution)/shard_map/ppermute | solution.py:895
  116.8 23.9 %collective-permute-start.21 = (bf16[256,1024]{1,0:T(8,128)(2,1)}, bf16[256,1024]{1,0:T(8,128)(2,1)}, u32[]{:S(2)}, u32[]{:S(2)}) collective-permute-start(bf16[256,1024]{1,0:T(8,128)(2,1)} %get-tuple-element.187), channel_id=1, source_target_pairs={{0,2},{1,3},{2,0},{3,1},{4,6},{5,7},{6,4},{7,5},{8,10},{9,11},{10,... | collective-permute-start | bytes 1572872 | tf_op jit(solution)/shard_map/ppermute | solution.py:898
  144.7 27.8 %collective-permute-start.22 = (bf16[2,3,352,128]{3,2,1,0:T(8,128)(2,1)}, bf16[2,3,352,128]{3,2,1,0:T(8,128)(2,1)}, u32[]{:S(2)}, u32[]{:S(2)}) collective-permute-start(bf16[2,3,352,128]{3,2,1,0:T(8,128)(2,1)} %get-tuple-element.192), channel_id=1, source_target_pairs={{0,8},{4,12},{8,0},{12,4},{16,24},{20,28},{24,16},{28,20},{1,9},{5... | collective-permute-start | bytes 1622024 | tf_op jit(solution)/shard_map/ppermute | solution.py:786
  147.8 27.5 %collective-permute-start.23 = (bf16[2,3,352,128]{3,2,1,0:T(8,128)(2,1)}, bf16[2,3,352,128]{3,2,1,0:T(8,128)(2,1)}, u32[]{:S(2)}, u32[]{:S(2)}) collective-permute-start(bf16[2,3,352,128]{3,2,1,0:T(8,128)(2,1)} %get-tuple-element.193), channel_id=1, source_target_pairs={{0,16},{4,20},{8,24},{12,28},{16,0},{20,4},{24,8},{28,12},{1,17},{... | collective-permute-start | bytes 1622024 | tf_op jit(solution)/shard_map/ppermute | solution.py:786
  158.3 7.8 %collective-permute-start.24 = (bf16[256,1024]{1,0:T(8,128)(2,1)}, bf16[256,1024]{1,0:T(8,128)(2,1)}, u32[]{:S(2)}, u32[]{:S(2)}) collective-permute-start(bf16[256,1024]{1,0:T(8,128)(2,1)} %get-tuple-element.199), channel_id=1, source_target_pairs={{0,1},{1,0},{2,3},{3,2},{4,5},{5,4},{6,7},{7,6},{8,9},{9,8},{10,11... | collective-permute-start | bytes 1572872 | tf_op jit(solution)/shard_map/ppermute | solution.py:895
  158.3 7.7 %collective-permute-start.25 = (bf16[256,1024]{1,0:T(8,128)(2,1)}, bf16[256,1024]{1,0:T(8,128)(2,1)}, u32[]{:S(2)}, u32[]{:S(2)}) collective-permute-start(bf16[256,1024]{1,0:T(8,128)(2,1)} %get-tuple-element.200), channel_id=1, source_target_pairs={{0,1},{1,0},{2,3},{3,2},{4,5},{5,4},{6,7},{7,6},{8,9},{9,8},{10,11... | collective-permute-start | bytes 1572872 | tf_op jit(solution)/shard_map/ppermute | solution.py:895
  166.1 15.9 %collective-permute-start.27 = (bf16[4,64,1024]{2,1,0:T(8,128)(2,1)}, bf16[4,64,1024]{2,1,0:T(8,128)(2,1)}, u32[]{:S(2)}, u32[]{:S(2)}) collective-permute-start(bf16[4,64,1024]{2,1,0:T(8,128)(2,1)} %get-tuple-element.223), channel_id=1, source_target_pairs={{0,4},{4,0},{8,12},{12,8},{16,20},{20,16},{24,28},{28,24},{1,5},{5... | collective-permute-start | bytes 1572872 | tf_op jit(solution)/shard_map/ppermute | solution.py:786
  167.6 18.9 %collective-permute-start.28 = (bf16[4,64,1024]{2,1,0:T(8,128)(2,1)}, bf16[4,64,1024]{2,1,0:T(8,128)(2,1)}, u32[]{:S(2)}, u32[]{:S(2)}) collective-permute-start(bf16[4,64,1024]{2,1,0:T(8,128)(2,1)} %get-tuple-element.224), channel_id=1, source_target_pairs={{0,8},{4,12},{8,0},{12,4},{16,24},{20,28},{24,16},{28,20},{1,9},{5... | collective-permute-start | bytes 1572872 | tf_op jit(solution)/shard_map/ppermute | solution.py:786
  178.5 2.9 %copy-start.3 = (f32[32,16]{1,0:T(8,128)S(1)}, f32[32,16]{1,0:T(8,128)}, u32[]{:S(2)}) copy-start(f32[32,16]{1,0:T(8,128)} %get-tuple-element.241) | copy-start | bytes 6148
  180.8 13.2 %collective-permute-start.26 = (bf16[256,1024]{1,0:T(8,128)(2,1)}, bf16[256,1024]{1,0:T(8,128)(2,1)}, u32[]{:S(2)}, u32[]{:S(2)}) collective-permute-start(bf16[256,1024]{1,0:T(8,128)(2,1)} %add_convert_fusion.1), channel_id=1, source_target_pairs={{0,2},{1,3},{2,0},{3,1},{4,6},{5,7},{6,4},{7,5},{8,10},{9,11},{10,... | collective-permute-start | bytes 1572872 | tf_op jit(solution)/shard_map/ppermute | solution.py:898
  181.5 30.0 %collective-permute-start.33 = (bf16[1,3,352,128]{3,2,1,0:T(8,128)(2,1)}, bf16[1,3,352,128]{3,2,1,0:T(8,128)(2,1)}, u32[]{:S(2)}, u32[]{:S(2)}) collective-permute-start(bf16[1,3,352,128]{3,2,1,0:T(8,128)(2,1)} %get-tuple-element.220), channel_id=1, source_target_pairs={{0,16},{4,20},{8,24},{12,28},{16,0},{20,4},{24,8},{28,12},{1,17},{... | collective-permute-start | bytes 811016 | tf_op jit(solution)/shard_map/ppermute | solution.py:786
  189.7 14.6 %collective-permute-start.29 = (bf16[2,64,1024]{2,1,0:T(8,128)(2,1)}, bf16[2,64,1024]{2,1,0:T(8,128)(2,1)}, u32[]{:S(2)}, u32[]{:S(2)}) collective-permute-start(bf16[2,64,1024]{2,1,0:T(8,128)(2,1)} %get-tuple-element.228), channel_id=1, source_target_pairs={{0,8},{4,12},{8,0},{12,4},{16,24},{20,28},{24,16},{28,20},{1,9},{5... | collective-permute-start | bytes 786440 | tf_op jit(solution)/shard_map/ppermute | solution.py:786
  189.7 16.3 %collective-permute-start.30 = (bf16[2,64,1024]{2,1,0:T(8,128)(2,1)}, bf16[2,64,1024]{2,1,0:T(8,128)(2,1)}, u32[]{:S(2)}, u32[]{:S(2)}) collective-permute-start(bf16[2,64,1024]{2,1,0:T(8,128)(2,1)} %get-tuple-element.229), channel_id=1, source_target_pairs={{0,16},{4,20},{8,24},{12,28},{16,0},{20,4},{24,8},{28,12},{1,17},{... | collective-permute-start | bytes 786440 | tf_op jit(solution)/shard_map/ppermute | solution.py:786
  192.5 19.6 %collective-permute-start.34 = (bf16[1,3,352,128]{3,2,1,0:T(8,128)(2,1)}, bf16[1,3,352,128]{3,2,1,0:T(8,128)(2,1)}, u32[]{:S(2)}, u32[]{:S(2)}) collective-permute-start(bf16[1,3,352,128]{3,2,1,0:T(8,128)(2,1)} %get-tuple-element.221), channel_id=1, source_target_pairs={{0,4},{4,0},{8,12},{12,8},{16,20},{20,16},{24,28},{28,24},{1,5},{5... | collective-permute-start | bytes 811016 | tf_op jit(solution)/shard_map/ppermute | solution.py:786
  194.0 4.5 %copy-start.4 = (f32[1,1024]{1,0:T(1,128)S(1)}, f32[1,1024]{1,0:T(1,128)}, u32[]{:S(2)}) copy-start(f32[1,1024]{1,0:T(1,128)} %get-tuple-element.240) | copy-start | bytes 12292
  200.1 11.3 %all-to-all-start = ((f32[32,1,112]{2,1,0:T(1,128)}), f32[32,1,112]{2,1,0:T(1,128)S(1)}, u32[]{:S(2)}, u32[]{:S(2)}) async-start(f32[32,1,112]{2,1,0:T(1,128)} %bitcast.15), calls=%async_computation | async-start | bytes 32768 | tf_op jit(solution)/shard_map/all_to_all | solution.py:907
  208.8 8.2 %collective-permute-start.31 = (bf16[1,64,1024]{2,1,0:T(8,128)(2,1)}, bf16[1,64,1024]{2,1,0:T(8,128)(2,1)S(1)}, u32[]{:S(2)}, u32[]{:S(2)}) collective-permute-start(bf16[1,64,1024]{2,1,0:T(8,128)(2,1)} %get-tuple-element.236), channel_id=1, source_target_pairs={{0,16},{4,20},{8,24},{12,28},{16,0},{20,4},{24,8},{28,12},{1,17},{... | collective-permute-start | bytes 393224 | tf_op jit(solution)/shard_map/ppermute | solution.py:786
  209.7 7.3 %collective-permute-start.32 = (bf16[1,64,1024]{2,1,0:T(8,128)(2,1)}, bf16[1,64,1024]{2,1,0:T(8,128)(2,1)}, u32[]{:S(2)}, u32[]{:S(2)}) collective-permute-start(bf16[1,64,1024]{2,1,0:T(8,128)(2,1)} %get-tuple-element.237), channel_id=1, source_target_pairs={{0,4},{4,0},{8,12},{12,8},{16,20},{20,16},{24,28},{28,24},{1,5},{5... | collective-permute-start | bytes 393224 | tf_op jit(solution)/shard_map/ppermute | solution.py:786
  217.0 0.7 copy-start.2

commit v3 on v2

--- a/solution.py
+++ b/solution.py
@@ -782,6 +782,48 @@
     )(ids, *(a for a, _ in ins))
 
 
+def heads_kernel(shards, ids, g_ref, wa_ref, wb_ref, normed_ref, da_ref, ctx_ref, fs_ref, fk_ref, ns_ref, nk_ref, ka_ref, sa_ref, kb_ref, sb_ref, acc, turned):
+    step = pl.program_id(0)
+    rows = fs_ref.shape[0]
+    width = wa_ref.shape[1]
+    for at_step, (send, keep) in enumerate(((fs_ref, fk_ref), (ns_ref, nk_ref))):
+
+        @pl.when(step == at_step)
+        def _():
+            at = pl.ds(pl.multiple_of((1 - at_step + ids[2]) % 2 * 2 * rows, 2 * rows), 2 * rows)
+            total = dot_nt(g_ref[at, 0:width], wa_ref[...]) + dot_nt(g_ref[at, width:], wb_ref[...])
+            lower = ids[1] == 0
+            send[...] = jnp.where(lower, total[rows:], total[:rows]).astype(bf16)
+            keep[...] = jnp.where(lower, total[:rows], total[rows:])
+
+    @pl.when(step == 2)
+    def _():
+        head_sums_kernel(shards, ids, normed_ref, da_ref, g_ref, ctx_ref, ka_ref, sa_ref, kb_ref, sb_ref, acc, turned)
+
+
+def heads_back(ids, grads, weights, normed, d_attn, context, shards):
+    total, model = normed.shape
+    rows = total // 4
+    columns = grads.shape[1] + context.shape[1]
+    shape = (shards // 2, model // shards // 2, columns)
+    ins = [(a, whole(a.shape)) for a in (grads, *weights, normed, d_attn, context)]
+    outs = [((rows, model), kind) for kind in (bf16, f32, bf16, f32)] + [(shape, bf16)] * 4
+    return pl.pallas_call(
+        functools.partial(heads_kernel, shards),
+        out_shape=[jax.ShapeDtypeStruct(*out) for out in outs],
+        grid_spec=pltpu.PrefetchScalarGridSpec(
+            num_scalar_prefetch=1,
+            grid=(3,),
+            in_specs=[spec for _, spec in ins],
+            out_specs=[whole(out[0]) for out in outs],
+            scratch_shapes=[pltpu.VMEM((model, columns), f32), pltpu.VMEM((model, total), bf16)],
+        ),
+        compiler_params=params(),
+        cost_estimate=estimate(),
+        name="heads_back",
+    )(ids, *(a for a, _ in ins))
+
+
 def swap(sent, bit, n_dp):
     return lax.ppermute(sent, "dp", [(i, i ^ (1 << bit)) for i in range(n_dp)])
 
@@ -973,16 +1015,17 @@
         unit_kept, sends = onward(ids, unit[0::2], unit_came)
         unit_came = swaps(sends, 1)
         d_first = after(d_heads, *sends)
-    f_send, f_keep, n_send, n_keep = project_back(ids, d_first, w_pairs)
+    if pairwise:
+        f_send, f_keep, n_send, n_keep, *attn = heads_back(ids, d_first, w_pairs, normed, d_attn, context, n_dp)
+    else:
+        f_send, f_keep, n_send, n_keep = project_back(ids, d_first, w_pairs)
     f_core, n_core = by_core(f_send), by_core(n_send)
     if pairwise:
-        attn = head_sums(ids, normed, d_attn, after(d_heads, f_keep), context, n_dp)
-        f_core, n_core, *attn = together(f_core, n_core, *attn)
         result = result_of(ids, mixed, r_own, after(r_far, attn[0]))
         *unit_came, result = together(*unit_came, result)
         unit_kept, sends = onward(ids, unit_kept, unit_came)
         unit_came = swaps(sends, 2)
-        f_core = after(f_core, *sends)
+        f_core, n_core = together(f_core, n_core, *sends)[:2]
         came = swaps(attn[1::2], 0)
     f_sum = (f_keep + f_core.astype(f32)).astype(bf16)
     far = by_chip(f_sum)

time: 224 us -> 224 us (level)
  waiting for transfers between devices: 32.9 us -> 40.2 us
  starting transfers between devices: 34.1 us -> 30.4 us
  Pallas kernels: 138 us -> 135 us
    pallas_call x12 -> x11, Pallas kernels: 61.1 us -> 54.2 us  [call(): pl.pallas_call(kernel, out_shape=[jax.ShapeDtypeStruct(shape, kind) for s...]
    ppermute x12, waiting for transfers between devices: 12.1 us -> 19 us  [swap(): return lax.ppermute(sent, 'dp', [(i, i ^ 1 << bit) for i in range(n_dp)])]
    pallas_call x1, Pallas kernels: 7.23 us -> 11.7 us  [heads_back(): pl.pallas_call(functools.partial(heads_kernel, shards), out_shape=[jax.Sh...]
    ppermute x12, starting transfers between devices: 19.2 us -> 15.6 us  [swap(): return lax.ppermute(sent, 'dp', [(i, i ^ 1 << bit) for i in range(n_dp)])]
  transfers between devices with their start and end apart: 36 -> 36, of which waited for: 14 -> 14; matrix products, arithmetic and copies ran while one was open for 5% -> 5% of each run, Pallas kernels for 50% -> 49%
where the time goes in v3:
time: 224 us; the launch traced here: 221 us
  Pallas kernels  135 us (60%)
  waiting for transfers between devices  40.2 us (18%)
  starting transfers between devices  30.4 us (14%)
  other arithmetic  9.07 us (4%)
  local copies, waits for them, and re-layouts  5.07 us (2%)
    pallas_call x11, Pallas kernels, call(): pl.pallas_call(kernel, out_shape=[jax.ShapeDtypeStruct(shape, kind) for s...  54.2 us
    pallas_call x2, Pallas kernels, attend(): pl.pallas_call(functools.partial(fwd_kernel, n_heads, qb, 2 * chunk), out...  24.1 us
    pallas_call x1, Pallas kernels, attend_back(): pl.pallas_call(functools.partial(bwd_kernel, n_heads, qb), out_shape=[jax...  20.8 us
    ppermute x12, waiting for transfers between devices, swap(): return lax.ppermute(sent, 'dp', [(i, i ^ 1 << bit) for i in range(n_dp)])  19 us
    ppermute x12, starting transfers between devices, swap(): return lax.ppermute(sent, 'dp', [(i, i ^ 1 << bit) for i in range(n_dp)])  15.6 us
    ppermute x8, waiting for transfers between devices, by_chip(): return lax.ppermute(a, 'mp', [(i, i ^ 2) for i in range(n_mp)])  12.3 us
    pallas_call x1, Pallas kernels, heads_back(): pl.pallas_call(functools.partial(heads_kernel, shards), out_shape=[jax.Sh...  11.7 us
    pallas_call x1, Pallas kernels, unit_parts(): pl.pallas_call(unit_parts_kernel, out_shape=[jax.ShapeDtypeStruct(shape,...  11.3 us
  transfers between devices with their start and end apart: 36, of which 14 were waited for; matrix products, arithmetic and copies ran while one was open for 5% of the time, Pallas kernels for 49%

profile of v3, /device:TPU:0, one launch (start us, length us, event | category | flops | bytes accessed | tf_op | source)
XLA Modules:
  0.0 220.8 jit_solution(4140935489008481716)
XLA Ops:
  0.7 0.5 collective-permute-start.1
  1.2 2.6 %collective-permute-start = (bf16[256,1024]{1,0:T(8,128)(2,1)}, bf16[256,1024]{1,0:T(8,128)(2,1)}, u32[]{:S(2)}, u32[]{:S(2)}) collective-permute-start(bf16[256,1024]{1,0:T(8,128)(2,1)} %x_ref.1), channel_id=1, source_target_pairs={{0,2},{1,3},{2,0},{3,1},{4,6},{5,7},{6,4},{7,5},{8,10},{9,11},{10,... | collective-permute-start | bytes 1572872 | tf_op jit(solution)/shard_map/ppermute | solution.py:940
  3.8 1.1 fusion
  4.8 1.1 fusion.1
  6.0 1.1 copy.42
  7.1 0.7 pad_add_fusion.ids
  7.8 1.4 pad_maximum_fusion
  9.2 0.7 maximum_maximum_fusion.tab_ref
  9.9 4.4 %project.2 = (bf16[1024,1024]{1,0:T(8,128)(2,1)}, bf16[1024,1024]{1,0:T(8,128)(2,1)}, bf16[1024,256]{1,0:T(8,128)(2,1)}, bf16[1024,256]{1,0:T(8,128)(2,1)}, bf16[1024,256]{1,0:T(8,128)(2,1)}) custom-call(s32[4]{0:T(128)} %pad_add_fusion.ids, bf16[256,1024]{1,0:T(8,128)(2,1)} %x_ref.1, bf16[256,1024]{1,0:T(8,128)(2,1)} %collective-permute-done.1.xb_ref, ...), custom_call_target="tpu_custom_call" | custom-call | flops 1000 | bytes 1000 | tf_op jit(solution)/shard_map/project/pallas_call | solution.py:489
  14.2 2.4 %collective-permute-done.xa_ref = bf16[256,1024]{1,0:T(8,128)(2,1)} collective-permute-done((bf16[256,1024]{1,0:T(8,128)(2,1)}, bf16[256,1024]{1,0:T(8,128)(2,1)}, u32[]{:S(2)}, u32[]{:S(2)}) %collective-permute-start) | collective-permute-done | bytes 524320 | tf_op jit(solution)/shard_map/ppermute | solution.py:940
  16.6 1.8 collective-permute-start.5
  18.4 0.3 collective-permute-start.6
  18.9 4.4 %project.3 = (bf16[1024,1024]{1,0:T(8,128)(2,1)}, bf16[1024,1024]{1,0:T(8,128)(2,1)}, bf16[1024,256]{1,0:T(8,128)(2,1)}, bf16[1024,256]{1,0:T(8,128)(2,1)}, bf16[1024,256]{1,0:T(8,128)(2,1)}) custom-call(s32[4]{0:T(128)} %pad_add_fusion.ids, ...), custom_call_target="tpu_custom_call", output_to_operand_aliasing={{0}: (7, {}), {1}: (8, {}), {2}: (9, {}), {3}: (10, {}), {4... | custom-call | flops 1000 | bytes 1000 | tf_op jit(solution)/shard_map/project/pallas_call | solution.py:489
  23.2 12.3 %attend.2 = (bf16[1024,256]{1,0:T(8,128)(2,1)}, f32[256,1024]{1,0:T(8,128)}, f32[8,1024]{1,0:T(8,128)}, bf16[4,1024,1024]{2,1,0:T(8,128)(2,1)}, bf16[512,256]{1,0:T(8,128)(2,1)}) custom-call(s32[1,2]{1,0:T(1,128)} %lens.5, f32[16,32]{1,0:T(8,128)} %maximum_maximum_fusion.tab_ref, s32[1024,2]{1,0:T(8,128)} %bitcast.26, s32[2,1024]{1,0:T(2,128)} %box_rows.5, ...), custom_call_target="tpu_custom_call" | custom-call | flops 1000 | bytes 1000 | tf_op jit(solution)/shard_map/attend/pallas_call | solution.py:232
  35.5 1.8 collective-permute-start.4
  37.3 0.5 collective-permute-start.9
  37.8 11.8 %attend.3 = (bf16[1024,256]{1,0:T(8,128)(2,1)}, f32[256,1024]{1,0:T(8,128)}, f32[8,1024]{1,0:T(8,128)}, bf16[4,1024,1024]{2,1,0:T(8,128)(2,1)}, bf16[512,256]{1,0:T(8,128)(2,1)}) custom-call(s32[1,2]{1,0:T(1,128)} %lens.5, f32[16,32]{1,0:T(8,128)} %maximum_maximum_fusion.tab_ref, ...), custom_call_target="tpu_custom_call", output_to_operand_aliasing={{0}: (7, {}), {1}: (8, {}), {2}: (9, {}), {3}: (10, {})} | custom-call | flops 1000 | bytes 1000 | tf_op jit(solution)/shard_map/attend/pallas_call | solution.py:232
  49.8 0.3 collective-permute-start.11
  50.2 0.3 collective-permute-start.14
  50.8 1.2 collective-permute-done.10.refs_3_
  52.1 4.1 %assemble.1.cot_ref.refs_5_ = bf16[1024,1024]{1,0:T(8,128)(2,1)} custom-call(s32[4]{0:T(128)} %pad_add_fusion.ids, bf16[256,1024]{1,0:T(8,128)(2,1)} %refs_0_.1, bf16[256,1024]{1,0:T(8,128)(2,1)} %collective-permute-done.9.refs_1_, bf16[256,1024]{1,0:T(8,128)(2,1)} %collective-permute-done.6.refs_2_, bf16[256,1024]{1,0:T(8,128)(2,1)} %collective-permute-done.10.refs_3_), custom_call_target="tpu_custom_call" | custom-call | flops 1000 | bytes 1000 | tf_op jit(solution)/shard_map/assemble/pallas_call | solution.py:521
  56.3 2.5 %collective-permute-done.11.b2 = bf16[512,256]{1,0:T(8,128)(2,1)} collective-permute-done((bf16[512,256]{1,0:T(8,128)(2,1)}, bf16[512,256]{1,0:T(8,128)(2,1)}, u32[]{:S(2)}, u32[]{:S(2)}) %collective-permute-start.11) | collective-permute-done | bytes 262176 | tf_op jit(solution)/shard_map/ppermute | solution.py:940
  58.8 1.8 collective-permute-done.12.b3
  60.7 19.7 %ffn.1 = (f32[512,1024]{1,0:T(8,128)}, bf16[1024,1024]{1,0:T(8,128)(2,1)}, bf16[704,1024]{1,0:T(8,128)(2,1)}, bf16[704,1024]{1,0:T(8,128)(2,1)}, bf16[704,1024]{...) custom-call(s32[4]{0:T(128)} %pad_add_fusion.ids, ...), custom_call_target="tpu_custom_call" | custom-call | flops 1000 | bytes 1000 | tf_op jit(solution)/shard_map/ffn/pallas_call | solution.py:832
  80.5 2.7 %collective-permute-done.15 = bf16[512,1024]{1,0:T(8,128)(2,1)S(1)} collective-permute-done((bf16[512,1024]{1,0:T(8,128)(2,1)}, bf16[512,1024]{1,0:T(8,128)(2,1)S(1)}, u32[]{:S(2)}, u32[]{:S(2)}) %collective-permute-start.15) | collective-permute-done | bytes 1048608 | tf_op jit(solution)/shard_map/ppermute | solution.py:937
  83.3 2.6 %add_convert_fusion.a_ref = bf16[512,1024]{1,0:T(8,128)(2,1)} fusion(bf16[512,1024]{1,0:T(8,128)(2,1)S(1)} %collective-permute-done.15, bf16[512,1024]{1,0:T(8,128)(2,1)} %get-tuple-element.162), kind=kLoop, calls=%fused_computation | loop fusion | flops 2097152 | bytes 3145728 | tf_op jit(solution)/shard_map/convert_element_type | solution.py:983
  86.0 0.3 collective-permute-start.16
  86.3 11.3 %unit_parts.1 = (bf16[4,3,352,128]{3,2,1,0:T(8,128)(2,1)}, bf16[4,3,352,128]{3,2,1,0:T(8,128)(2,1)}, bf16[4,3,352,128]{3,2,1,0:T(8,128)(2,1)}, bf16[4,3,352,128]{3,2,1,0:T(8,128)(2,1)}) custom-call(s32[4]{0:T(128)} %pad_add_fusion.ids, bf16[704,1024]{1,0:T(8,128)(2,1)} %get-tuple-element.158.refs_0_, bf16[704,1024]{1,0:T(8,128)(2,1)} %get-tuple-element.159.refs_1_, ...), custom_call_target="tpu_custom_call" | custom-call | flops 1000 | bytes 1000 | tf_op jit(solution)/shard_map/unit_parts/pallas_call | solution.py:702
  97.6 2.0 collective-permute-start.18
  99.6 1.6 collective-permute-start.19
  101.2 3.2 %out_sums.1 = (bf16[256,1024]{1,0:T(8,128)(2,1)}, f32[256,1024]{1,0:T(8,128)}) custom-call(s32[4]{0:T(128)} %pad_add_fusion.ids, bf16[512,1024]{1,0:T(8,128)(2,1)} %get-tuple-element.167.ka_ref.kb_ref, bf16[512,1024]{1,0:T(8,128)(2,1)} %collective-permute-done.17.ca_ref.cb_ref, bf16[512,1024]{1,0:T(8,128)(2,1)} %get-tuple-element.167.ka_ref.kb_ref, ...), custom_call_target="tpu_custom_call" | custom-call | flops 1000 | bytes 1000 | tf_op jit(solution)/shard_map/out_sums/pallas_call | solution.py:832
  104.4 7.4 %collective-permute-done.16.b_ref = bf16[512,1024]{1,0:T(8,128)(2,1)} collective-permute-done((bf16[512,1024]{1,0:T(8,128)(2,1)}, bf16[512,1024]{1,0:T(8,128)(2,1)}, u32[]{:S(2)}, u32[]{:S(2)}) %collective-permute-start.16) | collective-permute-done | bytes 1048608 | tf_op jit(solution)/shard_map/ppermute | solution.py:940
  111.8 5.0 %mid.1 = (f32[512,1024]{1,0:T(8,128)}, bf16[512,1024]{1,0:T(8,128)(2,1)}, f32[1,1024]{1,0:T(1,128)}) custom-call(s32[4]{0:T(128)} %pad_add_fusion.ids, bf16[512,1024]{1,0:T(8,128)(2,1)} %add_convert_fusion.a_ref, bf16[512,1024]{1,0:T(8,128)(2,1)} %collective-permute-done.16.b_ref, f32[512,1024]{1,0:T(8,128)} %get-tuple-element.175.mixed_ref, ...), custom_call_target="tpu_custom_call" | custom-call | flops 1000 | bytes 1000 | tf_op jit(solution)/shard_map/mid/pallas_call | solution.py:832
  116.7 0.3 collective-permute-start.21
  117.1 2.6 %collective-permute-done.20.core_ref = bf16[512,1024]{1,0:T(8,128)(2,1)} collective-permute-done((bf16[512,1024]{1,0:T(8,128)(2,1)}, bf16[512,1024]{1,0:T(8,128)(2,1)}, u32[]{:S(2)}, u32[]{:S(2)}) %collective-permute-start.20) | collective-permute-done | bytes 1048608 | tf_op jit(solution)/shard_map/ppermute | solution.py:937
  119.7 20.8 %attend_back.1 = (bf16[1024,768]{1,0:T(8,128)(2,1)}, f32[32,16]{1,0:T(8,128)}, bf16[1024,1024]{1,0:T(8,128)(2,1)}) custom-call(s32[4]{0:T(128)} %pad_add_fusion.ids, s32[1,2]{1,0:T(1,128)} %lens.5, s32[1024,2]{1,0:T(8,128)} %bitcast.28, s32[2,1024]{1,0:T(2,128)} %box_rows.5, bf16[1024,256]{1,0:T(8,128)(2,1)} %get-tuple-element.142.q_ref, ...), custom_call_target="tpu_custom_call" | custom-call | flops 1000 | bytes 1000 | tf_op jit(solution)/shard_map/attend_back/pallas_call | solution.py:415
  140.6 4.1 %onward.4 = (bf16[2,3,352,128]{3,2,1,0:T(8,128)(2,1)}, bf16[2,3,352,128]{3,2,1,0:T(8,128)(2,1)}, bf16[2,3,352,128]{3,2,1,0:T(8,128)(2,1)}, bf16[2,3,352,128]{3,2,1,0:T(8,128)(2,1)}) custom-call(s32[4]{0:T(128)} %pad_add_fusion.ids, bf16[4,3,352,128]{3,2,1,0:T(8,128)(2,1)} %get-tuple-element.171.refs_0_.refs_1_, ...), custom_call_target="tpu_custom_call" | custom-call | flops 1000 | bytes 1000 | tf_op jit(solution)/shard_map/onward/pallas_call | solution.py:832
  144.7 3.1 %collective-permute-start.22 = (bf16[2,3,352,128]{3,2,1,0:T(8,128)(2,1)}, bf16[2,3,352,128]{3,2,1,0:T(8,128)(2,1)}, u32[]{:S(2)}, u32[]{:S(2)}) collective-permute-start(bf16[2,3,352,128]{3,2,1,0:T(8,128)(2,1)} %get-tuple-element.186), channel_id=1, source_target_pairs={{0,8},{4,12},{8,0},{12,4},{16,24},{20,28},{24,16},{28,20},{1,9},{5... | collective-permute-start | bytes 1622024 | tf_op jit(solution)/shard_map/ppermute | solution.py:828
  147.7 3.4 %collective-permute-start.23 = (bf16[2,3,352,128]{3,2,1,0:T(8,128)(2,1)}, bf16[2,3,352,128]{3,2,1,0:T(8,128)(2,1)}, u32[]{:S(2)}, u32[]{:S(2)}) collective-permute-start(bf16[2,3,352,128]{3,2,1,0:T(8,128)(2,1)} %get-tuple-element.187), channel_id=1, source_target_pairs={{0,16},{4,20},{8,24},{12,28},{16,0},{20,4},{24,8},{28,12},{1,17},{... | collective-permute-start | bytes 1622024 | tf_op jit(solution)/shard_map/ppermute | solution.py:828
  151.2 11.7 %heads_back.1 = (bf16[256,1024]{1,0:T(8,128)(2,1)}, f32[256,1024]{1,0:T(8,128)}, bf16[256,1024]{1,0:T(8,128)(2,1)}, f32[256,1024]{1,0:T(8,128)}, bf16[4,64,1024]...) custom-call(s32[4]{0:T(128)} %pad_add_fusion.ids, ...), custom_call_target="tpu_custom_call" | custom-call | flops 1000 | bytes 1000 | tf_op jit(solution)/shard_map/heads_back/pallas_call | solution.py:811
  162.9 0.5 collective-permute-start.25
  163.4 1.5 collective-permute-start.27
  164.9 3.2 %result_of.1 = f32[256,1024]{1,0:T(8,128)} custom-call(s32[4]{0:T(128)} %pad_add_fusion.ids, f32[512,1024]{1,0:T(8,128)} %get-tuple-element.175.mixed_ref, f32[256,1024]{1,0:T(8,128)} %get-tuple-element.188.own_ref, bf16[256,1024]{1,0:T(8,128)(2,1)} %collective-permute-done.21.far_ref), custom_call_target="tpu_custom_call" | custom-call | flops 1000 | bytes 1000 | tf_op jit(solution)/shard_map/result_of/pallas_call | solution.py:832
  168.1 3.9 %collective-permute-done.22.refs_2_.refs_3_ = bf16[2,3,352,128]{3,2,1,0:T(8,128)(2,1)} collective-permute-done((bf16[2,3,352,128]{3,2,1,0:T(8,128)(2,1)}, bf16[2,3,352,128]{3,2,1,0:T(8,128)(2,1)}, u32[]{:S(2)}, u32[]{:S(2)}) %collective-permute-start.22) | collective-permute-done | bytes 540704 | tf_op jit(solution)/shard_map/ppermute | solution.py:828
  172.0 3.5 %collective-permute-done.23.refs_6_.refs_7_ = bf16[2,3,352,128]{3,2,1,0:T(8,128)(2,1)} collective-permute-done((bf16[2,3,352,128]{3,2,1,0:T(8,128)(2,1)}, bf16[2,3,352,128]{3,2,1,0:T(8,128)(2,1)}, u32[]{:S(2)}, u32[]{:S(2)}) %collective-permute-start.23) | collective-permute-done | bytes 540704 | tf_op jit(solution)/shard_map/ppermute | solution.py:828
  175.5 3.2 %onward.5 = (bf16[1,3,352,128]{3,2,1,0:T(8,128)(2,1)}, bf16[1,3,352,128]{3,2,1,0:T(8,128)(2,1)}, bf16[1,3,352,128]{3,2,1,0:T(8,128)(2,1)}, bf16[1,3,352,128]{3,2,1,0:T(8,128)(2,1)}) custom-call(s32[4]{0:T(128)} %pad_add_fusion.ids, bf16[2,3,352,128]{3,2,1,0:T(8,128)(2,1)} %get-tuple-element.202.refs_0_.refs_1_, ...), custom_call_target="tpu_custom_call" | custom-call | flops 1000 | bytes 1000 | tf_op jit(solution)/shard_map/onward/pallas_call | solution.py:832
  178.8 2.3 %add_convert_fusion.1 = bf16[256,1024]{1,0:T(8,128)(2,1)} fusion(f32[256,1024]{1,0:T(8,128)} %get-tuple-element.209, bf16[256,1024]{1,0:T(8,128)(2,1)} %collective-permute-done.24), kind=kLoop, calls=%fused_computation.1 | loop fusion | flops 786432 | bytes 2097152 | tf_op jit(solution)/shard_map/convert_element_type | solution.py:1030
  181.1 0.5 collective-permute-start.26
  181.7 1.6 collective-permute-start.34
  183.3 6.4 %collective-permute-done.28.refs_6_.refs_7_ = bf16[4,64,1024]{2,1,0:T(8,128)(2,1)} collective-permute-done((bf16[4,64,1024]{2,1,0:T(8,128)(2,1)}, bf16[4,64,1024]{2,1,0:T(8,128)(2,1)}, u32[]{:S(2)}, u32[]{:S(2)}) %collective-permute-start.28) | collective-permute-done | bytes 524320 | tf_op jit(solution)/shard_map/ppermute | solution.py:828
  189.7 3.1 %onward.6 = (bf16[2,64,1024]{2,1,0:T(8,128)(2,1)}, bf16[2,64,1024]{2,1,0:T(8,128)(2,1)}, bf16[2,64,1024]{2,1,0:T(8,128)(2,1)}, bf16[2,64,1024]{2,1,0:T(8,128)(2,1)}) custom-call(s32[4]{0:T(128)} %pad_add_fusion.ids, bf16[4,64,1024]{2,1,0:T(8,128)(2,1)} %get-tuple-element.196.refs_0_.refs_1_, bf16[4,64,1024]{2,1,0:T(8,128)(2,1)} %get-tuple-element.196.refs_0_.refs_1_, ...), custom_call_target="tpu_custom_call" | custom-call | flops 1000 | bytes 1000 | tf_op jit(solution)/shard_map/onward/pallas_call | solution.py:832
  192.9 1.0 collective-permute-start.30
  194.0 4.5 %last.1 = (f32[256,1024]{1,0:T(8,128)}, f32[1,1024]{1,0:T(1,128)}) custom-call(s32[4]{0:T(128)} %pad_add_fusion.ids, f32[256,1024]{1,0:T(8,128)} %get-tuple-element.199.keep_ref, bf16[256,1024]{1,0:T(8,128)(2,1)} %collective-permute-done.25.core_ref, bf16[256,1024]{1,0:T(8,128)(2,1)} %collective-permute-done.26.y_ref, bf16[256,1024]{1,0:T(8,128)(2,1)} %x_ref.1, ...), custom_call_target="tpu_custom_call" | custom-call | flops 1000 | bytes 1000 | tf_op jit(solution)/shard_map/last/pallas_call | solution.py:832
  198.5 0.7 pad_maximum_fusion.3
  199.4 0.7 pad_maximum_fusion.2
  200.1 4.1 %all-to-all-start = ((f32[32,1,112]{2,1,0:T(1,128)}), f32[32,1,112]{2,1,0:T(1,128)S(1)}, u32[]{:S(2)}, u32[]{:S(2)}) async-start(f32[32,1,112]{2,1,0:T(1,128)} %bitcast.15), calls=%async_computation | async-start | bytes 32768 | tf_op jit(solution)/shard_map/all_to_all | solution.py:949
  204.2 2.8 %collective-permute-done.30.refs_6_.refs_7_ = bf16[2,64,1024]{2,1,0:T(8,128)(2,1)} collective-permute-done((bf16[2,64,1024]{2,1,0:T(8,128)(2,1)}, bf16[2,64,1024]{2,1,0:T(8,128)(2,1)}, u32[]{:S(2)}, u32[]{:S(2)}) %collective-permute-start.30) | collective-permute-done | bytes 262176 | tf_op jit(solution)/shard_map/ppermute | solution.py:828
  207.0 2.8 %onward.7 = (bf16[1,64,1024]{2,1,0:T(8,128)(2,1)}, bf16[1,64,1024]{2,1,0:T(8,128)(2,1)}, bf16[1,64,1024]{2,1,0:T(8,128)(2,1)}, bf16[1,64,1024]{2,1,0:T(8,128)(2,1)}) custom-call(s32[4]{0:T(128)} %pad_add_fusion.ids, bf16[2,64,1024]{2,1,0:T(8,128)(2,1)} %get-tuple-element.221.refs_0_.refs_1_, bf16[2,64,1024]{2,1,0:T(8,128)(2,1)} %get-tuple-element.221.refs_0_.refs_1_, ...), custom_call_target="tpu_custom_call" | custom-call | flops 1000 | bytes 1000 | tf_op jit(solution)/shard_map/onward/pallas_call | solution.py:832
  210.0 1.1 collective-permute-start.32
  211.4 2.9 %unit_last.1 = (f32[704,128]{1,0:T(8,128)}, f32[704,128]{1,0:T(8,128)}, f32[704,128]{1,0:T(8,128)}) custom-call(s32[4]{0:T(128)} %pad_add_fusion.ids, bf16[1,3,352,128]{3,2,1,0:T(8,128)(2,1)} %get-tuple-element.226.ka, bf16[1,3,352,128]{3,2,1,0:T(8,128)(2,1)} %collective-permute-done.33.ca, bf16[1,3,352,128]{3,2,1,0:T(8,128)(2,1)} %get-tuple-element.232.kb, ...), custom_call_target="tpu_custom_call" | custom-call | flops 1000 | bytes 1000 | tf_op jit(solution)/shard_map/unit_last/pallas_call | solution.py:832
  214.3 0.6 fusion.4
  214.9 2.4 %collective-permute-done.31.ca = bf16[1,64,1024]{2,1,0:T(8,128)(2,1)S(1)} collective-permute-done((bf16[1,64,1024]{2,1,0:T(8,128)(2,1)}, bf16[1,64,1024]{2,1,0:T(8,128)(2,1)S(1)}, u32[]{:S(2)}, u32[]{:S(2)}) %collective-permute-start.31) | collective-permute-done | bytes 131104 | tf_op jit(solution)/shard_map/ppermute | solution.py:828
  217.4 0.6 fusion.3
  218.0 2.6 %head_last.1 = (f32[128,256]{1,0:T(8,128)}, f32[128,256]{1,0:T(8,128)}, f32[128,256]{1,0:T(8,128)}, f32[256,128]{1,0:T(8,128)}) custom-call(s32[4]{0:T(128)} %pad_add_fusion.ids, bf16[1,64,1024]{2,1,0:T(8,128)(2,1)} %get-tuple-element.223.ka, bf16[1,64,1024]{2,1,0:T(8,128)(2,1)} %copy-done.2, bf16[1,64,1024]{2,1,0:T(8,128)(2,1)} %get-tuple-element.237.kb, ...), custom_call_target="tpu_custom_call" | custom-call | flops 1000 | bytes 1000 | tf_op jit(solution)/shard_map/head_last/pallas_call | solution.py:832
  (70 shorter events, 2.5 us)
Async XLA Ops:
  0.6 5.3 %copy-start = (bf16[1024,256]{1,0:T(8,128)(2,1)S(1)}, bf16[1024,256]{1,0:T(8,128)(2,1)}, u32[]{:S(2)}) copy-start(bf16[1024,256]{1,0:T(8,128)(2,1)} %wv_ref.3) | copy-start | bytes 1572868
  0.7 5.3 %copy-start.1 = (s32[2,1024]{1,0:T(2,128)S(1)}, s32[2,1024]{1,0:T(2,128)}, u32[]{:S(2)}) copy-start(s32[2,1024]{1,0:T(2,128)} %box_rows.5) | copy-start | bytes 24580
  0.7 9.2 %collective-permute-start.1 = (bf16[256,1024]{1,0:T(8,128)(2,1)}, bf16[256,1024]{1,0:T(8,128)(2,1)}, u32[]{:S(2)}, u32[]{:S(2)}) collective-permute-start(bf16[256,1024]{1,0:T(8,128)(2,1)} %x_ref.1), channel_id=1, source_target_pairs={{0,1},{1,0},{2,3},{3,2},{4,5},{5,4},{6,7},{7,6},{8,9},{9,8},{10,11... | collective-permute-start | bytes 1572872 | tf_op jit(solution)/shard_map/ppermute | solution.py:937
  1.2 15.4 %collective-permute-start = (bf16[256,1024]{1,0:T(8,128)(2,1)}, bf16[256,1024]{1,0:T(8,128)(2,1)}, u32[]{:S(2)}, u32[]{:S(2)}) collective-permute-start(bf16[256,1024]{1,0:T(8,128)(2,1)} %x_ref.1), channel_id=1, source_target_pairs={{0,2},{1,3},{2,0},{3,1},{4,6},{5,7},{6,4},{7,5},{8,10},{9,11},{10,... | collective-permute-start | bytes 1572872 | tf_op jit(solution)/shard_map/ppermute | solution.py:940
  7.8 1.4 copy-start.5
  7.8 1.4 copy-start.6
  7.8 1.4 copy-start.7
  16.6 2.3 %collective-permute-start.2 = (bf16[256,1024]{1,0:T(8,128)(2,1)}, bf16[256,1024]{1,0:T(8,128)(2,1)}, u32[]{:S(2)}, u32[]{:S(2)}) collective-permute-start(bf16[256,1024]{1,0:T(8,128)(2,1)} %collective-permute-done.xa_ref), channel_id=1, source_target_pairs={{0,1},{1,0},{2,3},{3,2},{4,5},{5,4},{6,7},{7,6},{8,9},{9,8},{10,11... | collective-permute-start | bytes 1572872 | tf_op jit(solution)/shard_map/ppermute | solution.py:937
  16.6 33.0 %collective-permute-start.5 = (bf16[256,1024]{1,0:T(8,128)(2,1)}, bf16[256,1024]{1,0:T(8,128)(2,1)}, u32[]{:S(2)}, u32[]{:S(2)}) collective-permute-start(bf16[256,1024]{1,0:T(8,128)(2,1)} %wo_ref.1), channel_id=1, source_target_pairs={{0,2},{1,3},{2,0},{3,1},{4,6},{5,7},{6,4},{7,5},{8,10},{9,11},{10,... | collective-permute-start | bytes 1572872 | tf_op jit(solution)/shard_map/ppermute | solution.py:940
  18.4 31.3 %collective-permute-start.6 = (bf16[256,1024]{1,0:T(8,128)(2,1)}, bf16[256,1024]{1,0:T(8,128)(2,1)}, u32[]{:S(2)}, u32[]{:S(2)}) collective-permute-start(bf16[256,1024]{1,0:T(8,128)(2,1)} %refs_0_.1), channel_id=1, source_target_pairs={{0,2},{1,3},{2,0},{3,1},{4,6},{5,7},{6,4},{7,5},{8,10},{9,11},{10,... | collective-permute-start | bytes 1572872 | tf_op jit(solution)/shard_map/ppermute | solution.py:940
  35.5 14.1 %collective-permute-start.4 = (bf16[512,256]{1,0:T(8,128)(2,1)}, bf16[512,256]{1,0:T(8,128)(2,1)}, u32[]{:S(2)}, u32[]{:S(2)}) collective-permute-start(bf16[512,256]{1,0:T(8,128)(2,1)} %get-tuple-element.141.a0), channel_id=1, source_target_pairs={{0,2},{1,3},{2,0},{3,1},{4,6},{5,7},{6,4},{7,5},{8,10},{9,11},{10,... | collective-permute-start | bytes 786440 | tf_op jit(solution)/shard_map/ppermute | solution.py:940
  37.3 12.4 %collective-permute-start.3 = (bf16[512,256]{1,0:T(8,128)(2,1)}, bf16[512,256]{1,0:T(8,128)(2,1)}, u32[]{:S(2)}, u32[]{:S(2)}) collective-permute-start(bf16[512,256]{1,0:T(8,128)(2,1)} %get-tuple-element.141.a0), channel_id=1, source_target_pairs={{0,1},{1,0},{2,3},{3,2},{4,5},{5,4},{6,7},{7,6},{8,9},{9,8},{10,11... | collective-permute-start | bytes 786440 | tf_op jit(solution)/shard_map/ppermute | solution.py:937
  37.3 13.3 %collective-permute-start.9 = (bf16[256,1024]{1,0:T(8,128)(2,1)}, bf16[256,1024]{1,0:T(8,128)(2,1)}, u32[]{:S(2)}, u32[]{:S(2)}) collective-permute-start(bf16[256,1024]{1,0:T(8,128)(2,1)} %refs_0_.1), channel_id=1, source_target_pairs={{0,1},{1,0},{2,3},{3,2},{4,5},{5,4},{6,7},{7,6},{8,9},{9,8},{10,11... | collective-permute-start | bytes 1572872 | tf_op jit(solution)/shard_map/ppermute | solution.py:937
  49.7 2.3 %collective-permute-start.10 = (bf16[256,1024]{1,0:T(8,128)(2,1)}, bf16[256,1024]{1,0:T(8,128)(2,1)}, u32[]{:S(2)}, u32[]{:S(2)}) collective-permute-start(bf16[256,1024]{1,0:T(8,128)(2,1)} %collective-permute-done.6.refs_2_), channel_id=1, source_target_pairs={{0,1},{1,0},{2,3},{3,2},{4,5},{5,4},{6,7},{7,6},{8,9},{9,8},{10,11... | collective-permute-start | bytes 1572872 | tf_op jit(solution)/shard_map/ppermute | solution.py:937
  49.8 9.0 %collective-permute-start.11 = (bf16[512,256]{1,0:T(8,128)(2,1)}, bf16[512,256]{1,0:T(8,128)(2,1)}, u32[]{:S(2)}, u32[]{:S(2)}) collective-permute-start(bf16[512,256]{1,0:T(8,128)(2,1)} %get-tuple-element.152.b0), channel_id=1, source_target_pairs={{0,2},{1,3},{2,0},{3,1},{4,6},{5,7},{6,4},{7,5},{8,10},{9,11},{10,... | collective-permute-start | bytes 786440 | tf_op jit(solution)/shard_map/ppermute | solution.py:940
  50.1 8.7 %collective-permute-start.13 = (bf16[256,1024]{1,0:T(8,128)(2,1)}, bf16[256,1024]{1,0:T(8,128)(2,1)}, u32[]{:S(2)}, u32[]{:S(2)}) collective-permute-start(bf16[256,1024]{1,0:T(8,128)(2,1)} %wo_ref.1), channel_id=1, source_target_pairs={{0,1},{1,0},{2,3},{3,2},{4,5},{5,4},{6,7},{7,6},{8,9},{9,8},{10,11... | collective-permute-start | bytes 1572872 | tf_op jit(solution)/shard_map/ppermute | solution.py:937
  50.2 8.6 %collective-permute-start.14 = (bf16[256,1024]{1,0:T(8,128)(2,1)}, bf16[256,1024]{1,0:T(8,128)(2,1)}, u32[]{:S(2)}, u32[]{:S(2)}) collective-permute-start(bf16[256,1024]{1,0:T(8,128)(2,1)} %collective-permute-done.5.o2), channel_id=1, source_target_pairs={{0,1},{1,0},{2,3},{3,2},{4,5},{5,4},{6,7},{7,6},{8,9},{9,8},{10,11... | collective-permute-start | bytes 1572872 | tf_op jit(solution)/shard_map/ppermute | solution.py:937
  50.6 8.2 %collective-permute-start.8 = (bf16[512,256]{1,0:T(8,128)(2,1)}, bf16[512,256]{1,0:T(8,128)(2,1)}, u32[]{:S(2)}, u32[]{:S(2)}) collective-permute-start(bf16[512,256]{1,0:T(8,128)(2,1)} %get-tuple-element.152.b0), channel_id=1, source_target_pairs={{0,1},{1,0},{2,3},{3,2},{4,5},{5,4},{6,7},{7,6},{8,9},{9,8},{10,11... | collective-permute-start | bytes 786440 | tf_op jit(solution)/shard_map/ppermute | solution.py:937
  52.0 6.8 %collective-permute-start.7 = (bf16[512,256]{1,0:T(8,128)(2,1)}, bf16[512,256]{1,0:T(8,128)(2,1)}, u32[]{:S(2)}, u32[]{:S(2)}) collective-permute-start(bf16[512,256]{1,0:T(8,128)(2,1)} %collective-permute-done.4.a2), channel_id=1, source_target_pairs={{0,1},{1,0},{2,3},{3,2},{4,5},{5,4},{6,7},{7,6},{8,9},{9,8},{10,11... | collective-permute-start | bytes 786440 | tf_op jit(solution)/shard_map/ppermute | solution.py:937
  58.8 1.9 collective-permute-start.12
  80.3 2.9 %collective-permute-start.15 = (bf16[512,1024]{1,0:T(8,128)(2,1)}, bf16[512,1024]{1,0:T(8,128)(2,1)S(1)}, u32[]{:S(2)}, u32[]{:S(2)}) collective-permute-start(bf16[512,1024]{1,0:T(8,128)(2,1)} %get-tuple-element.163), channel_id=1, source_target_pairs={{0,1},{1,0},{2,3},{3,2},{4,5},{5,4},{6,7},{7,6},{8,9},{9,8},{10,11... | collective-permute-start | bytes 3145736 | tf_op jit(solution)/shard_map/ppermute | solution.py:937
  85.9 15.3 %collective-permute-start.17 = (bf16[512,1024]{1,0:T(8,128)(2,1)}, bf16[512,1024]{1,0:T(8,128)(2,1)}, u32[]{:S(2)}, u32[]{:S(2)}) collective-permute-start(bf16[512,1024]{1,0:T(8,128)(2,1)} %get-tuple-element.169), channel_id=1, source_target_pairs={{0,1},{1,0},{2,3},{3,2},{4,5},{5,4},{6,7},{7,6},{8,9},{9,8},{10,11... | collective-permute-start | bytes 3145736 | tf_op jit(solution)/shard_map/ppermute | solution.py:937
  86.0 25.8 %collective-permute-start.16 = (bf16[512,1024]{1,0:T(8,128)(2,1)}, bf16[512,1024]{1,0:T(8,128)(2,1)}, u32[]{:S(2)}, u32[]{:S(2)}) collective-permute-start(bf16[512,1024]{1,0:T(8,128)(2,1)} %add_convert_fusion.a_ref), channel_id=1, source_target_pairs={{0,2},{1,3},{2,0},{3,1},{4,6},{5,7},{6,4},{7,5},{8,10},{9,11},{10,... | collective-permute-start | bytes 3145736 | tf_op jit(solution)/shard_map/ppermute | solution.py:940
  97.6 43.0 %collective-permute-start.18 = (bf16[4,3,352,128]{3,2,1,0:T(8,128)(2,1)}, bf16[4,3,352,128]{3,2,1,0:T(8,128)(2,1)}, u32[]{:S(2)}, u32[]{:S(2)}) collective-permute-start(bf16[4,3,352,128]{3,2,1,0:T(8,128)(2,1)} %get-tuple-element.172), channel_id=1, source_target_pairs={{0,4},{4,0},{8,12},{12,8},{16,20},{20,16},{24,28},{28,24},{1,5},{5... | collective-permute-start | bytes 3244040 | tf_op jit(solution)/shard_map/ppermute | solution.py:828
  99.6 41.0 %collective-permute-start.19 = (bf16[4,3,352,128]{3,2,1,0:T(8,128)(2,1)}, bf16[4,3,352,128]{3,2,1,0:T(8,128)(2,1)}, u32[]{:S(2)}, u32[]{:S(2)}) collective-permute-start(bf16[4,3,352,128]{3,2,1,0:T(8,128)(2,1)} %get-tuple-element.173), channel_id=1, source_target_pairs={{0,8},{4,12},{8,0},{12,4},{16,24},{20,28},{24,16},{28,20},{1,9},{5... | collective-permute-start | bytes 3244040 | tf_op jit(solution)/shard_map/ppermute | solution.py:828
  116.7 3.0 %collective-permute-start.20 = (bf16[512,1024]{1,0:T(8,128)(2,1)}, bf16[512,1024]{1,0:T(8,128)(2,1)}, u32[]{:S(2)}, u32[]{:S(2)}) collective-permute-start(bf16[512,1024]{1,0:T(8,128)(2,1)} %get-tuple-element.176.own_ref), channel_id=1, source_target_pairs={{0,1},{1,0},{2,3},{3,2},{4,5},{5,4},{6,7},{7,6},{8,9},{9,8},{10,11... | collective-permute-start | bytes 3145736 | tf_op jit(solution)/shard_map/ppermute | solution.py:937
  116.7 23.8 %collective-permute-start.21 = (bf16[256,1024]{1,0:T(8,128)(2,1)}, bf16[256,1024]{1,0:T(8,128)(2,1)}, u32[]{:S(2)}, u32[]{:S(2)}) collective-permute-start(bf16[256,1024]{1,0:T(8,128)(2,1)} %get-tuple-element.181), channel_id=1, source_target_pairs={{0,2},{1,3},{2,0},{3,1},{4,6},{5,7},{6,4},{7,5},{8,10},{9,11},{10,... | collective-permute-start | bytes 1572872 | tf_op jit(solution)/shard_map/ppermute | solution.py:940
  144.7 27.3 %collective-permute-start.22 = (bf16[2,3,352,128]{3,2,1,0:T(8,128)(2,1)}, bf16[2,3,352,128]{3,2,1,0:T(8,128)(2,1)}, u32[]{:S(2)}, u32[]{:S(2)}) collective-permute-start(bf16[2,3,352,128]{3,2,1,0:T(8,128)(2,1)} %get-tuple-element.186), channel_id=1, source_target_pairs={{0,8},{4,12},{8,0},{12,4},{16,24},{20,28},{24,16},{28,20},{1,9},{5... | collective-permute-start | bytes 1622024 | tf_op jit(solution)/shard_map/ppermute | solution.py:828
  147.7 27.8 %collective-permute-start.23 = (bf16[2,3,352,128]{3,2,1,0:T(8,128)(2,1)}, bf16[2,3,352,128]{3,2,1,0:T(8,128)(2,1)}, u32[]{:S(2)}, u32[]{:S(2)}) collective-permute-start(bf16[2,3,352,128]{3,2,1,0:T(8,128)(2,1)} %get-tuple-element.187), channel_id=1, source_target_pairs={{0,16},{4,20},{8,24},{12,28},{16,0},{20,4},{24,8},{28,12},{1,17},{... | collective-permute-start | bytes 1622024 | tf_op jit(solution)/shard_map/ppermute | solution.py:828
  162.9 15.9 %collective-permute-start.24 = (bf16[256,1024]{1,0:T(8,128)(2,1)}, bf16[256,1024]{1,0:T(8,128)(2,1)}, u32[]{:S(2)}, u32[]{:S(2)}) collective-permute-start(bf16[256,1024]{1,0:T(8,128)(2,1)} %get-tuple-element.200), channel_id=1, source_target_pairs={{0,1},{1,0},{2,3},{3,2},{4,5},{5,4},{6,7},{7,6},{8,9},{9,8},{10,11... | collective-permute-start | bytes 1572872 | tf_op jit(solution)/shard_map/ppermute | solution.py:937
  162.9 15.9 %collective-permute-start.25 = (bf16[256,1024]{1,0:T(8,128)(2,1)}, bf16[256,1024]{1,0:T(8,128)(2,1)}, u32[]{:S(2)}, u32[]{:S(2)}) collective-permute-start(bf16[256,1024]{1,0:T(8,128)(2,1)} %get-tuple-element.201), channel_id=1, source_target_pairs={{0,1},{1,0},{2,3},{3,2},{4,5},{5,4},{6,7},{7,6},{8,9},{9,8},{10,11... | collective-permute-start | bytes 1572872 | tf_op jit(solution)/shard_map/ppermute | solution.py:937
  163.4 19.9 %collective-permute-start.27 = (bf16[4,64,1024]{2,1,0:T(8,128)(2,1)}, bf16[4,64,1024]{2,1,0:T(8,128)(2,1)}, u32[]{:S(2)}, u32[]{:S(2)}) collective-permute-start(bf16[4,64,1024]{2,1,0:T(8,128)(2,1)} %get-tuple-element.211), channel_id=1, source_target_pairs={{0,4},{4,0},{8,12},{12,8},{16,20},{20,16},{24,28},{28,24},{1,5},{5... | collective-permute-start | bytes 1572872 | tf_op jit(solution)/shard_map/ppermute | solution.py:828
  172.0 17.7 %collective-permute-start.28 = (bf16[4,64,1024]{2,1,0:T(8,128)(2,1)}, bf16[4,64,1024]{2,1,0:T(8,128)(2,1)}, u32[]{:S(2)}, u32[]{:S(2)}) collective-permute-start(bf16[4,64,1024]{2,1,0:T(8,128)(2,1)} %get-tuple-element.212), channel_id=1, source_target_pairs={{0,8},{4,12},{8,0},{12,4},{16,24},{20,28},{24,16},{28,20},{1,9},{5... | collective-permute-start | bytes 1572872 | tf_op jit(solution)/shard_map/ppermute | solution.py:828
  178.7 2.9 %copy-start.3 = (f32[32,16]{1,0:T(8,128)S(1)}, f32[32,16]{1,0:T(8,128)}, u32[]{:S(2)}) copy-start(f32[32,16]{1,0:T(8,128)} %get-tuple-element.229) | copy-start | bytes 6148
  181.1 13.0 %collective-permute-start.26 = (bf16[256,1024]{1,0:T(8,128)(2,1)}, bf16[256,1024]{1,0:T(8,128)(2,1)}, u32[]{:S(2)}, u32[]{:S(2)}) collective-permute-start(bf16[256,1024]{1,0:T(8,128)(2,1)} %add_convert_fusion.1), channel_id=1, source_target_pairs={{0,2},{1,3},{2,0},{3,1},{4,6},{5,7},{6,4},{7,5},{8,10},{9,11},{10,... | collective-permute-start | bytes 1572872 | tf_op jit(solution)/shard_map/ppermute | solution.py:940
  181.7 29.7 %collective-permute-start.33 = (bf16[1,3,352,128]{3,2,1,0:T(8,128)(2,1)}, bf16[1,3,352,128]{3,2,1,0:T(8,128)(2,1)}, u32[]{:S(2)}, u32[]{:S(2)}) collective-permute-start(bf16[1,3,352,128]{3,2,1,0:T(8,128)(2,1)} %get-tuple-element.206), channel_id=1, source_target_pairs={{0,16},{4,20},{8,24},{12,28},{16,0},{20,4},{24,8},{28,12},{1,17},{... | collective-permute-start | bytes 811016 | tf_op jit(solution)/shard_map/ppermute | solution.py:828
  181.7 29.7 %collective-permute-start.34 = (bf16[1,3,352,128]{3,2,1,0:T(8,128)(2,1)}, bf16[1,3,352,128]{3,2,1,0:T(8,128)(2,1)}, u32[]{:S(2)}, u32[]{:S(2)}) collective-permute-start(bf16[1,3,352,128]{3,2,1,0:T(8,128)(2,1)} %get-tuple-element.207), channel_id=1, source_target_pairs={{0,4},{4,0},{8,12},{12,8},{16,20},{20,16},{24,28},{28,24},{1,5},{5... | collective-permute-start | bytes 811016 | tf_op jit(solution)/shard_map/ppermute | solution.py:828
  192.8 11.4 %collective-permute-start.29 = (bf16[2,64,1024]{2,1,0:T(8,128)(2,1)}, bf16[2,64,1024]{2,1,0:T(8,128)(2,1)}, u32[]{:S(2)}, u32[]{:S(2)}) collective-permute-start(bf16[2,64,1024]{2,1,0:T(8,128)(2,1)} %get-tuple-element.216), channel_id=1, source_target_pairs={{0,8},{4,12},{8,0},{12,4},{16,24},{20,28},{24,16},{28,20},{1,9},{5... | collective-permute-start | bytes 786440 | tf_op jit(solution)/shard_map/ppermute | solution.py:828
  192.9 14.1 %collective-permute-start.30 = (bf16[2,64,1024]{2,1,0:T(8,128)(2,1)}, bf16[2,64,1024]{2,1,0:T(8,128)(2,1)}, u32[]{:S(2)}, u32[]{:S(2)}) collective-permute-start(bf16[2,64,1024]{2,1,0:T(8,128)(2,1)} %get-tuple-element.217), channel_id=1, source_target_pairs={{0,16},{4,20},{8,24},{12,28},{16,0},{20,4},{24,8},{28,12},{1,17},{... | collective-permute-start | bytes 786440 | tf_op jit(solution)/shard_map/ppermute | solution.py:828
  194.0 4.5 %copy-start.4 = (f32[1,1024]{1,0:T(1,128)S(1)}, f32[1,1024]{1,0:T(1,128)}, u32[]{:S(2)}) copy-start(f32[1,1024]{1,0:T(1,128)} %get-tuple-element.228) | copy-start | bytes 12292
  200.1 11.2 %all-to-all-start = ((f32[32,1,112]{2,1,0:T(1,128)}), f32[32,1,112]{2,1,0:T(1,128)S(1)}, u32[]{:S(2)}, u32[]{:S(2)}) async-start(f32[32,1,112]{2,1,0:T(1,128)} %bitcast.15), calls=%async_computation | async-start | bytes 32768 | tf_op jit(solution)/shard_map/all_to_all | solution.py:949
  209.8 7.5 %collective-permute-start.31 = (bf16[1,64,1024]{2,1,0:T(8,128)(2,1)}, bf16[1,64,1024]{2,1,0:T(8,128)(2,1)S(1)}, u32[]{:S(2)}, u32[]{:S(2)}) collective-permute-start(bf16[1,64,1024]{2,1,0:T(8,128)(2,1)} %get-tuple-element.224), channel_id=1, source_target_pairs={{0,16},{4,20},{8,24},{12,28},{16,0},{20,4},{24,8},{28,12},{1,17},{... | collective-permute-start | bytes 393224 | tf_op jit(solution)/shard_map/ppermute | solution.py:828
  210.0 7.2 %collective-permute-start.32 = (bf16[1,64,1024]{2,1,0:T(8,128)(2,1)}, bf16[1,64,1024]{2,1,0:T(8,128)(2,1)}, u32[]{:S(2)}, u32[]{:S(2)}) collective-permute-start(bf16[1,64,1024]{2,1,0:T(8,128)(2,1)} %get-tuple-element.225), channel_id=1, source_target_pairs={{0,4},{4,0},{8,12},{12,8},{16,20},{20,16},{24,28},{28,24},{1,5},{5... | collective-permute-start | bytes 393224 | tf_op jit(solution)/shard_map/ppermute | solution.py:828
  217.3 0.7 copy-start.2
